TPU v7x, 128 devices: a whole 4x4x4 slice. The times are simulated.
128 devices in a mesh: sample: 8 (over z_lo, y), feat: 16 (over x, z_hi, core).
Axes of the slice: x: 4, y: 4, z: 4 (z_hi: 2, z_lo: 2; z = z_hi * 2 + z_lo), core: 2. Of those that a mesh axis runs over, the one named last changes fastest.
Arguments:
- view_a: bfloat16 [1024, 16384], P('sample', 'feat'), may hold values from -60 to 60
- view_b: bfloat16 [1024, 16384], P('sample', 'feat'), may hold values from -60 to 60
Outputs:
- loss: float32 [], replicated
- grad_a: bfloat16 [1024, 16384], P('sample', 'feat')
- grad_b: bfloat16 [1024, 16384], P('sample', 'feat')
All inputs are finite; a program needn't handle non-finite values.
Results may differ from a plain program's by a relative error of at most 0.02.
Values may be sent and summed in bfloat16 or wider, within the bound.
No kernel may reach another device: no remote copies, remote signals or barrier semaphores. Data moves between devices by JAX's collectives and lax.ppermute only.
A program may use at most 64 MiB of HBM per device.

v0:
```python
import jax
import jax.numpy as jnp
from jax import lax
from jax.sharding import PartitionSpec as P

EPSILON = 1e-05
OFF_WEIGHT = 0.0051


def body(view_a, view_b):
    rows_dev, cols_dev = view_a.shape
    groups = lax.axis_size("sample")
    blocks = lax.axis_size("feat")
    total_rows = rows_dev * groups
    sub_width = cols_dev // groups
    inv_rows = 1.0 / total_rows
    sample_id = lax.axis_index("sample")
    feat_id = lax.axis_index("feat")
    float_a = view_a.astype(jnp.float32)
    float_b = view_b.astype(jnp.float32)
    moment_sums = lax.psum(
        (
            jnp.sum(float_a, axis=0),
            jnp.sum(float_a * float_a, axis=0),
            jnp.sum(float_b, axis=0),
            jnp.sum(float_b * float_b, axis=0),
        ),
        "sample",
    )
    mean_a = moment_sums[0] * inv_rows
    scale_a = lax.rsqrt(moment_sums[1] * inv_rows - mean_a * mean_a + EPSILON)
    mean_b = moment_sums[2] * inv_rows
    scale_block_b = lax.rsqrt(moment_sums[3] * inv_rows - mean_b * mean_b + EPSILON)
    local_a = ((float_a - mean_a) * scale_a).astype(jnp.bfloat16)
    source_b = ((float_b - mean_b) * scale_block_b).astype(jnp.bfloat16)
    scale_b = lax.dynamic_slice_in_dim(scale_block_b, sample_id * sub_width, sub_width)
    norm_a = lax.all_gather(local_a, "sample", axis=0, tiled=True)
    row_index = jnp.arange(cols_dev, dtype=jnp.int32)
    wide_b = lax.all_gather(source_b, "feat", axis=1, tiled=True)
    arranged = (
        wide_b.reshape(rows_dev, blocks, groups, sub_width)
        .transpose(0, 2, 1, 3)
        .reshape(rows_dev, blocks * cols_dev)
    )
    moved_b = lax.all_to_all(arranged, "sample", split_axis=1, concat_axis=0, tiled=True)
    own_b = lax.dynamic_slice_in_dim(moved_b, feat_id * sub_width, sub_width, 1)
    panel_width = moved_b.shape[1]
    correlation = (
        lax.dot_general(
            norm_a, moved_b, (((0,), (0,)), ((), ())), preferred_element_type=jnp.float32
        )
        * inv_rows
    )
    local_cols = jnp.arange(panel_width, dtype=jnp.int32)
    owner_block = local_cols // sub_width
    offset = local_cols % sub_width
    on_diagonal = (owner_block[None, :] == feat_id) & (
        offset[None, :] + sample_id * sub_width == row_index[:, None]
    )
    missing = 1.0 - correlation
    piece_loss = jnp.sum(
        jnp.where(on_diagonal, missing * missing, OFF_WEIGHT * correlation * correlation)
    )
    factor = jnp.where(on_diagonal, correlation - 1.0, OFF_WEIGHT * correlation).astype(
        jnp.bfloat16
    )
    grad_rows = lax.dot_general(
        moved_b, factor, (((1,), (1,)), ((), ())), preferred_element_type=jnp.float32
    )
    folded = (piece_loss, grad_rows, factor)
    loss_sum, grad_rows, factor_tile = folded
    row_grad = lax.psum_scatter(
        grad_rows.astype(jnp.bfloat16), "sample", scatter_dimension=0, tiled=True
    ).astype(jnp.float32)
    float_local = local_a.astype(jnp.float32)
    moments = lax.psum(
        (jnp.sum(row_grad, axis=0), jnp.sum(row_grad * float_local, axis=0)), "sample"
    )
    grad_a = (
        scale_a * (row_grad - moments[0] * inv_rows - float_local * (moments[1] * inv_rows))
    ).astype(jnp.bfloat16)
    col_grad = lax.psum_scatter(
        lax.dot_general(
            factor_tile, norm_a, (((0,), (1,)), ((), ())), preferred_element_type=jnp.float32
        ).astype(jnp.bfloat16),
        "feat",
        scatter_dimension=0,
        tiled=True,
    ).astype(jnp.float32)
    own_t = own_b.T.astype(jnp.float32)
    mean_grad = jnp.mean(col_grad, axis=1, keepdims=True)
    mean_cross = jnp.mean(col_grad * own_t, axis=1, keepdims=True)
    grad_b_t = (scale_b[:, None] * (col_grad - mean_grad - own_t * mean_cross)).astype(jnp.bfloat16)
    returned = lax.all_to_all(grad_b_t, "sample", split_axis=1, concat_axis=0, tiled=True)
    grad_b = returned.T
    loss = lax.psum(loss_sum, ("sample", "feat")) / (cols_dev * blocks)
    return (loss, grad_a, grad_b)


def solution(mesh):
    in_specs = (P("sample", "feat"), P("sample", "feat"))
    out_specs = (P(), P("sample", "feat"), P("sample", "feat"))
    return jax.shard_map(body, mesh=mesh, in_specs=in_specs, out_specs=out_specs, check_vma=False)
```

profile of v0, /device:TPU:0, one launch (start us, length us, event | category | flops | bytes accessed | tf_op | source)
XLA Modules:
  0.0 370.2 jit_solution(4005084618769182151)
XLA Ops:
  7.2 0.0 all-gather.5.cloned.1.call-start
  7.2 1.2 convert_reduce_fusion.2
  8.4 34.9 %all-reduce.1 = (f32[1024]{0:T(1024)S(1)}, f32[1024]{0:T(1024)S(1)}, f32[1024]{0:T(1024)S(1)}, f32[1024]{0:T(1024)S(1)}) all-reduce(f32[1024]{0:T(1024)S(1)} %get-tuple-element.23, f32[1024]{0:T(1024)S(1)} %get-tuple-element.24, f32[1024]{0:T(1024)S(1)} %get-tuple-element.8, ...), channel_id=1, replica_groups=mesh['sample'=8,'feat'=16] {'sample'}, use_global_device_ids=true, to_apply=%region_3.0 | all-reduce | flops 4096 | bytes 32768 | tf_op jit(solution)/shard_map/psum | solution.py:21
  43.4 1.7 fusion.8
  45.1 0.0 all-gather.5.cloned.1.call-update
  45.1 0.0 all-gather.3.cloned.1.call-start
  45.2 1.7 fusion.5
  46.9 0.0 all-gather.3.cloned.1.call-update
  46.9 53.7 %all-gather.5.cloned.1.call-done = bf16[128,16384]{1,0:T(8,128)(2,1)} async-done(((bf16[128,1024]{1,0:T(8,128)(2,1)}), bf16[128,16384]{1,0:T(8,128)(2,1)}) %all-gather.5.cloned.1.call-update) | async-done | bytes 4194320 | tf_op jit(solution)/shard_map/all_gather | solution.py:39
  100.6 5.4 %copy.13 = bf16[16,8,128,128]{3,2,1,0:T(8,128)(2,1)} copy(bf16[16,8,128,128]{3,1,2,0:T(8,128)(2,1)} %bitcast.43) | data formatting | bytes 8388608
  106.0 6.9 %copy.7 = bf16[128,16,8,128]{0,3,1,2:T(8,128)(2,1)} copy(bf16[128,16,8,128]{3,2,1,0:T(8,128)(2,1)} %bitcast.42) | data formatting | bytes 8388608 | tf_op jit(solution)/shard_map/reshape | solution.py:41
  112.9 4.6 %all-to-all-start = ((bf16[128,8,2048]{0,2,1:T(8,128)(2,1)}), bf16[128,8,2048]{0,2,1:T(8,128)(2,1)}, u32[]{:S(2)}, u32[]{:S(2)}) async-start(bf16[128,8,2048]{0,2,1:T(8,128)(2,1)} %bitcast.41), calls=%async_computation | async-start | bytes 8388608 | tf_op jit(solution)/shard_map/all_to_all | solution.py:45
  117.5 0.0 reduce-scatter.3.cloned.1.call-start
  117.6 80.9 %all-gather.3.cloned.1.call-done = bf16[1024,1024]{1,0:T(8,128)(2,1)} async-done(((bf16[128,1024]{1,0:T(8,128)(2,1)}), bf16[1024,1024]{1,0:T(8,128)(2,1)}) %all-gather.3.cloned.1.call-update) | async-done | bytes 2097168 | tf_op jit(solution)/shard_map/all_gather | solution.py:37
  198.5 0.0 all-to-all-done
  198.5 9.5 %select_reduce_fusion = (f32[]{:T(128)}, f32[1024,2048]{1,0:T(8,128)S(1)}) fusion(s32[2048]{0:T(1024)S(1)} %fusion.23, pred[2048]{0:T(1024)(128)(4,1)S(1)} %fusion.22, bf16[1024,1024]{1,0:T(8,128)(2,1)} %all-gather.3.cloned.1.call-done, bf16[128,8,2048]{0,2,1:T(8,128)(2,1)} %all-to-all-done), kind=kOutput, calls=%fused_computation.1 | convolution fusion | flops 4313841664 | bytes 14690308 | tf_op jit(solution)/shard_map/dot_general | solution.py:49
  208.0 0.0 copy-start.2
  208.0 3.2 copy-done.2
  211.2 0.0 copy-start.1
  211.2 8.4 %convolution_convert_fusion.1 = bf16[1024,1024]{1,0:T(8,128)(2,1)} fusion(f32[1024,2048]{1,0:T(8,128)S(1)} %get-tuple-element.22, s32[2048]{0:T(1024)S(1)} %fusion.23, pred[2048]{0:T(1024)(128)(4,1)S(1)} %fusion.22, bf16[128,8,2048]{0,2,1:T(8,128)(2,1)} %all-to-all-done), kind=kOutput, calls=%fused_computation.6 | convolution fusion | flops 4310695936 | bytes 14690304 | tf_op jit(solution)/shard_map/dot_general | solution.py:67
  219.7 0.0 reduce-scatter.3.cloned.1.call-update
  219.7 0.0 reduce-scatter.5.cloned.1.call-start
  219.7 0.0 copy-done.1
  219.7 12.0 %convolution_convert_fusion = bf16[2048,1024]{1,0:T(8,128)(2,1)} fusion(bf16[1024,1024]{1,0:T(8,128)(2,1)S(1)} %copy-done.1, f32[1024,2048]{1,0:T(8,128)} %copy-done.2, s32[2048]{0:T(1024)S(1)} %fusion.23, pred[2048]{0:T(1024)(128)(4,1)S(1)} %fusion.22), kind=kOutput, calls=%fused_computation.5 | convolution fusion | flops 4311744512 | bytes 14690304 | tf_op jit(solution)/shard_map/dot_general | solution.py:83
  231.7 0.0 reduce-scatter.5.cloned.1.call-update
  231.7 0.1 dynamic_slice.6
  231.8 65.5 %psum.53 = f32[]{:T(128)} all-reduce(f32[]{:T(128)} %get-tuple-element.21), channel_id=1, replica_groups=mesh['sample'=8,'feat'=16] {'sample','feat'}, use_global_device_ids=true, to_apply=%region_9.10 | all-reduce | flops 1 | bytes 8 | tf_op jit(solution)/shard_map/psum | solution.py:96
  298.0 0.0 copy-start
  298.0 4.8 %copy_bitcast_fusion = bf16[1024,2048]{0,1:T(8,128)(2,1)} fusion(bf16[128,8,2048]{0,2,1:T(8,128)(2,1)} %all-to-all-done), kind=kLoop, calls=%fused_computation.4 | loop fusion | bytes 8388608 | tf_op jit(solution)/shard_map/all_to_all | solution.py:45
  302.8 0.0 reduce-scatter.3.cloned.1.call-done
  302.8 0.0 copy-done
  302.8 1.1 convert_reduce_fusion.1
  303.9 17.7 %all-reduce = (f32[1024]{0:T(1024)S(1)}, f32[1024]{0:T(1024)S(1)}) all-reduce(f32[1024]{0:T(1024)S(1)} %get-tuple-element.6, f32[1024]{0:T(1024)S(1)} %get-tuple-element.5), channel_id=1, replica_groups=mesh['sample'=8,'feat'=16] {'sample'}, use_global_device_ids=true, to_apply=%region_14.15 | all-reduce | flops 2048 | bytes 16384 | tf_op jit(solution)/shard_map/psum | solution.py:76
  321.7 25.1 %reduce-scatter.5.cloned.1.call-done = bf16[128,1024]{1,0:T(8,128)(2,1)} async-done(((bf16[2048,1024]{1,0:T(8,128)(2,1)}), bf16[128,1024]{1,0:T(8,128)(2,1)}) %reduce-scatter.5.cloned.1.call-update) | async-done | bytes 262160 | tf_op jit(solution)/shard_map/reduce_scatter | solution.py:82
  346.8 1.2 convert_reduce_fusion
  348.0 2.0 copy_bitcast_fusion.1
  350.0 4.4 %all-to-all-start.1 = ((bf16[128,8,128]{2,0,1:T(8,128)(2,1)}), bf16[128,8,128]{2,0,1:T(8,128)(2,1)S(1)}, u32[]{:S(2)}, u32[]{:S(2)}) async-start(bf16[128,8,128]{2,0,1:T(8,128)(2,1)} %copy_bitcast_fusion.1), calls=%async_computation.3 | async-start | bytes 524288 | tf_op jit(solution)/shard_map/all_to_all | solution.py:94
  354.4 1.8 fusion.3
  356.2 5.5 %all-to-all-done.1 = bf16[128,8,128]{2,0,1:T(8,128)(2,1)S(1)} async-done(((bf16[128,8,128]{2,0,1:T(8,128)(2,1)}), bf16[128,8,128]{2,0,1:T(8,128)(2,1)S(1)}, u32[]{:S(2)}, u32[]{:S(2)}) %all-to-all-start.1) | async-done | bytes 262176 | tf_op jit(solution)/shard_map/all_to_all | solution.py:94
  361.7 0.8 copy.10
  (8 shorter events, 0.1 us)
Async XLA Ops:
  7.2 93.5 %all-gather.5.cloned.1.call-start = ((), (), s32[]{:S(2)}) async-start(), calls=%async_computation.5 | async-start | bytes 4456448 | tf_op jit(solution)/shard_map/all_gather | solution.py:39
  45.1 153.4 %all-gather.3.cloned.1.call-start = ((), (), s32[]{:S(2)}) async-start(), calls=%async_computation.4 | async-start | bytes 2359296 | tf_op jit(solution)/shard_map/all_gather | solution.py:37
  112.9 85.6 %all-to-all-start = ((bf16[128,8,2048]{0,2,1:T(8,128)(2,1)}), bf16[128,8,2048]{0,2,1:T(8,128)(2,1)}, u32[]{:S(2)}, u32[]{:S(2)}) async-start(bf16[128,8,2048]{0,2,1:T(8,128)(2,1)} %bitcast.41), calls=%async_computation | async-start | bytes 8388608 | tf_op jit(solution)/shard_map/all_to_all | solution.py:45
  117.5 185.3 %reduce-scatter.3.cloned.1.call-start = ((), (), s32[]{:S(2)}) async-start(), calls=%async_computation.6 | async-start | bytes 2359296 | tf_op jit(solution)/shard_map/reduce_scatter | solution.py:72
  208.0 3.2 copy-start.2
  211.2 8.5 %copy-start.1 = (bf16[1024,1024]{1,0:T(8,128)(2,1)S(1)}, bf16[1024,1024]{1,0:T(8,128)(2,1)}, u32[]{:S(2)}) copy-start(bf16[1024,1024]{1,0:T(8,128)(2,1)} %all-gather.3.cloned.1.call-done) | copy-start | bytes 6291460
  219.7 127.1 %reduce-scatter.5.cloned.1.call-start = ((), (), s32[]{:S(2)}) async-start(), calls=%async_computation.7 | async-start | bytes 4456448 | tf_op jit(solution)/shard_map/reduce_scatter | solution.py:82
  298.0 4.8 %copy-start = (bf16[128,1024]{1,0:T(8,128)(2,1)S(1)}, bf16[128,1024]{1,0:T(8,128)(2,1)}, u32[]{:S(2)}) copy-start(bf16[128,1024]{1,0:T(8,128)(2,1)} %param.2) | copy-start | bytes 786436
  350.0 11.7 %all-to-all-start.1 = ((bf16[128,8,128]{2,0,1:T(8,128)(2,1)}), bf16[128,8,128]{2,0,1:T(8,128)(2,1)S(1)}, u32[]{:S(2)}, u32[]{:S(2)}) async-start(bf16[128,8,128]{2,0,1:T(8,128)(2,1)} %copy_bitcast_fusion.1), calls=%async_computation.3 | async-start | bytes 524288 | tf_op jit(solution)/shard_map/all_to_all | solution.py:94
Sparse Core Ops, SparseCore 0:
  45.2 55.3 all-gather.4
  102.8 95.5 all-gather.2
  219.8 43.6 reduce-scatter.2
  267.4 79.3 reduce-scatter.4
where the time goes:
time: 371 us; the launch traced here: 370 us
  waiting for transfers between devices  165 us (44%)
  blocking collectives  118 us (32%)
  matrix products  29.9 us (8%)
  local copies, waits for them, and re-layouts  21.2 us (6%)
  between operations  15.6 us (4%)
  other arithmetic  10.8 us (3%)
  starting transfers between devices  9.14 us (2%)
    all_gather x1, waiting for transfers between devices, body(): norm_a = lax.all_gather(local_a, 'sample', axis=0, tiled=True)  80.9 us
    psum x1, blocking collectives, body(): loss = lax.psum(loss_sum, ('sample', 'feat')) / (cols_dev * blocks)  65.5 us
    all_gather x1, waiting for transfers between devices, body(): wide_b = lax.all_gather(source_b, 'feat', axis=1, tiled=True)  53.7 us
    psum x1, blocking collectives, body(): lax.psum((jnp.sum(float_a, axis=0), jnp.sum(float_a * float_a, axis=0), j...  34.9 us
    reduce_scatter x1, waiting for transfers between devices, body(): lax.psum_scatter(lax.dot_general(factor_tile, norm_a, (((0,), (1,)), ((),...  25.1 us
    psum x1, blocking collectives, body(): lax.psum((jnp.sum(row_grad, axis=0), jnp.sum(row_grad * float_local, axis...  17.7 us
    dot_general x1, matrix products, body(): lax.dot_general(factor_tile, norm_a, (((0,), (1,)), ((), ())), preferred_...  12 us
    dot_general x1, matrix products, body(): lax.dot_general(norm_a, moved_b, (((0,), (0,)), ((), ())), preferred_elem...  9.54 us
  transfers between devices with their start and end apart: 6, of which 4 were waited for; matrix products, arithmetic and copies ran while one was open for 9% of the time, Pallas kernels for 0%

commit v1 on v0

v1 whole, which is shorter than its diff:
```python
import jax
import jax.numpy as jnp
from jax import lax
from jax.sharding import PartitionSpec as P

EPSILON = 1e-05
OFF_WEIGHT = 0.0051


def gather_rows(block, axis):
    members = lax.axis_size(axis)
    copies = jnp.broadcast_to(block[None], (members,) + block.shape)
    copies = copies.reshape((members * block.shape[0],) + block.shape[1:])
    return lax.all_to_all(copies, axis, split_axis=0, concat_axis=0, tiled=True)


def normalize(raw, inv_rows):
    floats = raw.astype(jnp.float32)
    mean = jnp.sum(floats, axis=0) * inv_rows
    variance = jnp.sum(floats * floats, axis=0) * inv_rows - mean * mean
    scale = lax.rsqrt(variance + EPSILON)
    return ((floats - mean) * scale).astype(jnp.bfloat16), mean, scale


def own_rows(view, mean, scale):
    return ((view.astype(jnp.float32) - mean) * scale).astype(jnp.bfloat16)


def gram_rows(own, full, first_row, shift):
    rows = lax.dot_general(own, full, (((1,), (1,)), ((), ())), preferred_element_type=jnp.float32)
    row_ids = first_row + lax.broadcasted_iota(jnp.int32, rows.shape, 0)
    col_ids = lax.broadcasted_iota(jnp.int32, rows.shape, 1)
    return jnp.where(row_ids == col_ids, rows - shift, rows).astype(jnp.bfloat16)


def body(view_a, view_b):
    rows_dev, cols_dev = view_a.shape
    groups = lax.axis_size("sample")
    blocks = lax.axis_size("feat")
    total_rows = rows_dev * groups
    total_cols = cols_dev * blocks
    inv_rows = 1.0 / total_rows
    first_row = lax.axis_index("sample") * rows_dev
    f32 = jnp.float32
    bf16 = jnp.bfloat16

    raw_a = gather_rows(view_a, "sample")
    raw_b = gather_rows(view_b, "sample")
    full_a, mean_a, scale_a = normalize(raw_a, inv_rows)
    full_b, mean_b, scale_b = normalize(raw_b, inv_rows)
    own_a = own_rows(view_a, mean_a, scale_a)
    own_b = own_rows(view_b, mean_b, scale_b)

    part_a = gram_rows(own_a, full_a, first_row, float(cols_dev))
    part_b = gram_rows(own_b, full_b, first_row, float(cols_dev))
    diag = jnp.sum(full_a.astype(f32) * full_b.astype(f32), axis=0) * inv_rows
    slope = (diag - 1.0) - OFF_WEIGHT * diag
    diag_loss = jnp.sum((1.0 - diag) * (1.0 - diag) - OFF_WEIGHT * diag * diag)
    high = diag_loss.astype(bf16)
    low = (diag_loss - high.astype(f32)).astype(bf16)
    lane = lax.broadcasted_iota(jnp.int32, (2 * rows_dev, 128), 1)
    extra = jnp.where(lane == 0, high, jnp.where(lane == 1, low, jnp.zeros((), bf16)))
    payload = jnp.concatenate([jnp.concatenate([part_a, part_b], axis=0), extra], axis=1)
    moved = lax.all_to_all(payload, "feat", split_axis=0, concat_axis=0, tiled=True)
    summed = jnp.sum(moved.reshape(blocks, -1, payload.shape[1]).astype(f32), axis=0)
    diag_total = summed[0, total_rows] + summed[0, total_rows + 1]
    gram = gather_rows(summed[:, :total_rows].astype(bf16), "feat")
    gram_a, gram_b = gram[:rows_dev], gram[rows_dev:]

    factor = OFF_WEIGHT * inv_rows
    shift = factor * total_cols
    norm_a = own_a.astype(f32)
    norm_b = own_b.astype(f32)
    grad_na = (
        factor * jnp.dot(gram_b, full_a, preferred_element_type=f32)
        + shift * norm_a
        + slope * norm_b
    )
    grad_nb = (
        factor * jnp.dot(gram_a, full_b, preferred_element_type=f32)
        + shift * norm_b
        + slope * norm_a
    )

    row_ids = first_row + lax.broadcasted_iota(jnp.int32, gram_a.shape, 0)
    col_ids = lax.broadcasted_iota(jnp.int32, gram_a.shape, 1)
    back = jnp.where(row_ids == col_ids, f32(total_cols), f32(0.0))
    square = jnp.sum((gram_a.astype(f32) + back) * (gram_b.astype(f32) + back))
    stats = jnp.stack(
        [
            jnp.sum(grad_na, axis=0),
            jnp.sum(grad_na * norm_a, axis=0),
            jnp.sum(grad_nb, axis=0),
            jnp.sum(grad_nb * norm_b, axis=0),
            jnp.broadcast_to(square, (cols_dev,)),
        ]
        + [jnp.zeros((cols_dev,), f32)] * 3
    )
    stats = jnp.sum(gather_rows(stats, "sample").reshape(groups, 8, cols_dev), axis=0)
    means = stats[:4] * inv_rows
    grad_a = (scale_a * (grad_na - means[0] - norm_a * means[1])).astype(bf16)
    grad_b = (scale_b * (grad_nb - means[2] - norm_b * means[3])).astype(bf16)
    loss = (diag_total + OFF_WEIGHT * (stats[4, 0] * (inv_rows * inv_rows))) / total_cols
    return (loss, grad_a, grad_b)


def solution(mesh):
    in_specs = (P("sample", "feat"), P("sample", "feat"))
    out_specs = (P(), P("sample", "feat"), P("sample", "feat"))
    return jax.shard_map(body, mesh=mesh, in_specs=in_specs, out_specs=out_specs, check_vma=False)
```

time: 371 us -> 136 us (0.37)
  waiting for transfers between devices: 165 us -> 41.3 us
  blocking collectives: 118 us -> 53.2 us
  matrix products: 29.9 us -> 3.63 us
  local copies, waits for them, and re-layouts: 21.2 us -> 6.89 us
  between operations: 15.6 us -> 5.25 us
    all_gather x2 -> x0, waiting for transfers between devices: 135 us -> none  [the longest x1 80.9 us: body(): norm_a = lax.all_gather(local_a, 'sample', axis=0, tiled=True)]
    psum x3 -> x0, blocking collectives: 118 us -> none  [the longest x1 65.5 us: body(): loss = lax.psum(loss_sum, ('sample', 'feat')) / (cols_dev * blocks)]
    all_to_all x0 -> x2, blocking collectives: none -> 53.2 us  [the longest x1 32.8 us: gather_rows(): return lax.all_to_all(copies, axis, split_axis=0, concat_axis=0, tiled=True)]
    all_to_all x2 -> x3, waiting for transfers between devices: 5.48 us -> 41.3 us  [gather_rows(): return lax.all_to_all(copies, axis, split_axis=0, concat_axis=0, tiled=True)]
    dot_general x3 -> x4, matrix products: 29.9 us -> 3.63 us  [the longest x2 1.67 us: gram_rows(): lax.dot_general(own, full, (((1,), (1,)), ((), ())), preferred_element_ty...]
    reduce_scatter x2 -> x0, waiting for transfers between devices: 25.1 us -> none  [the longest x1 25.1 us: body(): lax.psum_scatter(lax.dot_general(factor_tile, norm_a, (((0,), (1,)), ((),...]
    unnamed x7 -> x10, local copies, waits for them, and re-layouts: 8.63 us -> 0.62 us
    reshape x1 -> x0, local copies, waits for them, and re-layouts: 6.87 us -> none  [body(): wide_b.reshape(rows_dev, blocks, groups, sub_width).transpose(0, 2, 1, 3)]
  transfers between devices with their start and end apart: 6 -> 3, of which waited for: 4 -> 3; matrix products, arithmetic and copies ran while one was open for 9% -> 2% of each run, Pallas kernels for 0% -> 0%
where the time goes in v1:
time: 136 us; the launch traced here: 135 us
  blocking collectives  53.2 us (39%)
  waiting for transfers between devices  41.3 us (30%)
  other arithmetic  13.3 us (10%)
  starting transfers between devices  11.3 us (8%)
  local copies, waits for them, and re-layouts  6.89 us (5%)
  between operations  5.25 us (4%)
  matrix products  3.63 us (3%)
    all_to_all x3, waiting for transfers between devices, gather_rows(): return lax.all_to_all(copies, axis, split_axis=0, concat_axis=0, tiled=True)  41.3 us
    all_to_all x1, blocking collectives, gather_rows(): return lax.all_to_all(copies, axis, split_axis=0, concat_axis=0, tiled=True)  32.8 us
    all_to_all x1, blocking collectives, body(): lax.all_to_all(payload, 'feat', split_axis=0, concat_axis=0, tiled=True)  20.5 us
    all_to_all x3, starting transfers between devices, gather_rows(): return lax.all_to_all(copies, axis, split_axis=0, concat_axis=0, tiled=True)  11.3 us
    reduce_sum x1, other arithmetic, body(): diag = jnp.sum(full_a.astype(f32) * full_b.astype(f32), axis=0) * inv_rows  4.89 us
    broadcast_in_dim x4, local copies, waits for them, and re-layouts, gather_rows(): copies = jnp.broadcast_to(block[None], (members,) + block.shape)  4.4 us
    reduce_sum x2, other arithmetic, normalize(): mean = jnp.sum(floats, axis=0) * inv_rows  2.8 us
    convert_element_type x2, other arithmetic, normalize(): return (((floats - mean) * scale).astype(jnp.bfloat16), mean, scale)  2.74 us
  transfers between devices with their start and end apart: 3, of which 3 were waited for; matrix products, arithmetic and copies ran while one was open for 2% of the time, Pallas kernels for 0%

profile of v1, /device:TPU:0, one launch (start us, length us, event | category | flops | bytes accessed | tf_op | source)
XLA Modules:
  0.0 134.9 jit_solution(14718167386824538526)
XLA Ops:
  0.6 1.2 broadcast_in_dim.26
  1.8 0.0 copy-start.3
  1.9 32.8 %all_to_all.30 = bf16[8,128,1024]{2,1,0:T(8,128)(2,1)S(1)} all-to-all(bf16[8,128,1024]{2,1,0:T(8,128)(2,1)S(1)} %broadcast_in_dim.26), channel_id=1, replica_groups=mesh['sample'=8,'feat'=16] {'sample'}, dimensions={0} | all-to-all | bytes 4194304 | tf_op jit(solution)/shard_map/all_to_all | solution.py:14
  34.6 0.0 copy-done.3
  34.6 1.6 %broadcast_in_dim.27 = bf16[8,128,1024]{2,1,0:T(8,128)(2,1)} broadcast(bf16[128,1024]{1,0:T(8,128)(2,1)S(1)} %copy-done.3), dimensions={1,2} | broadcast | bytes 2359296 | tf_op jit(solution)/shard_map/broadcast_in_dim | solution.py:12
  36.2 4.3 %all-to-all-start.1 = ((bf16[8,128,1024]{2,1,0:T(8,128)(2,1)}), bf16[8,128,1024]{2,1,0:T(8,128)(2,1)}, u32[]{:S(2)}, u32[]{:S(2)}) async-start(bf16[8,128,1024]{2,1,0:T(8,128)(2,1)} %broadcast_in_dim.27), calls=%async_computation.1 | async-start | bytes 4194304 | tf_op jit(solution)/shard_map/all_to_all | solution.py:14
  40.6 0.6 convert_reduce_fusion.1
  41.2 0.0 copy-start.2
  41.2 0.6 fusion.3
  41.8 0.4 copy-done.2
  42.2 0.8 fusion.10
  43.0 23.7 %all-to-all-done.1 = bf16[8,128,1024]{2,1,0:T(8,128)(2,1)} async-done(((bf16[8,128,1024]{2,1,0:T(8,128)(2,1)}), bf16[8,128,1024]{2,1,0:T(8,128)(2,1)}, u32[]{:S(2)}, u32[]{:S(2)}) %all-to-all-start.1) | async-done | bytes 2097184 | tf_op jit(solution)/shard_map/all_to_all | solution.py:14
  66.7 2.2 %convert_reduce_fusion = (f32[1024]{0:T(1024)S(1)}, f32[1024]{0:T(1024)S(1)}) fusion(bf16[8,128,1024]{2,1,0:T(8,128)(2,1)} %all-to-all-done.1), kind=kLoop, calls=%fused_computation.11 | loop fusion | flops 4192256 | bytes 2105344 | tf_op jit(solution)/shard_map/reduce_sum | solution.py:19
  68.9 2.2 %fusion.1 = bf16[1024,1024]{1,0:T(8,128)(2,1)S(1)} fusion(bf16[8,128,1024]{2,1,0:T(8,128)(2,1)} %all-to-all-done.1, f32[1024]{0:T(1024)S(1)} %get-tuple-element.25, f32[1024]{0:T(1024)S(1)} %get-tuple-element.24), kind=kLoop, calls=%fused_computation.2 | loop fusion | flops 4194304 | bytes 4202496 | tf_op jit(solution)/shard_map/convert_element_type | solution.py:22
  71.1 0.8 fusion.11
  71.9 4.9 %multiply_reduce_fusion = (f32[1024]{0:T(1024)S(1)}, bf16[8,128,1024]{2,1,0:T(8,128)(2,1)}, bf16[8,128,1024]{2,1,0:T(8,128)(2,1)}) fusion(f32[1024]{0:T(1024)S(1)} %get-tuple-element.27, f32[1024]{0:T(1024)S(1)} %get-tuple-element.26, bf16[8,128,1024]{2,1,0:T(8,128)(2,1)S(1)} %all_to_all.30, f32[1024]{0:T(1024)S(1)} %get-tuple-element.25, ...), kind=kLoop, calls=%fused_computation.6 | loop fusion | flops 12581888 | bytes 8409088 | tf_op jit(solution)/shard_map/reduce_sum | solution.py:56
  76.8 0.6 add_subtract_fusion
  78.8 0.0 copy-start.1
  78.8 20.5 %all_to_all.31 = bf16[16,16,1152]{2,1,0:T(8,128)(2,1)S(1)} all-to-all(bf16[16,16,1152]{2,1,0:T(8,128)(2,1)S(1)} %pad_maximum_fusion), channel_id=1, replica_groups=mesh['sample'=8,'feat'=16] {'feat'}, dimensions={0} | all-to-all | bytes 1179648 | tf_op jit(solution)/shard_map/all_to_all | solution.py:64
  99.3 0.1 convert_reduce_fusion.2
  99.4 0.9 broadcast_in_dim.33
  100.2 3.6 %all-to-all-start.3 = ((bf16[16,16,1024]{2,1,0:T(8,128)(2,1)}), bf16[16,16,1024]{2,1,0:T(8,128)(2,1)S(1)}, u32[]{:S(2)}, u32[]{:S(2)}) async-start(bf16[16,16,1024]{2,1,0:T(8,128)(2,1)} %broadcast_in_dim.33), calls=%async_computation.3 | async-start | bytes 1048576 | tf_op jit(solution)/shard_map/all_to_all | solution.py:14
  103.8 12.3 %all-to-all-done.3 = bf16[16,16,1024]{2,1,0:T(8,128)(2,1)S(1)} async-done(((bf16[16,16,1024]{2,1,0:T(8,128)(2,1)}), bf16[16,16,1024]{2,1,0:T(8,128)(2,1)S(1)}, u32[]{:S(2)}, u32[]{:S(2)}) %all-to-all-start.3) | async-done | bytes 524320 | tf_op jit(solution)/shard_map/all_to_all | solution.py:14
  116.2 0.0 copy-start
  116.2 0.0 copy-done.1
  116.2 1.4 %fusion.16 = (f32[1024]{0:T(1024)S(1)}, f32[1024]{0:T(1024)S(1)}, f32[128,1024]{1,0:T(8,128)}) fusion(f32[1024]{0:T(1024)S(1)} %get-tuple-element.25, f32[1024]{0:T(1024)S(1)} %get-tuple-element.24, bf16[128,1024]{1,0:T(8,128)(2,1)S(1)} %copy-done.3, f32[1024]{0:T(1024)S(1)} %get-tuple-element.27, f32[1024]{0:T(1024)S(1)} %get-tuple-element.26, ...), kind=kOutput, calls=%fused_computation.41 | convolution fusion | flops 270792704 | bytes 3436544 | tf_op jit(solution)/shard_map/dot_general | solution.py:80
  117.6 0.2 copy-done
  117.8 0.0 copy-start.4
  117.8 0.6 fusion.12
  118.4 1.0 fusion.9
  119.4 0.6 stack_broadcast_in_dim.6
  120.1 0.1 stack.23
  120.1 0.7 broadcast_in_dim.36
  120.9 3.4 %all-to-all-start.4 = ((f32[8,8,1024]{2,1,0:T(8,128)}), f32[8,8,1024]{2,1,0:T(8,128)S(1)}, u32[]{:S(2)}, u32[]{:S(2)}) async-start(f32[8,8,1024]{2,1,0:T(8,128)} %broadcast_in_dim.36), calls=%async_computation.4 | async-start | bytes 524288 | tf_op jit(solution)/shard_map/all_to_all | solution.py:14
  124.3 0.6 fusion.23
  126.2 5.3 %all-to-all-done.4 = f32[8,8,1024]{2,1,0:T(8,128)S(1)} async-done(((f32[8,8,1024]{2,1,0:T(8,128)}), f32[8,8,1024]{2,1,0:T(8,128)S(1)}, u32[]{:S(2)}, u32[]{:S(2)}) %all-to-all-start.4) | async-done | bytes 262176 | tf_op jit(solution)/shard_map/all_to_all | solution.py:14
  131.5 0.5 slice.58
  132.7 0.0 copy-done.4
  132.7 1.1 fusion.15
  (16 shorter events, 0.2 us)
Async XLA Ops:
  1.8 32.8 %copy-start.3 = (bf16[128,1024]{1,0:T(8,128)(2,1)S(1)}, bf16[128,1024]{1,0:T(8,128)(2,1)}, u32[]{:S(2)}) copy-start(bf16[128,1024]{1,0:T(8,128)(2,1)} %param.3) | copy-start | bytes 786436
  36.2 30.4 %all-to-all-start.1 = ((bf16[8,128,1024]{2,1,0:T(8,128)(2,1)}), bf16[8,128,1024]{2,1,0:T(8,128)(2,1)}, u32[]{:S(2)}, u32[]{:S(2)}) async-start(bf16[8,128,1024]{2,1,0:T(8,128)(2,1)} %broadcast_in_dim.27), calls=%async_computation.1 | async-start | bytes 4194304 | tf_op jit(solution)/shard_map/all_to_all | solution.py:14
  41.2 1.0 copy-start.2
  78.8 37.4 %copy-start.1 = (bf16[8,128,1024]{2,1,0:T(8,128)(2,1)S(1)}, bf16[8,128,1024]{2,1,0:T(8,128)(2,1)}, u32[]{:S(2)}) copy-start(bf16[8,128,1024]{2,1,0:T(8,128)(2,1)} %get-tuple-element.13) | copy-start | bytes 6291460
  100.2 15.9 %all-to-all-start.3 = ((bf16[16,16,1024]{2,1,0:T(8,128)(2,1)}), bf16[16,16,1024]{2,1,0:T(8,128)(2,1)S(1)}, u32[]{:S(2)}, u32[]{:S(2)}) async-start(bf16[16,16,1024]{2,1,0:T(8,128)(2,1)} %broadcast_in_dim.33), calls=%async_computation.3 | async-start | bytes 1048576 | tf_op jit(solution)/shard_map/all_to_all | solution.py:14
  116.2 1.6 %copy-start = (bf16[8,128,1024]{2,1,0:T(8,128)(2,1)S(1)}, bf16[8,128,1024]{2,1,0:T(8,128)(2,1)}, u32[]{:S(2)}) copy-start(bf16[8,128,1024]{2,1,0:T(8,128)(2,1)} %get-tuple-element.12) | copy-start | bytes 6291460
  117.8 14.9 %copy-start.4 = (f32[128,1024]{1,0:T(8,128)S(1)}, f32[128,1024]{1,0:T(8,128)}, u32[]{:S(2)}) copy-start(f32[128,1024]{1,0:T(8,128)} %get-tuple-element.29) | copy-start | bytes 1572868
  120.9 10.6 %all-to-all-start.4 = ((f32[8,8,1024]{2,1,0:T(8,128)}), f32[8,8,1024]{2,1,0:T(8,128)S(1)}, u32[]{:S(2)}, u32[]{:S(2)}) async-start(f32[8,8,1024]{2,1,0:T(8,128)} %broadcast_in_dim.36), calls=%async_computation.4 | async-start | bytes 524288 | tf_op jit(solution)/shard_map/all_to_all | solution.py:14

commit v2 on v1

v2 whole, which is shorter than its diff:
```python
import jax
import jax.numpy as jnp
from jax import lax
from jax.sharding import PartitionSpec as P

EPSILON = 1e-05
OFF_WEIGHT = 0.0051
RING = 4
CORES = 2
F32 = jnp.float32
BF16 = jnp.bfloat16


def send_sample(block, turn, step):
    pairs = lax.axis_size("sample") // RING
    moves = [
        (z * RING + y, (z + turn) % pairs * RING + (y + step) % RING)
        for z in range(pairs)
        for y in range(RING)
    ]
    return lax.ppermute(block, "sample", moves)


def swap_cores(block):
    return lax.ppermute(block, "feat", [(i, i ^ 1) for i in range(lax.axis_size("feat"))])


def exchange_chips(block):
    members = lax.axis_size("feat") // CORES
    groups = [[i * CORES + core for i in range(members)] for core in range(CORES)]
    return lax.all_to_all(
        block, "feat", split_axis=0, concat_axis=0, tiled=True, axis_index_groups=groups
    )


def repeat_block(block, members):
    copies = jnp.broadcast_to(block[None], (members,) + block.shape)
    return copies.reshape((members * block.shape[0],) + block.shape[1:])


def gather_views(a, b):
    rows = a.shape[0]
    half = rows // 2
    b_back = send_sample(b, 0, 1)
    b_on = send_sample(b, 0, -1)
    a_pair = jnp.concatenate([a, send_sample(a, 1, 0)])
    b_far = jnp.concatenate([send_sample(b_back[:half], 0, 1), send_sample(b_on[half:], 0, -1)])
    a_back = send_sample(a_pair, 0, 1)
    a_on = send_sample(a_pair, 0, -1)
    b_over = send_sample(jnp.concatenate([b, b_back, b_on]), 1, 0)
    a_far = send_sample(a_back[:rows], 0, 1)
    a_far_over = send_sample(a_on[rows:], 0, -1)
    b_far_over = send_sample(b_far, 1, 0)
    all_a = [a, a_back[:rows], a_on[:rows], a_far]
    all_a += [a_pair[rows:], a_back[rows:], a_on[rows:], a_far_over]
    all_b = [b, b_back, b_on, b_far, b_over, b_far_over]
    return jnp.concatenate(all_a), jnp.concatenate(all_b)


def normalize(raw, inv_rows):
    floats = raw.astype(F32)
    mean = jnp.sum(floats, axis=0) * inv_rows
    variance = jnp.sum(floats * floats, axis=0) * inv_rows - mean * mean
    scale = lax.rsqrt(variance + EPSILON)
    return ((floats - mean) * scale).astype(BF16), scale


def on_own(rows):
    row_ids = lax.broadcasted_iota(jnp.int32, rows.shape, 0)
    return row_ids == lax.broadcasted_iota(jnp.int32, rows.shape, 1)


def gram_rows(own, full, shift):
    rows = lax.dot_general(own, full, (((1,), (1,)), ((), ())), preferred_element_type=F32)
    return jnp.where(on_own(rows), rows - shift, rows)


def with_scalar(rows, value):
    high = value.astype(BF16)
    low = (value - high.astype(F32)).astype(BF16)
    lane = lax.broadcasted_iota(jnp.int32, (rows.shape[0], 128), 1)
    extra = jnp.where(lane == 0, high, jnp.where(lane == 1, low, jnp.zeros((), BF16)))
    return jnp.concatenate([rows.astype(BF16), extra], axis=1)


def body(view_a, view_b):
    rows_dev, cols_dev = view_a.shape
    groups = lax.axis_size("sample")
    blocks = lax.axis_size("feat")
    chips = blocks // CORES
    total_rows = rows_dev * groups
    total_cols = cols_dev * blocks
    inv_rows = 1.0 / total_rows
    first_core = lax.axis_index("feat") % CORES == 0

    raw_a, raw_b = gather_views(view_a, view_b)
    full_a, scale_a = normalize(raw_a, inv_rows)
    full_b, scale_b = normalize(raw_b, inv_rows)
    own_a = full_a[:rows_dev]
    own_b = full_b[:rows_dev]

    part_a = gram_rows(own_a, full_a, float(cols_dev))
    part_b = gram_rows(own_b, full_b, float(cols_dev))
    diag = jnp.sum(full_a.astype(F32) * full_b.astype(F32), axis=0) * inv_rows
    slope = (diag - 1.0) - OFF_WEIGHT * diag
    diag_loss = jnp.sum((1.0 - diag) * (1.0 - diag) - OFF_WEIGHT * diag * diag)

    other = swap_cores(with_scalar(jnp.where(first_core, part_b, part_a), diag_loss))
    other = other.astype(F32)
    kept = jnp.where(first_core, part_a, part_b) + other[:, :total_rows]
    chip_loss = diag_loss + (other[0, total_rows] + other[0, total_rows + 1])
    moved = exchange_chips(with_scalar(kept, chip_loss))
    summed = jnp.sum(moved.reshape(chips, -1, moved.shape[1]).astype(F32), axis=0)
    diag_total = summed[0, total_rows] + summed[0, total_rows + 1]
    mine = exchange_chips(repeat_block(summed[:, :total_rows].astype(BF16), chips))
    theirs = swap_cores(mine)
    gram_a = jnp.where(first_core, mine, theirs)
    gram_b = jnp.where(first_core, theirs, mine)

    factor = OFF_WEIGHT * inv_rows
    shift = factor * total_cols
    norm_a = own_a.astype(F32)
    norm_b = own_b.astype(F32)
    grad_na = (
        factor * jnp.dot(gram_b, full_a, preferred_element_type=F32)
        + shift * norm_a
        + slope * norm_b
    )
    grad_nb = (
        factor * jnp.dot(gram_a, full_b, preferred_element_type=F32)
        + shift * norm_b
        + slope * norm_a
    )

    back = jnp.where(on_own(gram_a), F32(total_cols), F32(0.0))
    square = jnp.sum((gram_a.astype(F32) + back) * (gram_b.astype(F32) + back))
    stats = jnp.stack(
        [
            jnp.sum(grad_na, axis=0),
            jnp.sum(grad_na * norm_a, axis=0),
            jnp.sum(grad_nb, axis=0),
            jnp.sum(grad_nb * norm_b, axis=0),
            jnp.broadcast_to(square, (cols_dev,)),
        ]
        + [jnp.zeros((cols_dev,), F32)] * 3
    )
    stats = lax.all_to_all(
        repeat_block(stats, groups), "sample", split_axis=0, concat_axis=0, tiled=True
    )
    stats = jnp.sum(stats.reshape(groups, 8, cols_dev), axis=0)
    means = stats[:4] * inv_rows
    grad_a = (scale_a * (grad_na - means[0] - norm_a * means[1])).astype(BF16)
    grad_b = (scale_b * (grad_nb - means[2] - norm_b * means[3])).astype(BF16)
    loss = (diag_total + OFF_WEIGHT * (stats[4, 0] * (inv_rows * inv_rows))) / total_cols
    return (loss, grad_a, grad_b)


def solution(mesh):
    in_specs = (P("sample", "feat"), P("sample", "feat"))
    out_specs = (P(), P("sample", "feat"), P("sample", "feat"))
    return jax.shard_map(body, mesh=mesh, in_specs=in_specs, out_specs=out_specs, check_vma=False)
```

time: 136 us -> 108 us (0.79)
  blocking collectives: 53.2 us -> 27.7 us
  starting transfers between devices: 11.3 us -> 21.7 us
  waiting for transfers between devices: 41.3 us -> 32.3 us
  other arithmetic: 13.3 us -> 9.09 us
  between operations: 5.25 us -> 7.34 us
  local copies, waits for them, and re-layouts: 6.89 us -> 5.47 us
    all_to_all x3 -> x1, waiting for transfers between devices: 41.3 us -> 5.69 us  [body(): lax.all_to_all(repeat_block(stats, groups), 'sample', split_axis=0, conca...]
    ppermute x0 -> x13, waiting for transfers between devices: none -> 26.6 us  [the longest x11 23.5 us: send_sample(): return lax.ppermute(block, 'sample', moves)]
    all_to_all x2, blocking collectives: 53.2 us -> 27.7 us  [exchange_chips(): lax.all_to_all(block, 'feat', split_axis=0, concat_axis=0, tiled=True, ax...]
    ppermute x0 -> x13, starting transfers between devices: none -> 17.5 us  [the longest x11 17.4 us: send_sample(): return lax.ppermute(block, 'sample', moves)]
    all_to_all x3 -> x1, starting transfers between devices: 11.3 us -> 4.23 us  [body(): lax.all_to_all(repeat_block(stats, groups), 'sample', split_axis=0, conca...]
    broadcast_in_dim x4 -> x2, local copies, waits for them, and re-layouts: 4.4 us -> 0.74 us  [repeat_block(): copies = jnp.broadcast_to(block[None], (members,) + block.shape)]
    convert_element_type x3, other arithmetic: 3.8 us -> 2.08 us  [the longest x1 1.95 us: body(): grad_a = (scale_a * (grad_na - means[0] - norm_a * means[1])).astype(BF16)]
    dot_general x2, matrix products: 1.67 us -> 3.34 us  [gram_rows(): lax.dot_general(own, full, (((1,), (1,)), ((), ())), preferred_element_ty...]
  transfers between devices with their start and end apart: 3 -> 14, of which waited for: 3 -> 8; matrix products, arithmetic and copies ran while one was open for 2% -> 3% of each run, Pallas kernels for 0% -> 0%
where the time goes in v2:
time: 108 us
  waiting for transfers between devices  32.3 us (30%)
  blocking collectives  27.7 us (26%)
  starting transfers between devices  21.7 us (20%)
  other arithmetic  9.09 us (8%)
  between operations  7.34 us (7%)
  local copies, waits for them, and re-layouts  5.47 us (5%)
  matrix products  4.44 us (4%)
    all_to_all x2, blocking collectives, exchange_chips(): lax.all_to_all(block, 'feat', split_axis=0, concat_axis=0, tiled=True, ax...  27.7 us
    ppermute x11, waiting for transfers between devices, send_sample(): return lax.ppermute(block, 'sample', moves)  23.5 us
    ppermute x11, starting transfers between devices, send_sample(): return lax.ppermute(block, 'sample', moves)  17.4 us
    all_to_all x1, waiting for transfers between devices, body(): lax.all_to_all(repeat_block(stats, groups), 'sample', split_axis=0, conca...  5.69 us
    all_to_all x1, starting transfers between devices, body(): lax.all_to_all(repeat_block(stats, groups), 'sample', split_axis=0, conca...  4.23 us
    reduce_sum x1, other arithmetic, body(): diag = jnp.sum(full_a.astype(F32) * full_b.astype(F32), axis=0) * inv_rows  4.19 us
    dot_general x2, matrix products, gram_rows(): lax.dot_general(own, full, (((1,), (1,)), ((), ())), preferred_element_ty...  3.34 us
    ppermute x2, waiting for transfers between devices, swap_cores(): lax.ppermute(block, 'feat', [(i, i ^ 1) for i in range(lax.axis_size('fea...  3.1 us
  transfers between devices with their start and end apart: 14, of which 8 were waited for; matrix products, arithmetic and copies ran while one was open for 3% of the time, Pallas kernels for 0%

profile of v2, /device:TPU:0, one launch (start us, length us, event | category | flops | bytes accessed | tf_op | source)
XLA Modules:
  0.0 108.0 jit_solution(16193995799328086979)
XLA Ops:
  0.6 1.7 %collective-permute-start.5 = (bf16[128,1024]{1,0:T(8,128)(2,1)}, bf16[128,1024]{1,0:T(8,128)(2,1)S(1)}, u32[]{:S(2)}, u32[]{:S(2)}) collective-permute-start(bf16[128,1024]{1,0:T(8,128)(2,1)} %param.3), channel_id=1, source_target_pairs={{0,16},{16,32},{32,48},{48,0},{64,80},{80,96},{96,112},{112,64},{1... | collective-permute-start | bytes 786440 | tf_op jit(solution)/shard_map/ppermute | solution.py:21
  2.4 1.6 %collective-permute-start.6 = (bf16[128,1024]{1,0:T(8,128)(2,1)}, bf16[128,1024]{1,0:T(8,128)(2,1)S(1)}, u32[]{:S(2)}, u32[]{:S(2)}) collective-permute-start(bf16[128,1024]{1,0:T(8,128)(2,1)} %param.3), channel_id=1, source_target_pairs={{0,48},{16,0},{32,16},{48,32},{64,112},{80,64},{96,80},{112,96},{1... | collective-permute-start | bytes 786440 | tf_op jit(solution)/shard_map/ppermute | solution.py:21
  3.9 2.0 %collective-permute-start = (bf16[128,1024]{1,0:T(8,128)(2,1)}, bf16[128,1024]{1,0:T(8,128)(2,1)S(1)}, u32[]{:S(2)}, u32[]{:S(2)}) collective-permute-start(bf16[128,1024]{1,0:T(8,128)(2,1)} %param.2), channel_id=1, source_target_pairs={{0,64},{16,80},{32,96},{48,112},{64,0},{80,16},{96,32},{112,48},{1... | collective-permute-start | bytes 786440 | tf_op jit(solution)/shard_map/ppermute | solution.py:21
  5.9 1.0 constant_dynamic-update-slice_fusion.14
  6.9 1.0 constant_dynamic-update-slice_fusion.1
  7.9 4.1 %collective-permute-done = bf16[128,1024]{1,0:T(8,128)(2,1)S(1)} collective-permute-done((bf16[128,1024]{1,0:T(8,128)(2,1)}, bf16[128,1024]{1,0:T(8,128)(2,1)S(1)}, u32[]{:S(2)}, u32[]{:S(2)}) %collective-permute-start) | collective-permute-done | bytes 262176 | tf_op jit(solution)/shard_map/ppermute | solution.py:21
  12.1 0.3 collective-permute-start.1
  12.4 3.0 %collective-permute-start.2 = (bf16[256,1024]{1,0:T(8,128)(2,1)S(1)}, bf16[256,1024]{1,0:T(8,128)(2,1)S(1)}, u32[]{:S(2)}, u32[]{:S(2)}) collective-permute-start(bf16[256,1024]{1,0:T(8,128)(2,1)S(1)} %constant_dynamic-update-slice_fusion), channel_id=1, source_target_pairs={{0,48},{16,0},{32,16},{48,32},{64,112},{80,64},{96,80},{112,96},{1... | collective-permute-start | bytes 1572872 | tf_op jit(solution)/shard_map/ppermute | solution.py:21
  15.4 0.1 collective-permute-start.7
  15.5 0.0 collective-permute-done.6
  15.5 3.3 %collective-permute-start.8 = (bf16[64,1024]{1,0:T(8,128)(2,1)S(1)}, bf16[64,1024]{1,0:T(8,128)(2,1)S(1)}, u32[]{:S(2)}, u32[]{:S(2)}) collective-permute-start(bf16[64,1024]{1,0:T(8,128)(2,1)S(1)} %slice.89), channel_id=1, source_target_pairs={{0,48},{16,0},{32,16},{48,32},{64,112},{80,64},{96,80},{112,96},{1... | collective-permute-start | bytes 393224 | tf_op jit(solution)/shard_map/ppermute | solution.py:21
  18.8 0.1 pad_maximum_fusion
  18.8 1.8 %collective-permute-start.9 = (bf16[384,1024]{1,0:T(8,128)(2,1)S(1)}, bf16[384,1024]{1,0:T(8,128)(2,1)S(1)}, u32[]{:S(2)}, u32[]{:S(2)}) collective-permute-start(bf16[384,1024]{1,0:T(8,128)(2,1)S(1)} %pad_maximum_fusion), channel_id=1, source_target_pairs={{0,64},{16,80},{32,96},{48,112},{64,0},{80,16},{96,32},{112,48},{1... | collective-permute-start | bytes 2359304 | tf_op jit(solution)/shard_map/ppermute | solution.py:21
  20.7 8.1 %collective-permute-done.7 = bf16[64,1024]{1,0:T(8,128)(2,1)S(1)} collective-permute-done((bf16[64,1024]{1,0:T(8,128)(2,1)S(1)}, bf16[64,1024]{1,0:T(8,128)(2,1)S(1)}, u32[]{:S(2)}, u32[]{:S(2)}) %collective-permute-start.7) | collective-permute-done | bytes 131104 | tf_op jit(solution)/shard_map/ppermute | solution.py:21
  28.8 1.5 %collective-permute-start.10 = (bf16[128,1024]{1,0:T(8,128)(2,1)S(1)}, bf16[128,1024]{1,0:T(8,128)(2,1)S(1)}, u32[]{:S(2)}, u32[]{:S(2)}) collective-permute-start(bf16[128,1024]{1,0:T(8,128)(2,1)S(1)} %pad_maximum_fusion.3), channel_id=1, source_target_pairs={{0,64},{16,80},{32,96},{48,112},{64,0},{80,16},{96,32},{112,48},{1... | collective-permute-start | bytes 786440 | tf_op jit(solution)/shard_map/ppermute | solution.py:21
  30.4 0.2 collective-permute-start.3
  30.6 0.0 collective-permute-done.2
  30.7 7.4 %collective-permute-done.3 = bf16[128,1024]{1,0:T(8,128)(2,1)S(1)} collective-permute-done((bf16[128,1024]{1,0:T(8,128)(2,1)S(1)}, bf16[128,1024]{1,0:T(8,128)(2,1)S(1)}, u32[]{:S(2)}, u32[]{:S(2)}) %collective-permute-start.3) | collective-permute-done | bytes 262176 | tf_op jit(solution)/shard_map/ppermute | solution.py:21
  38.1 0.1 fusion.27
  38.2 1.8 %collective-permute-start.4 = (bf16[128,1024]{1,0:T(8,128)(2,1)S(1)}, bf16[128,1024]{1,0:T(8,128)(2,1)S(1)}, u32[]{:S(2)}, u32[]{:S(2)}) collective-permute-start(bf16[128,1024]{1,0:T(8,128)(2,1)S(1)} %get-tuple-element.14), channel_id=1, source_target_pairs={{0,48},{16,0},{32,16},{48,32},{64,112},{80,64},{96,80},{112,96},{1... | collective-permute-start | bytes 786440 | tf_op jit(solution)/shard_map/ppermute | solution.py:21
  40.0 0.0 collective-permute-done.9
  40.0 0.1 constant_dynamic-update-slice_fusion.9
  40.0 1.6 %collective-permute-done.10 = bf16[128,1024]{1,0:T(8,128)(2,1)S(1)} collective-permute-done((bf16[128,1024]{1,0:T(8,128)(2,1)S(1)}, bf16[128,1024]{1,0:T(8,128)(2,1)S(1)}, u32[]{:S(2)}, u32[]{:S(2)}) %collective-permute-start.10) | collective-permute-done | bytes 262176 | tf_op jit(solution)/shard_map/ppermute | solution.py:21
  41.7 0.6 convert_reduce_fusion
  42.3 2.3 %collective-permute-done.4 = bf16[128,1024]{1,0:T(8,128)(2,1)S(1)} collective-permute-done((bf16[128,1024]{1,0:T(8,128)(2,1)S(1)}, bf16[128,1024]{1,0:T(8,128)(2,1)S(1)}, u32[]{:S(2)}, u32[]{:S(2)}) %collective-permute-start.4) | collective-permute-done | bytes 262176 | tf_op jit(solution)/shard_map/ppermute | solution.py:21
  44.6 0.6 convert_reduce_fusion.1
  45.3 4.2 %multiply_reduce_fusion = (f32[1024]{0:T(1024)S(1)}, bf16[1024,1024]{1,0:T(8,128)(2,1)}, bf16[1024,1024]{1,0:T(8,128)(2,1)S(1)}) fusion(f32[1024]{0:T(1024)S(1)} %get-tuple-element.33, f32[1024]{0:T(1024)S(1)} %get-tuple-element.32, bf16[1024,1024]{1,0:T(8,128)(2,1)S(1)} %constant_dynamic-update-slice_fusion.2, f32[1024]{0:T(1024)S(1)} %get-tuple-element.31, ...), kind=kLoop, calls=%fused_computation.12 | loop fusion | flops 12581888 | bytes 8409088 | tf_op jit(solution)/shard_map/reduce_sum | solution.py:104
  49.5 0.8 fusion.21
  50.3 0.6 add_subtract_fusion
  52.2 2.5 %select_convert_fusion = (bf16[128,1024]{1,0:T(8,128)(2,1)S(1)}, f32[128,1024]{1,0:T(8,128)S(1)}) fusion(f32[128,1024]{1,0:T(8,128)S(1)} %fusion.21, pred[]{:T(512)S(6)} %eq.30, bf16[1024,1024]{1,0:T(8,128)(2,1)} %get-tuple-element.12), kind=kOutput, calls=%fused_computation.45 | convolution fusion | flops 269352960 | bytes 3670017 | tf_op jit(solution)/shard_map/dot_general | solution.py:74
  54.8 0.1 collective-permute-start.11
  54.9 1.6 %collective-permute-done.11 = bf16[128,1152]{1,0:T(8,128)(2,1)S(1)} collective-permute-done((bf16[128,1152]{1,0:T(8,128)(2,1)S(1)}, bf16[128,1152]{1,0:T(8,128)(2,1)S(1)}, u32[]{:S(2)}, u32[]{:S(2)}) %collective-permute-start.11) | collective-permute-done | bytes 294944 | tf_op jit(solution)/shard_map/ppermute | solution.py:25
  56.4 0.6 fusion.29
  59.1 0.1 fusion.20
  59.2 16.8 %all_to_all.24 = bf16[8,16,1152]{2,1,0:T(8,128)(2,1)S(1)} all-to-all(bf16[8,16,1152]{2,1,0:T(8,128)(2,1)S(1)} %bitcast.17), channel_id=1, replica_groups={{0,2,4,6,8,10,12,14},{1,3,5,7,9,11,13,15},{16,18,20,22,24,26,28,30},{17..., dimensions={0} | all-to-all | bytes 589824 | tf_op jit(solution)/shard_map/all_to_all | solution.py:31
  76.1 10.9 %all_to_all.25 = bf16[8,16,1024]{2,1,0:T(8,128)(2,1)S(1)} all-to-all(bf16[8,16,1024]{2,1,0:T(8,128)(2,1)S(1)} %broadcast_in_dim.52), channel_id=1, replica_groups={{0,2,4,6,8,10,12,14},{1,3,5,7,9,11,13,15},{16,18,20,22,24,26,28,30},{17..., dimensions={0} | all-to-all | bytes 524288 | tf_op jit(solution)/shard_map/all_to_all | solution.py:31
  87.0 1.5 %collective-permute-done.12 = bf16[128,1024]{1,0:T(8,128)(2,1)S(1)} collective-permute-done((bf16[128,1024]{1,0:T(8,128)(2,1)S(1)}, bf16[128,1024]{1,0:T(8,128)(2,1)S(1)}, u32[]{:S(2)}, u32[]{:S(2)}) %collective-permute-start.12) | collective-permute-done | bytes 262176 | tf_op jit(solution)/shard_map/ppermute | solution.py:25
  88.5 0.8 fusion.11
  89.3 0.5 fusion.16
  89.8 0.6 fusion.12
  90.4 0.7 stack_broadcast_in_dim.6
  91.1 0.1 stack.23
  91.1 0.7 broadcast_in_dim.55
  91.8 4.2 %all-to-all-start.2 = ((f32[8,8,1024]{2,1,0:T(8,128)}), f32[8,8,1024]{2,1,0:T(8,128)S(1)}, u32[]{:S(2)}, u32[]{:S(2)}) async-start(f32[8,8,1024]{2,1,0:T(8,128)} %broadcast_in_dim.55), calls=%async_computation.2 | async-start | bytes 524288 | tf_op jit(solution)/shard_map/all_to_all | solution.py:147
  96.1 0.6 fusion.30
  98.0 5.7 %all-to-all-done.2 = f32[8,8,1024]{2,1,0:T(8,128)S(1)} async-done(((f32[8,8,1024]{2,1,0:T(8,128)}), f32[8,8,1024]{2,1,0:T(8,128)S(1)}, u32[]{:S(2)}, u32[]{:S(2)}) %all-to-all-start.2) | async-done | bytes 262176 | tf_op jit(solution)/shard_map/all_to_all | solution.py:147
  103.7 0.5 slice.97
  104.9 2.0 %fusion.15 = (bf16[128,1024]{1,0:T(8,128)(2,1)}, bf16[128,1024]{1,0:T(8,128)(2,1)}) fusion(f32[128,1024]{1,0:T(8,128)S(1)} %get-tuple-element.36, f32[1024]{0:T(1024)S(1)} %bitcast.23, f32[1024]{0:T(1024)S(1)} %bitcast.24, f32[1024]{0:T(1024)S(1)} %get-tuple-element.33, bf16[1024,1024]{1,0:T(8,128)(2,1)} %get-tuple-element.12, f32[1024]{0:T(1024)S(1)} %bitcast.22, ...), kind=kLoop, calls=%fused_computation.38 | loop fusion | flops 1572864 | bytes 2121728 | tf_op jit(solution)/shard_map/convert_element_type | solution.py:152
  (43 shorter events, 0.5 us)
Async XLA Ops:
  0.6 18.1 %copy-start.2 = (bf16[128,1024]{1,0:T(8,128)(2,1)S(1)}, bf16[128,1024]{1,0:T(8,128)(2,1)}, u32[]{:S(2)}) copy-start(bf16[128,1024]{1,0:T(8,128)(2,1)} %param.3) | copy-start | bytes 786436
  0.6 14.7 %collective-permute-start.5 = (bf16[128,1024]{1,0:T(8,128)(2,1)}, bf16[128,1024]{1,0:T(8,128)(2,1)S(1)}, u32[]{:S(2)}, u32[]{:S(2)}) collective-permute-start(bf16[128,1024]{1,0:T(8,128)(2,1)} %param.3), channel_id=1, source_target_pairs={{0,16},{16,32},{32,48},{48,0},{64,80},{80,96},{96,112},{112,64},{1... | collective-permute-start | bytes 786440 | tf_op jit(solution)/shard_map/ppermute | solution.py:21
  2.4 13.1 %collective-permute-start.6 = (bf16[128,1024]{1,0:T(8,128)(2,1)}, bf16[128,1024]{1,0:T(8,128)(2,1)S(1)}, u32[]{:S(2)}, u32[]{:S(2)}) collective-permute-start(bf16[128,1024]{1,0:T(8,128)(2,1)} %param.3), channel_id=1, source_target_pairs={{0,48},{16,0},{32,16},{48,32},{64,112},{80,64},{96,80},{112,96},{1... | collective-permute-start | bytes 786440 | tf_op jit(solution)/shard_map/ppermute | solution.py:21
  3.9 8.1 %collective-permute-start = (bf16[128,1024]{1,0:T(8,128)(2,1)}, bf16[128,1024]{1,0:T(8,128)(2,1)S(1)}, u32[]{:S(2)}, u32[]{:S(2)}) collective-permute-start(bf16[128,1024]{1,0:T(8,128)(2,1)} %param.2), channel_id=1, source_target_pairs={{0,64},{16,80},{32,96},{48,112},{64,0},{80,16},{96,32},{112,48},{1... | collective-permute-start | bytes 786440 | tf_op jit(solution)/shard_map/ppermute | solution.py:21
  12.1 18.3 %collective-permute-start.1 = (bf16[256,1024]{1,0:T(8,128)(2,1)S(1)}, bf16[256,1024]{1,0:T(8,128)(2,1)S(1)}, u32[]{:S(2)}, u32[]{:S(2)}) collective-permute-start(bf16[256,1024]{1,0:T(8,128)(2,1)S(1)} %constant_dynamic-update-slice_fusion), channel_id=1, source_target_pairs={{0,16},{16,32},{32,48},{48,0},{64,80},{80,96},{96,112},{112,64},{1... | collective-permute-start | bytes 1572872 | tf_op jit(solution)/shard_map/ppermute | solution.py:21
  12.4 18.3 %collective-permute-start.2 = (bf16[256,1024]{1,0:T(8,128)(2,1)S(1)}, bf16[256,1024]{1,0:T(8,128)(2,1)S(1)}, u32[]{:S(2)}, u32[]{:S(2)}) collective-permute-start(bf16[256,1024]{1,0:T(8,128)(2,1)S(1)} %constant_dynamic-update-slice_fusion), channel_id=1, source_target_pairs={{0,48},{16,0},{32,16},{48,32},{64,112},{80,64},{96,80},{112,96},{1... | collective-permute-start | bytes 1572872 | tf_op jit(solution)/shard_map/ppermute | solution.py:21
  15.4 13.4 %collective-permute-start.7 = (bf16[64,1024]{1,0:T(8,128)(2,1)S(1)}, bf16[64,1024]{1,0:T(8,128)(2,1)S(1)}, u32[]{:S(2)}, u32[]{:S(2)}) collective-permute-start(bf16[64,1024]{1,0:T(8,128)(2,1)S(1)} %slice.88), channel_id=1, source_target_pairs={{0,16},{16,32},{32,48},{48,0},{64,80},{80,96},{96,112},{112,64},{1... | collective-permute-start | bytes 393224 | tf_op jit(solution)/shard_map/ppermute | solution.py:21
  15.5 13.3 %collective-permute-start.8 = (bf16[64,1024]{1,0:T(8,128)(2,1)S(1)}, bf16[64,1024]{1,0:T(8,128)(2,1)S(1)}, u32[]{:S(2)}, u32[]{:S(2)}) collective-permute-start(bf16[64,1024]{1,0:T(8,128)(2,1)S(1)} %slice.89), channel_id=1, source_target_pairs={{0,48},{16,0},{32,16},{48,32},{64,112},{80,64},{96,80},{112,96},{1... | collective-permute-start | bytes 393224 | tf_op jit(solution)/shard_map/ppermute | solution.py:21
  18.8 21.2 %collective-permute-start.9 = (bf16[384,1024]{1,0:T(8,128)(2,1)S(1)}, bf16[384,1024]{1,0:T(8,128)(2,1)S(1)}, u32[]{:S(2)}, u32[]{:S(2)}) collective-permute-start(bf16[384,1024]{1,0:T(8,128)(2,1)S(1)} %pad_maximum_fusion), channel_id=1, source_target_pairs={{0,64},{16,80},{32,96},{48,112},{64,0},{80,16},{96,32},{112,48},{1... | collective-permute-start | bytes 2359304 | tf_op jit(solution)/shard_map/ppermute | solution.py:21
  28.8 12.9 %collective-permute-start.10 = (bf16[128,1024]{1,0:T(8,128)(2,1)S(1)}, bf16[128,1024]{1,0:T(8,128)(2,1)S(1)}, u32[]{:S(2)}, u32[]{:S(2)}) collective-permute-start(bf16[128,1024]{1,0:T(8,128)(2,1)S(1)} %pad_maximum_fusion.3), channel_id=1, source_target_pairs={{0,64},{16,80},{32,96},{48,112},{64,0},{80,16},{96,32},{112,48},{1... | collective-permute-start | bytes 786440 | tf_op jit(solution)/shard_map/ppermute | solution.py:21
  30.4 7.7 %collective-permute-start.3 = (bf16[128,1024]{1,0:T(8,128)(2,1)S(1)}, bf16[128,1024]{1,0:T(8,128)(2,1)S(1)}, u32[]{:S(2)}, u32[]{:S(2)}) collective-permute-start(bf16[128,1024]{1,0:T(8,128)(2,1)S(1)} %get-tuple-element.16), channel_id=1, source_target_pairs={{0,16},{16,32},{32,48},{48,0},{64,80},{80,96},{96,112},{112,64},{1... | collective-permute-start | bytes 786440 | tf_op jit(solution)/shard_map/ppermute | solution.py:21
  38.2 6.4 %collective-permute-start.4 = (bf16[128,1024]{1,0:T(8,128)(2,1)S(1)}, bf16[128,1024]{1,0:T(8,128)(2,1)S(1)}, u32[]{:S(2)}, u32[]{:S(2)}) collective-permute-start(bf16[128,1024]{1,0:T(8,128)(2,1)S(1)} %get-tuple-element.14), channel_id=1, source_target_pairs={{0,48},{16,0},{32,16},{48,32},{64,112},{80,64},{96,80},{112,96},{1... | collective-permute-start | bytes 786440 | tf_op jit(solution)/shard_map/ppermute | solution.py:21
  41.7 3.6 %copy-start.1 = (bf16[1024,1024]{1,0:T(8,128)(2,1)}, bf16[1024,1024]{1,0:T(8,128)(2,1)S(1)}, u32[]{:S(2)}) copy-start(bf16[1024,1024]{1,0:T(8,128)(2,1)S(1)} %constant_dynamic-update-slice_fusion.8) | copy-start | bytes 6291460
  54.8 1.7 %collective-permute-start.11 = (bf16[128,1152]{1,0:T(8,128)(2,1)S(1)}, bf16[128,1152]{1,0:T(8,128)(2,1)S(1)}, u32[]{:S(2)}, u32[]{:S(2)}) collective-permute-start(bf16[128,1152]{1,0:T(8,128)(2,1)S(1)} %pad_maximum_fusion.1), channel_id=1, source_target_pairs={{0,1},{1,0},{2,3},{3,2},{4,5},{5,4},{6,7},{7,6},{8,9},{9,8},{10,11... | collective-permute-start | bytes 884744 | tf_op jit(solution)/shard_map/ppermute | solution.py:25
  59.1 30.2 %copy-start = (bf16[1024,1024]{1,0:T(8,128)(2,1)S(1)}, bf16[1024,1024]{1,0:T(8,128)(2,1)}, u32[]{:S(2)}) copy-start(bf16[1024,1024]{1,0:T(8,128)(2,1)} %get-tuple-element.12) | copy-start | bytes 6291460
  87.0 1.5 %collective-permute-start.12 = (bf16[128,1024]{1,0:T(8,128)(2,1)S(1)}, bf16[128,1024]{1,0:T(8,128)(2,1)S(1)}, u32[]{:S(2)}, u32[]{:S(2)}) collective-permute-start(bf16[128,1024]{1,0:T(8,128)(2,1)S(1)} %bitcast.18), channel_id=1, source_target_pairs={{0,1},{1,0},{2,3},{3,2},{4,5},{5,4},{6,7},{7,6},{8,9},{9,8},{10,11... | collective-permute-start | bytes 786440 | tf_op jit(solution)/shard_map/ppermute | solution.py:25
  91.8 11.8 %all-to-all-start.2 = ((f32[8,8,1024]{2,1,0:T(8,128)}), f32[8,8,1024]{2,1,0:T(8,128)S(1)}, u32[]{:S(2)}, u32[]{:S(2)}) async-start(f32[8,8,1024]{2,1,0:T(8,128)} %broadcast_in_dim.55), calls=%async_computation.2 | async-start | bytes 524288 | tf_op jit(solution)/shard_map/all_to_all | solution.py:147

commit v3 on v2

v3 whole, which is shorter than its diff:
```python
import functools
import jax
import jax.numpy as jnp
from jax import lax
from jax.experimental import pallas as pl
from jax.experimental.pallas import tpu as pltpu
from jax.sharding import PartitionSpec as P

EPSILON = 1e-05
OFF_WEIGHT = 0.0051
RING = 4
CORES = 2
F32 = jnp.float32
BF16 = jnp.bfloat16
LANES = 128


def send_sample(block, turn, step):
    pairs = lax.axis_size("sample") // RING
    moves = [
        (z * RING + y, (z + turn) % pairs * RING + (y + step) % RING)
        for z in range(pairs)
        for y in range(RING)
    ]
    return lax.ppermute(block, "sample", moves)


def swap_cores(block):
    return lax.ppermute(block, "feat", [(i, i ^ 1) for i in range(lax.axis_size("feat"))])


def exchange_chips(block):
    members = lax.axis_size("feat") // CORES
    groups = [[i * CORES + core for i in range(members)] for core in range(CORES)]
    return lax.all_to_all(
        block, "feat", split_axis=0, concat_axis=0, tiled=True, axis_index_groups=groups
    )


def repeat_block(block, members):
    copies = jnp.broadcast_to(block[None], (members,) + block.shape)
    return copies.reshape((members * block.shape[0],) + block.shape[1:])


def gather_views(a, b):
    rows = a.shape[0]
    half = rows // 2
    b_back = send_sample(b, 0, 1)
    b_on = send_sample(b, 0, -1)
    a_pair = jnp.concatenate([a, send_sample(a, 1, 0)])
    b_far = jnp.concatenate([send_sample(b_back[:half], 0, 1), send_sample(b_on[half:], 0, -1)])
    a_back = send_sample(a_pair, 0, 1)
    a_on = send_sample(a_pair, 0, -1)
    b_over = send_sample(jnp.concatenate([b, b_back, b_on]), 1, 0)
    a_far = send_sample(a_back[:rows], 0, 1)
    a_far_over = send_sample(a_on[rows:], 0, -1)
    b_far_over = send_sample(b_far, 1, 0)
    parts_a = [a, a_back, a_on, a_far, a_pair[rows:], a_far_over]
    parts_b = [b, b_back, b_on, b_far, b_over, b_far_over]
    return parts_a, parts_b


def call(kernel, steps, args, outs, scratch=(), limit=16):
    def spec(shape, cut):
        rows, cols = shape
        if cut:
            return pl.BlockSpec((rows, cols // steps), lambda i: (0, i))
        return pl.BlockSpec((rows, cols), lambda i: (0, 0))

    def out_spec(out, cut):
        if out.shape == (1,):
            return pl.BlockSpec(memory_space=pltpu.SMEM)
        return spec(out.shape, cut)

    return pl.pallas_call(
        kernel,
        grid=(steps,),
        out_shape=[out for out, _ in outs],
        in_specs=[pl.BlockSpec(memory_space=pltpu.SMEM)] + [spec(x.shape, c) for x, c in args[1:]],
        out_specs=[out_spec(out, cut) for out, cut in outs],
        scratch_shapes=list(scratch),

    )(*[args[0]] + [x for x, _ in args[1:]])


def on_own(shape):
    row_ids = lax.broadcasted_iota(jnp.int32, shape, 0)
    return row_ids == lax.broadcasted_iota(jnp.int32, shape, 1)


def split_scalar(value, rows):
    wide = jnp.broadcast_to(value, (rows, LANES))
    high = wide.astype(BF16).astype(F32)
    lane = lax.broadcasted_iota(jnp.int32, wide.shape, 1)
    return jnp.where(lane < LANES // 2, high, (wide - high).astype(BF16).astype(F32))


def gram_kernel(core, *refs):
    a, a_back, a_on, a_far, a_over, a_far_over = refs[:6]
    b, b_back, b_on, b_far, b_over, b_far_over = refs[6:12]
    full_a, full_b, vecs, keep, send, part_a, part_b, loss = refs[12:]
    step = pl.program_id(0)
    steps = pl.num_programs(0)
    rows, cols = a.shape
    total_rows = full_a.shape[0]
    inv_rows = 1.0 / total_rows
    top, high = pl.ds(0, rows), pl.ds(rows, rows)
    raw_a = [(a, top), (a_back, top), (a_on, top), (a_far, top)]
    raw_a += [(a_over, top), (a_back, high), (a_on, high), (a_far_over, top)]
    raw_b = [(b, top), (b_back, top), (b_on, top), (b_far, top)]
    raw_b += [(b_over, pl.ds(i * rows, rows)) for i in range(3)] + [(b_far_over, top)]

    @pl.when(step == 0)
    def _():
        part_a[...] = jnp.zeros_like(part_a)
        part_b[...] = jnp.zeros_like(part_b)
        loss[...] = jnp.zeros_like(loss)

    def view(raw, full, part):
        floats = jnp.concatenate([ref[piece, :] for ref, piece in raw]).astype(F32)
        mean = jnp.sum(floats, axis=0, keepdims=True) * inv_rows
        square = jnp.sum(floats * floats, axis=0, keepdims=True) * inv_rows
        scale = lax.rsqrt(square - mean * mean + EPSILON)
        norm = ((floats - mean) * scale).astype(BF16)
        full[...] = norm
        part[...] += lax.dot_general(
            norm[:rows], norm, (((1,), (1,)), ((), ())), preferred_element_type=F32
        )
        return norm, scale

    norm_a, scale_a = view(raw_a, full_a, part_a)
    norm_b, scale_b = view(raw_b, full_b, part_b)
    diag = jnp.sum(norm_a.astype(F32) * norm_b.astype(F32), axis=0, keepdims=True) * inv_rows
    loss[...] += (1.0 - diag) * (1.0 - diag) - OFF_WEIGHT * diag * diag
    slope = (diag - 1.0) - OFF_WEIGHT * diag
    vecs[...] = jnp.concatenate([scale_a, scale_b, slope, jnp.zeros((5, cols), F32)])

    @pl.when(step == steps - 1)
    def _():
        own = on_own(part_a.shape)
        gram_a = part_a[...] - jnp.where(own, 1.0 * cols * steps, 0.0)
        gram_b = part_b[...] - jnp.where(own, 1.0 * cols * steps, 0.0)
        keep[:, total_rows:] = split_scalar(jnp.sum(loss[...], axis=1, keepdims=True), rows)
        send[:, total_rows:] = jnp.zeros((rows, LANES), BF16)

        @pl.when(core[0] == 0)
        def _():
            keep[:, :total_rows] = gram_a
            send[:, :total_rows] = gram_b.astype(BF16)

        @pl.when(core[0] != 0)
        def _():
            keep[:, :total_rows] = gram_b
            send[:, :total_rows] = gram_a.astype(BF16)


def grad_kernel(core, mine, theirs, full_a, full_b, vecs, grad_na, grad_nb, stats, *, total_cols):
    rows, total_rows = mine.shape
    cols = grad_na.shape[1]
    factor = OFF_WEIGHT / total_rows
    shift = factor * total_cols
    first = core[0] == 0
    gram_a = jnp.where(first, mine[...], theirs[...])
    gram_b = jnp.where(first, theirs[...], mine[...])
    norm_a = full_a[:rows, :].astype(F32)
    norm_b = full_b[:rows, :].astype(F32)
    slope = vecs[2:3, :]
    wide_a = jnp.dot(gram_b, full_a[...], preferred_element_type=F32)
    wide_b = jnp.dot(gram_a, full_b[...], preferred_element_type=F32)
    wide_a = factor * wide_a + shift * norm_a + slope * norm_b
    wide_b = factor * wide_b + shift * norm_b + slope * norm_a
    grad_na[...] = wide_a
    grad_nb[...] = wide_b
    sums = [
        jnp.sum(wide_a, axis=0, keepdims=True),
        jnp.sum(wide_a * norm_a, axis=0, keepdims=True),
        jnp.sum(wide_b, axis=0, keepdims=True),
        jnp.sum(wide_b * norm_b, axis=0, keepdims=True),
        jnp.zeros((4, cols), F32),
    ]
    sums = jnp.concatenate(sums)
    copies = stats.shape[0] // 8
    for member in range(copies):
        stats[pl.ds(member * 8, 8), :] = sums

    @pl.when(pl.program_id(0) == 0)
    def _():
        back = jnp.where(on_own(mine.shape), 1.0 * total_cols, 0.0)
        square = (gram_a.astype(F32) + back) * (gram_b.astype(F32) + back)
        square = jnp.sum(jnp.sum(square, axis=0, keepdims=True), axis=1, keepdims=True)
        for member in range(copies):
            stats[pl.ds(member * 8 + 4, 1), :] = jnp.broadcast_to(square, (1, cols))


def out_kernel(
    core, stats, grad_na, grad_nb, own_a, own_b, vecs, diag, grad_a, grad_b, loss, *, total_cols
):
    del core
    members = stats.shape[0] // 8
    inv_rows = 1.0 / (own_a.shape[0] * members)
    sums = stats[0:8, :]
    for member in range(1, members):
        sums += stats[pl.ds(member * 8, 8), :]
    means = sums * inv_rows
    norm_a = own_a[...].astype(F32)
    norm_b = own_b[...].astype(F32)
    wide_a = grad_na[...] - means[0:1] - norm_a * means[1:2]
    wide_b = grad_nb[...] - means[2:3] - norm_b * means[3:4]
    grad_a[...] = (vecs[0:1, :] * wide_a).astype(BF16)
    grad_b[...] = (vecs[1:2, :] * wide_b).astype(BF16)

    @pl.when(pl.program_id(0) == 0)
    def _():
        square = jnp.max(means[4:5, 0:LANES]) * inv_rows
        loss[0] = (jnp.max(diag[0:1, :]) + OFF_WEIGHT * square) / total_cols


def body(view_a, view_b):
    rows, cols = view_a.shape
    groups = lax.axis_size("sample")
    blocks = lax.axis_size("feat")
    chips = blocks // CORES
    total_rows = rows * groups
    total_cols = cols * blocks
    core = (lax.axis_index("feat") & (CORES - 1)).reshape(1)
    shape = jax.ShapeDtypeStruct

    parts_a, parts_b = gather_views(view_a, view_b)
    full_a, full_b, vecs, keep, send = call(
        gram_kernel,
        4,
        [core] + [(part, True) for part in parts_a + parts_b],
        [
            (shape((total_rows, cols), BF16), True),
            (shape((total_rows, cols), BF16), True),
            (shape((8, cols), F32), True),
            (shape((rows, total_rows + LANES), F32), False),
            (shape((rows, total_rows + LANES), BF16), False),
        ],
        [
            pltpu.VMEM((rows, total_rows), F32),
            pltpu.VMEM((rows, total_rows), F32),
            pltpu.VMEM((1, cols // 4), F32),
        ],
        limit=24,
    )
    total = (keep + swap_cores(send).astype(F32)).astype(BF16)
    moved = exchange_chips(total)
    summed = jnp.sum(moved.reshape(chips, -1, moved.shape[1]).astype(F32), axis=0)
    mine = exchange_chips(repeat_block(summed[:, :total_rows].astype(BF16), chips))
    diag = jnp.sum(summed[:8, total_rows:], axis=1, keepdims=True) * (2.0 / LANES)
    diag = jnp.broadcast_to(diag, (8, LANES))
    diag = diag + swap_cores(diag)
    theirs = swap_cores(mine)
    grad_na, grad_nb, stats = call(
        functools.partial(grad_kernel, total_cols=total_cols),
        2,
        [core, (mine, False), (theirs, False), (full_a, True), (full_b, True), (vecs, True)],
        [
            (shape((rows, cols), F32), True),
            (shape((rows, cols), F32), True),
            (shape((groups * 8, cols), F32), True),
        ],
    )
    stats = lax.all_to_all(stats, "sample", split_axis=0, concat_axis=0, tiled=True)
    own = [(full_a[:rows], True), (full_b[:rows], True)]
    grad_a, grad_b, loss = call(
        functools.partial(out_kernel, total_cols=total_cols),
        2,
        [core, (stats, True), (grad_na, True), (grad_nb, True)] + own + [(vecs, True), (diag, False)],
        [
            (shape((rows, cols), BF16), True),
            (shape((rows, cols), BF16), True),
            (shape((1,), F32), False),
        ],
    )
    return (loss.reshape(()), grad_a, grad_b)


def solution(mesh):
    in_specs = (P("sample", "feat"), P("sample", "feat"))
    out_specs = (P(), P("sample", "feat"), P("sample", "feat"))
    return jax.shard_map(body, mesh=mesh, in_specs=in_specs, out_specs=out_specs, check_vma=False)
```

time: 108 us -> 102 us (0.944); the launches traced: 108 us -> 101 us
  Pallas kernels: 0 us -> 14.1 us
  between operations: 7.34 us -> 0.8 us
  other arithmetic: 9.09 us -> 3.04 us
  waiting for transfers between devices: 32.3 us -> 26.9 us
  matrix products: 4.44 us -> 0 us
  local copies, waits for them, and re-layouts: 5.47 us -> 8.96 us
  starting transfers between devices: 21.7 us -> 19.2 us
    pallas_call x0 -> x3, Pallas kernels: none -> 14.1 us  [call(): pl.pallas_call(kernel, grid=(steps,), out_shape=[out for out, _ in outs],...]
    reduce_sum x5 -> x1, other arithmetic: 6.18 us -> 0.11 us  [body(): jnp.sum(summed[:8, total_rows:], axis=1, keepdims=True) * (2.0 / LANES)]
    dot_general x4 -> x0, matrix products: 4.44 us -> none  [the longest x2 3.34 us: gram_rows(): lax.dot_general(own, full, (((1,), (1,)), ((), ())), preferred_element_ty...]
    ppermute x11, waiting for transfers between devices: 23.5 us -> 20.2 us  [send_sample(): return lax.ppermute(block, 'sample', moves)]
    slice x6 -> x4, local copies, waits for them, and re-layouts: 1.78 us -> 4.17 us  [the longest x2 3.34 us: body(): own = [(full_a[:rows], True), (full_b[:rows], True)]]
    all_to_all x1, waiting for transfers between devices: 5.69 us -> 3.55 us  [body(): lax.all_to_all(stats, 'sample', split_axis=0, concat_axis=0, tiled=True)]
    unnamed x17 -> x24, local copies, waits for them, and re-layouts: 2.15 us -> 4.01 us
    ppermute x11, starting transfers between devices: 17.4 us -> 15.6 us  [send_sample(): return lax.ppermute(block, 'sample', moves)]
  transfers between devices with their start and end apart: 14 -> 15, of which waited for: 8 -> 8; matrix products, arithmetic and copies ran while one was open for 3% -> 8% of each run, Pallas kernels for 0% -> 0%
where the time goes in v3:
time: 102 us; the launch traced here: 101 us
  blocking collectives  27.6 us (27%)
  waiting for transfers between devices  26.9 us (26%)
  starting transfers between devices  19.2 us (19%)
  Pallas kernels  14.1 us (14%)
  local copies, waits for them, and re-layouts  8.96 us (9%)
  other arithmetic  3.04 us (3%)
    all_to_all x2, blocking collectives, exchange_chips(): lax.all_to_all(block, 'feat', split_axis=0, concat_axis=0, tiled=True, ax...  27.6 us
    ppermute x11, waiting for transfers between devices, send_sample(): return lax.ppermute(block, 'sample', moves)  20.2 us
    ppermute x11, starting transfers between devices, send_sample(): return lax.ppermute(block, 'sample', moves)  15.6 us
    pallas_call x3, Pallas kernels, call(): pl.pallas_call(kernel, grid=(steps,), out_shape=[out for out, _ in outs],...  14.1 us
    unnamed x24, local copies, waits for them, and re-layouts  4.01 us
    all_to_all x1, waiting for transfers between devices, body(): lax.all_to_all(stats, 'sample', split_axis=0, concat_axis=0, tiled=True)  3.55 us
    all_to_all x1, starting transfers between devices, body(): lax.all_to_all(stats, 'sample', split_axis=0, concat_axis=0, tiled=True)  3.41 us
    slice x2, local copies, waits for them, and re-layouts, body(): own = [(full_a[:rows], True), (full_b[:rows], True)]  3.34 us
  transfers between devices with their start and end apart: 15, of which 8 were waited for; matrix products, arithmetic and copies ran while one was open for 8% of the time, Pallas kernels for 0%

profile of v3, /device:TPU:0, one launch (start us, length us, event | category | flops | bytes accessed | tf_op | source)
XLA Modules:
  0.0 100.6 jit_solution(6802725621458120583)
XLA Ops:
  0.6 2.1 %collective-permute-start = (bf16[128,1024]{1,0:T(8,128)(2,1)}, bf16[128,1024]{1,0:T(8,128)(2,1)S(1)}, u32[]{:S(2)}, u32[]{:S(2)}) collective-permute-start(bf16[128,1024]{1,0:T(8,128)(2,1)} %refs_0_.1), channel_id=1, source_target_pairs={{0,64},{16,80},{32,96},{48,112},{64,0},{80,16},{96,32},{112,48},{1... | collective-permute-start | bytes 786440 | tf_op jit(solution)/shard_map/ppermute | solution.py:25
  2.7 3.0 %collective-permute-start.6 = (bf16[128,1024]{1,0:T(8,128)(2,1)}, bf16[128,1024]{1,0:T(8,128)(2,1)S(1)}, u32[]{:S(2)}, u32[]{:S(2)}) collective-permute-start(bf16[128,1024]{1,0:T(8,128)(2,1)} %refs_6_.1), channel_id=1, source_target_pairs={{0,48},{16,0},{32,16},{48,32},{64,112},{80,64},{96,80},{112,96},{1... | collective-permute-start | bytes 786440 | tf_op jit(solution)/shard_map/ppermute | solution.py:25
  5.7 0.0 collective-permute-start.5
  5.7 1.0 constant_dynamic-update-slice_fusion.1
  6.7 2.5 %collective-permute-done.refs_4_ = bf16[128,1024]{1,0:T(8,128)(2,1)S(1)} collective-permute-done((bf16[128,1024]{1,0:T(8,128)(2,1)}, bf16[128,1024]{1,0:T(8,128)(2,1)S(1)}, u32[]{:S(2)}, u32[]{:S(2)}) %collective-permute-start) | collective-permute-done | bytes 262176 | tf_op jit(solution)/shard_map/ppermute | solution.py:25
  9.3 3.1 %collective-permute-start.2 = (bf16[256,1024]{1,0:T(8,128)(2,1)S(1)}, bf16[256,1024]{1,0:T(8,128)(2,1)S(1)}, u32[]{:S(2)}, u32[]{:S(2)}) collective-permute-start(bf16[256,1024]{1,0:T(8,128)(2,1)S(1)} %constant_dynamic-update-slice_fusion), channel_id=1, source_target_pairs={{0,48},{16,0},{32,16},{48,32},{64,112},{80,64},{96,80},{112,96},{1... | collective-permute-start | bytes 1572872 | tf_op jit(solution)/shard_map/ppermute | solution.py:25
  12.3 0.0 collective-permute-start.1
  12.3 0.0 collective-permute-done.6.refs_8_
  12.3 2.3 %collective-permute-done.5.refs_7_ = bf16[128,1024]{1,0:T(8,128)(2,1)S(1)} collective-permute-done((bf16[128,1024]{1,0:T(8,128)(2,1)}, bf16[128,1024]{1,0:T(8,128)(2,1)S(1)}, u32[]{:S(2)}, u32[]{:S(2)}) %collective-permute-start.5) | collective-permute-done | bytes 262176 | tf_op jit(solution)/shard_map/ppermute | solution.py:25
  14.6 1.1 %pad_maximum_fusion = bf16[384,1024]{1,0:T(8,128)(2,1)S(1)} fusion(bf16[128,1024]{1,0:T(8,128)(2,1)S(1)} %collective-permute-done.6.refs_8_, bf16[128,1024]{1,0:T(8,128)(2,1)S(1)} %collective-permute-done.5.refs_7_, bf16[128,1024]{1,0:T(8,128)(2,1)} %refs_6_.1), kind=kLoop, calls=%fused_computation | loop fusion | flops 2359296 | bytes 1572864 | tf_op jit(solution)/shard_map/concatenate | solution.py:54
  15.7 0.4 collective-permute-start.9
  16.2 0.1 collective-permute-start.7
  16.3 3.3 %collective-permute-start.8 = (bf16[64,1024]{1,0:T(8,128)(2,1)S(1)}, bf16[64,1024]{1,0:T(8,128)(2,1)S(1)}, u32[]{:S(2)}, u32[]{:S(2)}) collective-permute-start(bf16[64,1024]{1,0:T(8,128)(2,1)S(1)} %slice.36), channel_id=1, source_target_pairs={{0,48},{16,0},{32,16},{48,32},{64,112},{80,64},{96,80},{112,96},{1... | collective-permute-start | bytes 393224 | tf_op jit(solution)/shard_map/ppermute | solution.py:25
  19.6 9.5 %collective-permute-done.7 = bf16[64,1024]{1,0:T(8,128)(2,1)S(1)} collective-permute-done((bf16[64,1024]{1,0:T(8,128)(2,1)S(1)}, bf16[64,1024]{1,0:T(8,128)(2,1)S(1)}, u32[]{:S(2)}, u32[]{:S(2)}) %collective-permute-start.7) | collective-permute-done | bytes 131104 | tf_op jit(solution)/shard_map/ppermute | solution.py:25
  29.1 0.7 constant_dynamic-update-slice_fusion.3
  29.8 0.0 collective-permute-done.8
  29.8 0.7 constant_dynamic-update-slice_fusion.2.refs_9_
  30.4 1.5 %collective-permute-start.10 = (bf16[128,1024]{1,0:T(8,128)(2,1)}, bf16[128,1024]{1,0:T(8,128)(2,1)}, u32[]{:S(2)}, u32[]{:S(2)}) collective-permute-start(bf16[128,1024]{1,0:T(8,128)(2,1)} %constant_dynamic-update-slice_fusion.2.refs_9_), channel_id=1, source_target_pairs={{0,64},{16,80},{32,96},{48,112},{64,0},{80,16},{96,32},{112,48},{1... | collective-permute-start | bytes 786440 | tf_op jit(solution)/shard_map/ppermute | solution.py:25
  32.0 0.0 collective-permute-done.2.refs_2_
  32.0 0.1 collective-permute-start.4
  32.1 0.0 collective-permute-done.1.refs_1_
  32.1 0.8 slice.33
  32.9 2.0 %collective-permute-start.3 = (bf16[128,1024]{1,0:T(8,128)(2,1)}, bf16[128,1024]{1,0:T(8,128)(2,1)S(1)}, u32[]{:S(2)}, u32[]{:S(2)}) collective-permute-start(bf16[128,1024]{1,0:T(8,128)(2,1)} %slice.33), channel_id=1, source_target_pairs={{0,16},{16,32},{32,48},{48,0},{64,80},{80,96},{96,112},{112,64},{1... | collective-permute-start | bytes 786440 | tf_op jit(solution)/shard_map/ppermute | solution.py:25
  34.9 4.5 %collective-permute-done.10.refs_11_ = bf16[128,1024]{1,0:T(8,128)(2,1)} collective-permute-done((bf16[128,1024]{1,0:T(8,128)(2,1)}, bf16[128,1024]{1,0:T(8,128)(2,1)}, u32[]{:S(2)}, u32[]{:S(2)}) %collective-permute-start.10) | collective-permute-done | bytes 262176 | tf_op jit(solution)/shard_map/ppermute | solution.py:25
  39.3 1.4 %collective-permute-done.3.refs_3_ = bf16[128,1024]{1,0:T(8,128)(2,1)S(1)} collective-permute-done((bf16[128,1024]{1,0:T(8,128)(2,1)}, bf16[128,1024]{1,0:T(8,128)(2,1)S(1)}, u32[]{:S(2)}, u32[]{:S(2)}) %collective-permute-start.3) | collective-permute-done | bytes 262176 | tf_op jit(solution)/shard_map/ppermute | solution.py:25
  40.7 0.7 copy-done.9
  41.4 0.3 copy-done.7
  41.7 7.7 %shard_map.49 = (bf16[1024,1024]{1,0:T(8,128)(2,1)}, bf16[1024,1024]{1,0:T(8,128)(2,1)}, f32[8,1024]{1,0:T(8,128)}, f32[128,1152]{1,0:T(8,128)}, bf16[128,1152]{1,0:T(8,128)(2,1)}) custom-call(s32[1]{0:T(128)} %bitcast.core, bf16[128,1024]{1,0:T(8,128)(2,1)} %refs_0_.1, bf16[256,1024]{1,0:T(8,128)(2,1)} %copy-done.3, bf16[256,1024]{1,0:T(8,128)(2,1)} %copy-done.2, ...), custom_call_target="tpu_custom_call" | custom-call | tf_op jit(solution)/shard_map/pallas_call | solution.py:75
  49.4 0.1 collective-permute-start.11
  49.4 1.8 %collective-permute-done.11 = bf16[128,1152]{1,0:T(8,128)(2,1)S(1)} collective-permute-done((bf16[128,1152]{1,0:T(8,128)(2,1)}, bf16[128,1152]{1,0:T(8,128)(2,1)S(1)}, u32[]{:S(2)}, u32[]{:S(2)}) %collective-permute-start.11) | collective-permute-done | bytes 294944 | tf_op jit(solution)/shard_map/ppermute | solution.py:29
  51.2 1.1 %add_convert_fusion = bf16[128,1152]{1,0:T(8,128)(2,1)S(1)} fusion(f32[128,1152]{1,0:T(8,128)} %get-tuple-element.14, bf16[128,1152]{1,0:T(8,128)(2,1)S(1)} %collective-permute-done.11), kind=kLoop, calls=%fused_computation.2 | loop fusion | flops 442368 | bytes 1179648 | tf_op jit(solution)/shard_map/convert_element_type | solution.py:247
  52.4 16.7 %all_to_all.28 = bf16[8,16,1152]{2,1,0:T(8,128)(2,1)S(1)} all-to-all(bf16[8,16,1152]{2,1,0:T(8,128)(2,1)S(1)} %bitcast.6), channel_id=1, replica_groups={{0,2,4,6,8,10,12,14},{1,3,5,7,9,11,13,15},{16,18,20,22,24,26,28,30},{17..., dimensions={0} | all-to-all | bytes 589824 | tf_op jit(solution)/shard_map/all_to_all | solution.py:35
  69.2 10.9 %all_to_all.29 = bf16[8,16,1024]{2,1,0:T(8,128)(2,1)S(1)} all-to-all(bf16[8,16,1024]{2,1,0:T(8,128)(2,1)S(1)} %broadcast_in_dim.4), channel_id=1, replica_groups={{0,2,4,6,8,10,12,14},{1,3,5,7,9,11,13,15},{16,18,20,22,24,26,28,30},{17..., dimensions={0} | all-to-all | bytes 524288 | tf_op jit(solution)/shard_map/all_to_all | solution.py:35
  80.0 0.0 collective-permute-start.12
  80.0 0.1 slice_reduce_fusion
  80.1 1.4 %collective-permute-done.12.theirs = bf16[128,1024]{1,0:T(8,128)(2,1)S(1)} collective-permute-done((bf16[128,1024]{1,0:T(8,128)(2,1)S(1)}, bf16[128,1024]{1,0:T(8,128)(2,1)S(1)}, u32[]{:S(2)}, u32[]{:S(2)}) %collective-permute-start.12) | collective-permute-done | bytes 262176 | tf_op jit(solution)/shard_map/ppermute | solution.py:29
  81.5 0.7 copy-done.10
  82.2 4.1 %shard_map.50 = (f32[128,1024]{1,0:T(8,128)}, f32[128,1024]{1,0:T(8,128)}, f32[64,1024]{1,0:T(8,128)}) custom-call(s32[1]{0:T(128)} %bitcast.core, bf16[128,1024]{1,0:T(8,128)(2,1)} %bitcast.8, bf16[128,1024]{1,0:T(8,128)(2,1)} %copy-done.10, bf16[1024,1024]{1,0:T(8,128)(2,1)} %get-tuple-element.16.full_a, bf16[1024,1024]{1,0:T(8,128)(2,1)} %get-tuple-element.17.full_b, ...), custom_call_target="tpu_custom_call" | custom-call | tf_op jit(solution)/shard_map/pallas_call | solution.py:75
  86.3 3.4 %all-to-all-start.2 = ((f32[8,8,1024]{2,1,0:T(8,128)}), f32[8,8,1024]{2,1,0:T(8,128)S(1)}, u32[]{:S(2)}, u32[]{:S(2)}) async-start(f32[8,8,1024]{2,1,0:T(8,128)} %bitcast.10), calls=%async_computation.2 | async-start | bytes 524288 | tf_op jit(solution)/shard_map/all_to_all | solution.py:265
  89.8 0.1 broadcast_in_dim.5
  89.8 0.2 collective-permute-start.13
  90.0 1.7 %slice.30.own_a = bf16[128,1024]{1,0:T(8,128)(2,1)} slice(bf16[1024,1024]{1,0:T(8,128)(2,1)} %get-tuple-element.16.full_a), slice={[0:128], [0:1024]} | slice | bytes 524288 | tf_op jit(solution)/shard_map/slice | solution.py:266
  91.7 1.7 %slice.31.own_b = bf16[128,1024]{1,0:T(8,128)(2,1)} slice(bf16[1024,1024]{1,0:T(8,128)(2,1)} %get-tuple-element.17.full_b), slice={[0:128], [0:1024]} | slice | bytes 524288 | tf_op jit(solution)/shard_map/slice | solution.py:266
  93.3 0.0 collective-permute-done.13
  93.3 0.7 broadcast_add_fusion.diag
  94.0 3.5 %all-to-all-done.2 = f32[8,8,1024]{2,1,0:T(8,128)S(1)} async-done(((f32[8,8,1024]{2,1,0:T(8,128)}), f32[8,8,1024]{2,1,0:T(8,128)S(1)}, u32[]{:S(2)}, u32[]{:S(2)}) %all-to-all-start.2) | async-done | bytes 262176 | tf_op jit(solution)/shard_map/all_to_all | solution.py:265
  97.5 0.7 copy-done.6
  98.2 2.3 %shard_map.51 = (bf16[128,1024]{1,0:T(8,128)(2,1)}, bf16[128,1024]{1,0:T(8,128)(2,1)}, f32[1]{0:T(128)}) custom-call(s32[1]{0:T(128)} %bitcast.core, f32[64,1024]{1,0:T(8,128)} %bitcast.9, f32[128,1024]{1,0:T(8,128)} %get-tuple-element.20.grad_na, f32[128,1024]{1,0:T(8,128)} %get-tuple-element.21.grad_nb, bf16[128,1024]{1,0:T(8,128)(2,1)} %slice.30.own_a, ...), custom_call_target="tpu_custom_call" | custom-call | tf_op jit(solution)/shard_map/pallas_call | solution.py:75
  (28 shorter events, 0.2 us)
Async XLA Ops:
  0.6 8.6 %collective-permute-start = (bf16[128,1024]{1,0:T(8,128)(2,1)}, bf16[128,1024]{1,0:T(8,128)(2,1)S(1)}, u32[]{:S(2)}, u32[]{:S(2)}) collective-permute-start(bf16[128,1024]{1,0:T(8,128)(2,1)} %refs_0_.1), channel_id=1, source_target_pairs={{0,64},{16,80},{32,96},{48,112},{64,0},{80,16},{96,32},{112,48},{1... | collective-permute-start | bytes 786440 | tf_op jit(solution)/shard_map/ppermute | solution.py:25
  2.7 9.6 %collective-permute-start.6 = (bf16[128,1024]{1,0:T(8,128)(2,1)}, bf16[128,1024]{1,0:T(8,128)(2,1)S(1)}, u32[]{:S(2)}, u32[]{:S(2)}) collective-permute-start(bf16[128,1024]{1,0:T(8,128)(2,1)} %refs_6_.1), channel_id=1, source_target_pairs={{0,48},{16,0},{32,16},{48,32},{64,112},{80,64},{96,80},{112,96},{1... | collective-permute-start | bytes 786440 | tf_op jit(solution)/shard_map/ppermute | solution.py:25
  5.7 8.9 %collective-permute-start.5 = (bf16[128,1024]{1,0:T(8,128)(2,1)}, bf16[128,1024]{1,0:T(8,128)(2,1)S(1)}, u32[]{:S(2)}, u32[]{:S(2)}) collective-permute-start(bf16[128,1024]{1,0:T(8,128)(2,1)} %refs_6_.1), channel_id=1, source_target_pairs={{0,16},{16,32},{32,48},{48,0},{64,80},{80,96},{96,112},{112,64},{1... | collective-permute-start | bytes 786440 | tf_op jit(solution)/shard_map/ppermute | solution.py:25
  9.2 21.2 %copy-start.4 = (bf16[128,1024]{1,0:T(8,128)(2,1)}, bf16[128,1024]{1,0:T(8,128)(2,1)S(1)}, u32[]{:S(2)}) copy-start(bf16[128,1024]{1,0:T(8,128)(2,1)S(1)} %collective-permute-done.refs_4_) | copy-start | bytes 786436
  9.3 22.7 %collective-permute-start.2 = (bf16[256,1024]{1,0:T(8,128)(2,1)S(1)}, bf16[256,1024]{1,0:T(8,128)(2,1)S(1)}, u32[]{:S(2)}, u32[]{:S(2)}) collective-permute-start(bf16[256,1024]{1,0:T(8,128)(2,1)S(1)} %constant_dynamic-update-slice_fusion), channel_id=1, source_target_pairs={{0,48},{16,0},{32,16},{48,32},{64,112},{80,64},{96,80},{112,96},{1... | collective-permute-start | bytes 1572872 | tf_op jit(solution)/shard_map/ppermute | solution.py:25
  12.3 19.7 %collective-permute-start.1 = (bf16[256,1024]{1,0:T(8,128)(2,1)S(1)}, bf16[256,1024]{1,0:T(8,128)(2,1)S(1)}, u32[]{:S(2)}, u32[]{:S(2)}) collective-permute-start(bf16[256,1024]{1,0:T(8,128)(2,1)S(1)} %constant_dynamic-update-slice_fusion), channel_id=1, source_target_pairs={{0,16},{16,32},{32,48},{48,0},{64,80},{80,96},{96,112},{112,64},{1... | collective-permute-start | bytes 1572872 | tf_op jit(solution)/shard_map/ppermute | solution.py:25
  12.3 19.6 %copy-start = (bf16[128,1024]{1,0:T(8,128)(2,1)}, bf16[128,1024]{1,0:T(8,128)(2,1)S(1)}, u32[]{:S(2)}) copy-start(bf16[128,1024]{1,0:T(8,128)(2,1)S(1)} %collective-permute-done.6.refs_8_) | copy-start | bytes 786436
  14.6 17.4 %copy-start.1 = (bf16[128,1024]{1,0:T(8,128)(2,1)}, bf16[128,1024]{1,0:T(8,128)(2,1)S(1)}, u32[]{:S(2)}) copy-start(bf16[128,1024]{1,0:T(8,128)(2,1)S(1)} %collective-permute-done.5.refs_7_) | copy-start | bytes 786436
  15.7 25.0 %collective-permute-start.9 = (bf16[384,1024]{1,0:T(8,128)(2,1)S(1)}, bf16[384,1024]{1,0:T(8,128)(2,1)S(1)}, u32[]{:S(2)}, u32[]{:S(2)}) collective-permute-start(bf16[384,1024]{1,0:T(8,128)(2,1)S(1)} %pad_maximum_fusion), channel_id=1, source_target_pairs={{0,64},{16,80},{32,96},{48,112},{64,0},{80,16},{96,32},{112,48},{1... | collective-permute-start | bytes 2359304 | tf_op jit(solution)/shard_map/ppermute | solution.py:25
  16.2 12.9 %collective-permute-start.7 = (bf16[64,1024]{1,0:T(8,128)(2,1)S(1)}, bf16[64,1024]{1,0:T(8,128)(2,1)S(1)}, u32[]{:S(2)}, u32[]{:S(2)}) collective-permute-start(bf16[64,1024]{1,0:T(8,128)(2,1)S(1)} %slice.35), channel_id=1, source_target_pairs={{0,16},{16,32},{32,48},{48,0},{64,80},{80,96},{96,112},{112,64},{1... | collective-permute-start | bytes 393224 | tf_op jit(solution)/shard_map/ppermute | solution.py:25
  16.3 13.5 %collective-permute-start.8 = (bf16[64,1024]{1,0:T(8,128)(2,1)S(1)}, bf16[64,1024]{1,0:T(8,128)(2,1)S(1)}, u32[]{:S(2)}, u32[]{:S(2)}) collective-permute-start(bf16[64,1024]{1,0:T(8,128)(2,1)S(1)} %slice.36), channel_id=1, source_target_pairs={{0,48},{16,0},{32,16},{48,32},{64,112},{80,64},{96,80},{112,96},{1... | collective-permute-start | bytes 393224 | tf_op jit(solution)/shard_map/ppermute | solution.py:25
  30.4 8.9 %collective-permute-start.10 = (bf16[128,1024]{1,0:T(8,128)(2,1)}, bf16[128,1024]{1,0:T(8,128)(2,1)}, u32[]{:S(2)}, u32[]{:S(2)}) collective-permute-start(bf16[128,1024]{1,0:T(8,128)(2,1)} %constant_dynamic-update-slice_fusion.2.refs_9_), channel_id=1, source_target_pairs={{0,64},{16,80},{32,96},{48,112},{64,0},{80,16},{96,32},{112,48},{1... | collective-permute-start | bytes 786440 | tf_op jit(solution)/shard_map/ppermute | solution.py:25
  32.0 8.8 %copy-start.2 = (bf16[256,1024]{1,0:T(8,128)(2,1)}, bf16[256,1024]{1,0:T(8,128)(2,1)S(1)}, u32[]{:S(2)}) copy-start(bf16[256,1024]{1,0:T(8,128)(2,1)S(1)} %collective-permute-done.2.refs_2_) | copy-start | bytes 1572868
  32.0 7.3 %collective-permute-start.4 = (bf16[128,1024]{1,0:T(8,128)(2,1)S(1)}, bf16[128,1024]{1,0:T(8,128)(2,1)S(1)}, u32[]{:S(2)}, u32[]{:S(2)}) collective-permute-start(bf16[128,1024]{1,0:T(8,128)(2,1)S(1)} %slice.34), channel_id=1, source_target_pairs={{0,48},{16,0},{32,16},{48,32},{64,112},{80,64},{96,80},{112,96},{1... | collective-permute-start | bytes 786440 | tf_op jit(solution)/shard_map/ppermute | solution.py:25
  32.1 8.6 %copy-start.3 = (bf16[256,1024]{1,0:T(8,128)(2,1)}, bf16[256,1024]{1,0:T(8,128)(2,1)S(1)}, u32[]{:S(2)}) copy-start(bf16[256,1024]{1,0:T(8,128)(2,1)S(1)} %collective-permute-done.1.refs_1_) | copy-start | bytes 1572868
  32.9 7.8 %collective-permute-start.3 = (bf16[128,1024]{1,0:T(8,128)(2,1)}, bf16[128,1024]{1,0:T(8,128)(2,1)S(1)}, u32[]{:S(2)}, u32[]{:S(2)}) collective-permute-start(bf16[128,1024]{1,0:T(8,128)(2,1)} %slice.33), channel_id=1, source_target_pairs={{0,16},{16,32},{32,48},{48,0},{64,80},{80,96},{96,112},{112,64},{1... | collective-permute-start | bytes 786440 | tf_op jit(solution)/shard_map/ppermute | solution.py:25
  39.3 1.4 %copy-start.8 = (bf16[128,1024]{1,0:T(8,128)(2,1)}, bf16[128,1024]{1,0:T(8,128)(2,1)S(1)}, u32[]{:S(2)}) copy-start(bf16[128,1024]{1,0:T(8,128)(2,1)S(1)} %collective-permute-done.4.refs_5_) | copy-start | bytes 786436
  40.7 0.7 copy-start.9
  40.7 1.0 copy-start.7
  49.4 1.9 %collective-permute-start.11 = (bf16[128,1152]{1,0:T(8,128)(2,1)}, bf16[128,1152]{1,0:T(8,128)(2,1)S(1)}, u32[]{:S(2)}, u32[]{:S(2)}) collective-permute-start(bf16[128,1152]{1,0:T(8,128)(2,1)} %get-tuple-element.15), channel_id=1, source_target_pairs={{0,1},{1,0},{2,3},{3,2},{4,5},{5,4},{6,7},{7,6},{8,9},{9,8},{10,11... | collective-permute-start | bytes 884744 | tf_op jit(solution)/shard_map/ppermute | solution.py:29
  80.0 1.5 %copy-start.5 = (bf16[8,16,1024]{2,1,0:T(8,128)(2,1)}, bf16[8,16,1024]{2,1,0:T(8,128)(2,1)S(1)}, u32[]{:S(2)}) copy-start(bf16[8,16,1024]{2,1,0:T(8,128)(2,1)S(1)} %all_to_all.29) | copy-start | bytes 786436
  80.0 1.5 %collective-permute-start.12 = (bf16[128,1024]{1,0:T(8,128)(2,1)S(1)}, bf16[128,1024]{1,0:T(8,128)(2,1)S(1)}, u32[]{:S(2)}, u32[]{:S(2)}) collective-permute-start(bf16[128,1024]{1,0:T(8,128)(2,1)S(1)} %bitcast.7), channel_id=1, source_target_pairs={{0,1},{1,0},{2,3},{3,2},{4,5},{5,4},{6,7},{7,6},{8,9},{9,8},{10,11... | collective-permute-start | bytes 786440 | tf_op jit(solution)/shard_map/ppermute | solution.py:29
  81.5 0.7 copy-start.10
  86.3 11.2 %all-to-all-start.2 = ((f32[8,8,1024]{2,1,0:T(8,128)}), f32[8,8,1024]{2,1,0:T(8,128)S(1)}, u32[]{:S(2)}, u32[]{:S(2)}) async-start(f32[8,8,1024]{2,1,0:T(8,128)} %bitcast.10), calls=%async_computation.2 | async-start | bytes 524288 | tf_op jit(solution)/shard_map/all_to_all | solution.py:265
  89.8 3.5 %collective-permute-start.13 = (f32[8,128]{1,0:T(8,128)S(1)}, f32[8,128]{1,0:T(8,128)S(1)}, u32[]{:S(2)}, u32[]{:S(2)}) collective-permute-start(f32[8,128]{1,0:T(8,128)S(1)} %broadcast_in_dim.5), channel_id=1, source_target_pairs={{0,1},{1,0},{2,3},{3,2},{4,5},{5,4},{6,7},{7,6},{8,9},{9,8},{10,11... | collective-permute-start | bytes 12296 | tf_op jit(solution)/shard_map/ppermute | solution.py:29
  97.5 0.7 copy-start.6

commit v4 on v3

v4 whole, which is shorter than its diff:
```python
import functools
import jax
import jax.numpy as jnp
from jax import lax
from jax.experimental import pallas as pl
from jax.experimental.pallas import tpu as pltpu
from jax.sharding import PartitionSpec as P

EPSILON = 1e-05
OFF_WEIGHT = 0.0051
RING = 4
CORES = 2
F32 = jnp.float32
BF16 = jnp.bfloat16
LANES = 128


def send_sample(block, turn, step):
    pairs = lax.axis_size("sample") // RING
    moves = [
        (z * RING + y, (z + turn) % pairs * RING + (y + step) % RING)
        for z in range(pairs)
        for y in range(RING)
    ]
    return lax.ppermute(block, "sample", moves)


def swap_cores(block):
    return lax.ppermute(block, "feat", [(i, i ^ 1) for i in range(lax.axis_size("feat"))])


def exchange_chips(block):
    members = lax.axis_size("feat") // CORES
    groups = [[i * CORES + core for i in range(members)] for core in range(CORES)]
    return lax.all_to_all(
        block, "feat", split_axis=0, concat_axis=0, tiled=True, axis_index_groups=groups
    )


def repeat_block(block, members):
    copies = jnp.broadcast_to(block[None], (members,) + block.shape)
    return copies.reshape((members * block.shape[0],) + block.shape[1:])


def after(block, *others):
    return lax.optimization_barrier((block,) + others)[0]


def call(kernel, steps, args, outs, scratch=()):
    def spec(shape, cut, rows=None):
        rows, cols = rows or shape[0], shape[1]
        if cut:
            return pl.BlockSpec((rows, cols // steps), lambda i: (0, i))
        return pl.BlockSpec((rows, cols), lambda i: (0, 0))

    def out_spec(out, cut):
        if out.shape == (1,):
            return pl.BlockSpec(memory_space=pltpu.SMEM)
        return spec(out.shape, cut)

    return pl.pallas_call(
        kernel,
        grid=(steps,),
        out_shape=[out for out, _ in outs],
        in_specs=[pl.BlockSpec(memory_space=pltpu.SMEM)] + [
            spec(arg[0].shape, *arg[1:]) for arg in args[1:]
        ],
        out_specs=[out_spec(out, cut) for out, cut in outs],
        scratch_shapes=list(scratch),

    )(args[0], *[arg[0] for arg in args[1:]])


def on_own(shape):
    row_ids = lax.broadcasted_iota(jnp.int32, shape, 0)
    return row_ids == lax.broadcasted_iota(jnp.int32, shape, 1)


def split_scalar(value, rows):
    wide = jnp.broadcast_to(value, (rows, LANES))
    high = wide.astype(BF16).astype(F32)
    lane = lax.broadcasted_iota(jnp.int32, wide.shape, 1)
    return jnp.where(lane < LANES // 2, high, (wide - high).astype(BF16).astype(F32))


def normalize(pieces, full, part):
    rows = part.shape[0]
    inv_rows = 1.0 / full.shape[0]
    floats = jnp.concatenate(pieces).astype(F32)
    mean = jnp.sum(floats, axis=0, keepdims=True) * inv_rows
    square = jnp.sum(floats * floats, axis=0, keepdims=True) * inv_rows
    scale = lax.rsqrt(square - mean * mean + EPSILON)
    norm = ((floats - mean) * scale).astype(BF16)
    full[...] = norm
    part[...] += lax.dot_general(
        norm[:rows], norm, (((1,), (1,)), ((), ())), preferred_element_type=F32
    )
    return norm, scale


def share_rows(core, part, cols, keep, send):
    rows, total_rows = part.shape
    half = rows // CORES
    gram = part[...] - jnp.where(on_own(part.shape), 1.0 * cols, 0.0)

    @pl.when(core[0] == 0)
    def _():
        keep[:, :total_rows] = gram[:half]
        send[:, :total_rows] = gram[half:].astype(BF16)

    @pl.when(core[0] != 0)
    def _():
        keep[:, :total_rows] = gram[half:]
        send[:, :total_rows] = gram[:half].astype(BF16)


def gram_a_kernel(core, *refs):
    full, scale_ref, keep, send, part = refs[8:]
    step = pl.program_id(0)

    @pl.when(step == 0)
    def _():
        part[...] = jnp.zeros_like(part)

    _, scale = normalize([ref[...] for ref in refs[:8]], full, part)
    scale_ref[...] = jnp.broadcast_to(scale, scale_ref.shape)

    @pl.when(step == pl.num_programs(0) - 1)
    def _():
        share_rows(core, part, full.shape[1] * pl.num_programs(0), keep, send)


def gram_b_kernel(core, *refs):
    b, b_back, b_on, b_far, b_over, b_over_far, full_a = refs[:7]
    full, vecs, keep, send, part, loss = refs[7:]
    step = pl.program_id(0)
    rows, cols = b.shape
    half, total_rows = keep.shape[0], full.shape[0]

    @pl.when(step == 0)
    def _():
        part[...] = jnp.zeros_like(part)
        loss[...] = jnp.zeros_like(loss)

    pieces = [b[...], b_back[:rows, :], b_on[:rows, :], b_far[...]]
    pieces += [b_over[...], b_back[rows:, :], b_on[rows:, :], b_over_far[...]]
    norm, scale = normalize(pieces, full, part)
    diag = jnp.sum(full_a[...].astype(F32) * norm.astype(F32), axis=0, keepdims=True)
    diag = diag * (1.0 / total_rows)
    loss[...] += (1.0 - diag) * (1.0 - diag) - OFF_WEIGHT * diag * diag
    slope = (diag - 1.0) - OFF_WEIGHT * diag
    vecs[...] = jnp.concatenate([scale, slope, jnp.zeros((6, cols), F32)])

    @pl.when(step == pl.num_programs(0) - 1)
    def _():
        share_rows(core, part, cols * pl.num_programs(0), keep, send)
        keep[:, total_rows:] = split_scalar(jnp.sum(loss[...], axis=1, keepdims=True), half)
        send[:, total_rows:] = jnp.zeros((half, LANES), BF16)


def join_rows(core, mine, theirs):
    first = core[0] == 0
    low = jnp.where(first, mine[...], theirs[...])
    return jnp.concatenate([low, jnp.where(first, theirs[...], mine[...])])


def grad_kernel(core, mine, theirs, full, other, vecs, *refs, total_cols, squared):
    grad, stats = refs[-2:]
    total_rows = full.shape[0]
    cols = grad.shape[1]
    factor = OFF_WEIGHT / total_rows
    gram = join_rows(core, mine, theirs)
    rows = gram.shape[0]
    norm = full[:rows, :].astype(F32)
    wide = jnp.dot(gram, full[...], preferred_element_type=F32)
    wide = factor * wide + factor * total_cols * norm + vecs[1:2, :] * other[...].astype(F32)
    grad[...] = wide
    sums = jnp.concatenate(
        [
            jnp.sum(wide, axis=0, keepdims=True),
            jnp.sum(wide * norm, axis=0, keepdims=True),
            jnp.zeros((6, cols), F32),
        ]
    )
    copies = stats.shape[0] // 8
    for member in range(copies):
        stats[pl.ds(member * 8, 8), :] = sums

    if squared:

        @pl.when(pl.program_id(0) == 0)
        def _():
            back = jnp.where(on_own(gram.shape), 1.0 * total_cols, 0.0)
            second = join_rows(core, refs[0], refs[1])
            square = (gram.astype(F32) + back) * (second.astype(F32) + back)
            square = jnp.sum(jnp.sum(square, axis=0, keepdims=True), axis=1, keepdims=True)
            for member in range(copies):
                stats[pl.ds(member * 8 + 2, 1), :] = jnp.broadcast_to(square, (1, cols))


def out_kernel(core, stats, grad, own, scale, *refs, total_cols, with_loss):
    del core
    members = stats.shape[0] // 8
    inv_rows = 1.0 / (own.shape[0] * members)
    sums = stats[0:8, :]
    for member in range(1, members):
        sums += stats[pl.ds(member * 8, 8), :]
    means = sums * inv_rows
    wide = grad[...] - means[0:1] - own[...].astype(F32) * means[1:2]
    refs[-2 if with_loss else -1][...] = (scale[0:1, :] * wide).astype(BF16)

    if with_loss:
        diag, loss = refs[0], refs[-1]

        @pl.when(pl.program_id(0) == 0)
        def _():
            square = jnp.max(means[2:3, 0:LANES]) * inv_rows
            loss[0] = (jnp.max(diag[0:1, :]) + OFF_WEIGHT * square) / total_cols


def add_cores(keep, send):
    return (keep + swap_cores(send).astype(F32)).astype(BF16)


def add_chips(total):
    moved = exchange_chips(total)
    members = lax.axis_size("feat") // CORES
    return jnp.sum(moved.reshape(members, -1, moved.shape[1]).astype(F32), axis=0)


def share_sums(summed):
    members = lax.axis_size("feat") // CORES
    mine = exchange_chips(repeat_block(summed.astype(BF16), members))
    return mine, swap_cores(mine)


def body(view_a, view_b):
    rows, cols = view_a.shape
    groups = lax.axis_size("sample")
    blocks = lax.axis_size("feat")
    half = rows // CORES
    total_rows = rows * groups
    total_cols = cols * blocks
    core = (lax.axis_index("feat") & (CORES - 1)).reshape(1)
    shape = jax.ShapeDtypeStruct
    wide = total_rows + LANES

    a_over = send_sample(view_a, 1, 0)
    a_back = send_sample(view_a, 0, 1)
    a_on = send_sample(view_a, 0, -1)
    b_over = send_sample(after(view_b, a_back, a_on, a_over), 1, 0)
    a_far = send_sample(a_back, 0, 1)
    a_pass = after(a_over, a_back, a_on)
    a_over_back = send_sample(a_pass, 0, 1)
    a_over_on = send_sample(a_pass, 0, -1)
    a_over_far = send_sample(a_over_on, 0, -1)
    b_pair = after(jnp.concatenate([view_b, b_over]), a_over_back, a_over_on)
    b_back = send_sample(b_pair, 0, 1)
    b_on = send_sample(b_pair, 0, -1)
    parts_a = [view_a, a_back, a_on, a_far, a_over, a_over_back, a_over_on, a_over_far]
    full_a, scale_a, keep_a, send_a = call(
        gram_a_kernel,
        4,
        [core] + [(part, True) for part in parts_a],
        [
            (shape((total_rows, cols), BF16), True),
            (shape((8, cols), F32), True),
            (shape((half, total_rows), F32), False),
            (shape((half, total_rows), BF16), False),
        ],
        [pltpu.VMEM((rows, total_rows), F32)],
    )
    total_a = add_cores(keep_a, send_a)
    b_far = send_sample(after(b_back[:rows], total_a), 0, 1)
    b_over_far = send_sample(after(b_on[rows:], total_a), 0, -1)
    summed_a = add_chips(after(total_a, b_back, b_on))
    parts_b = [view_b, b_back, b_on, b_far, after(b_over, summed_a), b_over_far]
    a_mine, a_theirs = share_sums(summed_a)
    full_b, vecs, keep_b, send_b = call(
        gram_b_kernel,
        4,
        [core] + [(part, True) for part in parts_b] + [(full_a, True)],
        [
            (shape((total_rows, cols), BF16), True),
            (shape((8, cols), F32), True),
            (shape((half, wide), F32), False),
            (shape((half, wide), BF16), False),
        ],
        [pltpu.VMEM((rows, total_rows), F32), pltpu.VMEM((1, cols // 4), F32)],
    )
    summed_b = add_chips(add_cores(keep_b, send_b))
    b_mine, b_theirs = share_sums(summed_b[:, :total_rows])
    diag = jnp.sum(summed_b[:, total_rows:], axis=1, keepdims=True) * (2.0 / LANES)
    diag = jnp.broadcast_to(diag, (diag.shape[0], LANES))
    diag = diag + swap_cores(diag)

    def gradient(mine, theirs, full, other, extra):
        grad, stats = call(
            functools.partial(grad_kernel, total_cols=total_cols, squared=bool(extra)),
            2,
            [core, (mine, False), (theirs, False), (full, True), (other, True, rows), (vecs, True)]
            + extra,
            [(shape((rows, cols), F32), True), (shape((groups * 8, cols), F32), True)],
        )
        stats = lax.all_to_all(stats, "sample", split_axis=0, concat_axis=0, tiled=True)
        return grad, stats

    def output(stats, grad, full, scale, extra):
        return call(
            functools.partial(out_kernel, total_cols=total_cols, with_loss=bool(extra)),
            2,
            [core, (stats, True), (grad, True), (full, True, rows), (scale, True)] + extra,
            [(shape((rows, cols), BF16), True)] + [(shape((1,), F32), False)] * len(extra),
        )

    raw_b, stats_b = gradient(a_mine, a_theirs, full_b, full_a, [])
    raw_a, stats_a = gradient(
        b_mine, b_theirs, full_a, full_b, [(a_mine, False), (a_theirs, False)]
    )
    (grad_b,) = output(stats_b, raw_b, full_b, vecs, [])
    grad_a, loss = output(stats_a, raw_a, full_a, scale_a, [(diag, False)])
    return (loss.reshape(()), grad_a, grad_b)


def solution(mesh):
    in_specs = (P("sample", "feat"), P("sample", "feat"))
    out_specs = (P(), P("sample", "feat"), P("sample", "feat"))
    return jax.shard_map(body, mesh=mesh, in_specs=in_specs, out_specs=out_specs, check_vma=False)
```

time: 102 us -> 125 us (1.23)
  waiting for transfers between devices: 26.9 us -> 43.9 us
  starting transfers between devices: 19.2 us -> 33.6 us
  blocking collectives: 27.6 us -> 15 us
  Pallas kernels: 14.1 us -> 21 us
  local copies, waits for them, and re-layouts: 8.96 us -> 4.86 us
  other arithmetic: 3.04 us -> 4.53 us
    all_to_all x1 -> x5, waiting for transfers between devices: 3.55 us -> 24.2 us  [the longest x3 18.5 us: exchange_chips(): lax.all_to_all(block, 'feat', split_axis=0, concat_axis=0, tiled=True, ax...]
    all_to_all x1 -> x5, starting transfers between devices: 3.41 us -> 17.1 us  [the longest x3 10.1 us: exchange_chips(): lax.all_to_all(block, 'feat', split_axis=0, concat_axis=0, tiled=True, ax...]
    all_to_all x2 -> x1, blocking collectives: 27.6 us -> 15 us  [exchange_chips(): lax.all_to_all(block, 'feat', split_axis=0, concat_axis=0, tiled=True, ax...]
    pallas_call x3 -> x6, Pallas kernels: 14.1 us -> 21 us  [call(): pl.pallas_call(kernel, grid=(steps,), out_shape=[out for out, _ in outs],...]
    ppermute x11 -> x12, waiting for transfers between devices: 20.2 us -> 15.8 us  [send_sample(): return lax.ppermute(block, 'sample', moves)]
    slice x7 -> x3, local copies, waits for them, and re-layouts: 4.19 us -> 0.04 us  [the longest x1 0.02 us: body(): b_over_far = send_sample(after(b_on[rows:], total_a), 0, -1)]
    all_to_all x0 -> x1, other arithmetic: none -> 1.65 us  [exchange_chips(): lax.all_to_all(block, 'feat', split_axis=0, concat_axis=0, tiled=True, ax...]
    broadcast_in_dim x1 -> x2, local copies, waits for them, and re-layouts: 0.02 us -> 1.33 us  [repeat_block(): copies = jnp.broadcast_to(block[None], (members,) + block.shape)]
  transfers between devices with their start and end apart: 15 -> 22, of which waited for: 8 -> 13; matrix products, arithmetic and copies ran while one was open for 8% -> 5% of each run, Pallas kernels for 0% -> 11%
where the time goes in v4:
time: 125 us; the launch traced here: 124 us
  waiting for transfers between devices  43.9 us (35%)
  starting transfers between devices  33.6 us (27%)
  Pallas kernels  21 us (17%)
  blocking collectives  15 us (12%)
  local copies, waits for them, and re-layouts  4.86 us (4%)
  other arithmetic  4.53 us (4%)
    pallas_call x6, Pallas kernels, call(): pl.pallas_call(kernel, grid=(steps,), out_shape=[out for out, _ in outs],...  21 us
    all_to_all x3, waiting for transfers between devices, exchange_chips(): lax.all_to_all(block, 'feat', split_axis=0, concat_axis=0, tiled=True, ax...  18.5 us
    ppermute x12, starting transfers between devices, send_sample(): return lax.ppermute(block, 'sample', moves)  16.1 us
    ppermute x12, waiting for transfers between devices, send_sample(): return lax.ppermute(block, 'sample', moves)  15.8 us
    all_to_all x1, blocking collectives, exchange_chips(): lax.all_to_all(block, 'feat', split_axis=0, concat_axis=0, tiled=True, ax...  15 us
    all_to_all x3, starting transfers between devices, exchange_chips(): lax.all_to_all(block, 'feat', split_axis=0, concat_axis=0, tiled=True, ax...  10.1 us
    all_to_all x2, starting transfers between devices, gradient(): lax.all_to_all(stats, 'sample', split_axis=0, concat_axis=0, tiled=True)  7 us
    all_to_all x2, waiting for transfers between devices, gradient(): lax.all_to_all(stats, 'sample', split_axis=0, concat_axis=0, tiled=True)  5.68 us
  transfers between devices with their start and end apart: 22, of which 13 were waited for; matrix products, arithmetic and copies ran while one was open for 5% of the time, Pallas kernels for 11%

profile of v4, /device:TPU:0, one launch (start us, length us, event | category | flops | bytes accessed | tf_op | source)
XLA Modules:
  0.0 123.8 jit_solution(13461360869200576024)
XLA Ops:
  0.6 1.7 %collective-permute-start = (bf16[128,1024]{1,0:T(8,128)(2,1)}, bf16[128,1024]{1,0:T(8,128)(2,1)S(1)}, u32[]{:S(2)}, u32[]{:S(2)}) collective-permute-start(bf16[128,1024]{1,0:T(8,128)(2,1)} %refs_0_.2), channel_id=1, source_target_pairs={{0,16},{16,32},{32,48},{48,0},{64,80},{80,96},{96,112},{112,64},{1... | collective-permute-start | bytes 786440 | tf_op jit(solution)/shard_map/ppermute | solution.py:25
  2.4 1.6 %collective-permute-start.1 = (bf16[128,1024]{1,0:T(8,128)(2,1)}, bf16[128,1024]{1,0:T(8,128)(2,1)S(1)}, u32[]{:S(2)}, u32[]{:S(2)}) collective-permute-start(bf16[128,1024]{1,0:T(8,128)(2,1)} %refs_0_.2), channel_id=1, source_target_pairs={{0,48},{16,0},{32,16},{48,32},{64,112},{80,64},{96,80},{112,96},{1... | collective-permute-start | bytes 786440 | tf_op jit(solution)/shard_map/ppermute | solution.py:25
  3.9 2.0 %collective-permute-start.2 = (bf16[128,1024]{1,0:T(8,128)(2,1)}, bf16[128,1024]{1,0:T(8,128)(2,1)S(1)}, u32[]{:S(2)}, u32[]{:S(2)}) collective-permute-start(bf16[128,1024]{1,0:T(8,128)(2,1)} %refs_0_.2), channel_id=1, source_target_pairs={{0,64},{16,80},{32,96},{48,112},{64,0},{80,16},{96,32},{112,48},{1... | collective-permute-start | bytes 786440 | tf_op jit(solution)/shard_map/ppermute | solution.py:25
  5.9 4.4 %collective-permute-done.refs_1_ = bf16[128,1024]{1,0:T(8,128)(2,1)S(1)} collective-permute-done((bf16[128,1024]{1,0:T(8,128)(2,1)}, bf16[128,1024]{1,0:T(8,128)(2,1)S(1)}, u32[]{:S(2)}, u32[]{:S(2)}) %collective-permute-start) | collective-permute-done | bytes 262176 | tf_op jit(solution)/shard_map/ppermute | solution.py:25
  10.3 1.7 %collective-permute-done.2.refs_4_ = bf16[128,1024]{1,0:T(8,128)(2,1)S(1)} collective-permute-done((bf16[128,1024]{1,0:T(8,128)(2,1)}, bf16[128,1024]{1,0:T(8,128)(2,1)S(1)}, u32[]{:S(2)}, u32[]{:S(2)}) %collective-permute-start.2) | collective-permute-done | bytes 262176 | tf_op jit(solution)/shard_map/ppermute | solution.py:25
  12.1 1.7 %collective-permute-start.5 = (bf16[128,1024]{1,0:T(8,128)(2,1)S(1)}, bf16[128,1024]{1,0:T(8,128)(2,1)S(1)}, u32[]{:S(2)}, u32[]{:S(2)}) collective-permute-start(bf16[128,1024]{1,0:T(8,128)(2,1)S(1)} %collective-permute-done.2.refs_4_), channel_id=1, source_target_pairs={{0,48},{16,0},{32,16},{48,32},{64,112},{80,64},{96,80},{112,96},{1... | collective-permute-start | bytes 786440 | tf_op jit(solution)/shard_map/ppermute | solution.py:25
  13.7 1.7 %collective-permute-start.3 = (bf16[128,1024]{1,0:T(8,128)(2,1)}, bf16[128,1024]{1,0:T(8,128)(2,1)S(1)}, u32[]{:S(2)}, u32[]{:S(2)}) collective-permute-start(bf16[128,1024]{1,0:T(8,128)(2,1)} %refs_0_.3), channel_id=1, source_target_pairs={{0,64},{16,80},{32,96},{48,112},{64,0},{80,16},{96,32},{112,48},{1... | collective-permute-start | bytes 786440 | tf_op jit(solution)/shard_map/ppermute | solution.py:25
  15.4 0.4 collective-permute-start.4
  15.8 0.2 collective-permute-start.8
  16.0 3.0 %collective-permute-done.5.refs_6_ = bf16[128,1024]{1,0:T(8,128)(2,1)S(1)} collective-permute-done((bf16[128,1024]{1,0:T(8,128)(2,1)S(1)}, bf16[128,1024]{1,0:T(8,128)(2,1)S(1)}, u32[]{:S(2)}, u32[]{:S(2)}) %collective-permute-start.5) | collective-permute-done | bytes 262176 | tf_op jit(solution)/shard_map/ppermute | solution.py:25
  19.1 2.7 %collective-permute-start.9 = (bf16[128,1024]{1,0:T(8,128)(2,1)S(1)}, bf16[128,1024]{1,0:T(8,128)(2,1)}, u32[]{:S(2)}, u32[]{:S(2)}) collective-permute-start(bf16[128,1024]{1,0:T(8,128)(2,1)S(1)} %collective-permute-done.5.refs_6_), channel_id=1, source_target_pairs={{0,48},{16,0},{32,16},{48,32},{64,112},{80,64},{96,80},{112,96},{1... | collective-permute-start | bytes 786440 | tf_op jit(solution)/shard_map/ppermute | solution.py:25
  21.8 1.1 pad_maximum_fusion
  22.8 3.1 %collective-permute-done.4.refs_5_ = bf16[128,1024]{1,0:T(8,128)(2,1)S(1)} collective-permute-done((bf16[128,1024]{1,0:T(8,128)(2,1)S(1)}, bf16[128,1024]{1,0:T(8,128)(2,1)S(1)}, u32[]{:S(2)}, u32[]{:S(2)}) %collective-permute-start.4) | collective-permute-done | bytes 262176 | tf_op jit(solution)/shard_map/ppermute | solution.py:25
  25.9 2.0 %collective-permute-start.6 = (bf16[256,1024]{1,0:T(8,128)(2,1)S(1)}, bf16[256,1024]{1,0:T(8,128)(2,1)S(1)}, u32[]{:S(2)}, u32[]{:S(2)}) collective-permute-start(bf16[256,1024]{1,0:T(8,128)(2,1)S(1)} %pad_maximum_fusion), channel_id=1, source_target_pairs={{0,16},{16,32},{32,48},{48,0},{64,80},{80,96},{96,112},{112,64},{1... | collective-permute-start | bytes 1572872 | tf_op jit(solution)/shard_map/ppermute | solution.py:25
  27.9 3.6 %collective-permute-done.8.refs_3_ = bf16[128,1024]{1,0:T(8,128)(2,1)S(1)} collective-permute-done((bf16[128,1024]{1,0:T(8,128)(2,1)S(1)}, bf16[128,1024]{1,0:T(8,128)(2,1)S(1)}, u32[]{:S(2)}, u32[]{:S(2)}) %collective-permute-start.8) | collective-permute-done | bytes 262176 | tf_op jit(solution)/shard_map/ppermute | solution.py:25
  31.6 0.6 copy-done.13
  32.2 5.2 %shard_map.49 = (bf16[1024,1024]{1,0:T(8,128)(2,1)}, f32[8,1024]{1,0:T(8,128)}, f32[64,1024]{1,0:T(8,128)}, bf16[64,1024]{1,0:T(8,128)(2,1)}) custom-call(s32[1]{0:T(128)} %bitcast.core, bf16[128,1024]{1,0:T(8,128)(2,1)} %refs_0_.2, bf16[128,1024]{1,0:T(8,128)(2,1)} %copy-done.8, bf16[128,1024]{1,0:T(8,128)(2,1)} %copy-done.9, bf16[128,1024]{1,0:T(8,128)(2,1)} %copy-done.13, ...), custom_call_target="tpu_custom_call" | custom-call | tf_op jit(solution)/shard_map/pallas_call | solution.py:61
  37.5 1.5 %collective-permute-done.10 = bf16[64,1024]{1,0:T(8,128)(2,1)S(1)} collective-permute-done((bf16[64,1024]{1,0:T(8,128)(2,1)}, bf16[64,1024]{1,0:T(8,128)(2,1)S(1)}, u32[]{:S(2)}, u32[]{:S(2)}) %collective-permute-start.10) | collective-permute-done | bytes 131104 | tf_op jit(solution)/shard_map/ppermute | solution.py:29
  39.1 1.0 add_convert_fusion.1
  40.1 0.2 collective-permute-start.12
  40.3 1.9 %collective-permute-start.11 = (bf16[128,1024]{1,0:T(8,128)(2,1)S(1)}, bf16[128,1024]{1,0:T(8,128)(2,1)S(1)}, u32[]{:S(2)}, u32[]{:S(2)}) collective-permute-start(bf16[128,1024]{1,0:T(8,128)(2,1)S(1)} %slice.17), channel_id=1, source_target_pairs={{0,16},{16,32},{32,48},{48,0},{64,80},{80,96},{96,112},{112,64},{1... | collective-permute-start | bytes 786440 | tf_op jit(solution)/shard_map/ppermute | solution.py:25
  42.3 15.0 %all_to_all.56 = bf16[8,8,1024]{2,1,0:T(8,128)(2,1)S(1)} all-to-all(bf16[8,8,1024]{2,1,0:T(8,128)(2,1)S(1)} %bitcast.18), channel_id=1, replica_groups={{0,2,4,6,8,10,12,14},{1,3,5,7,9,11,13,15},{16,18,20,22,24,26,28,30},{17..., dimensions={0} | all-to-all | bytes 262144 | tf_op jit(solution)/shard_map/all_to_all | solution.py:35
  57.4 0.6 copy-done.14
  58.1 5.8 %shard_map.50 = (bf16[1024,1024]{1,0:T(8,128)(2,1)}, f32[8,1024]{1,0:T(8,128)}, f32[64,1152]{1,0:T(8,128)}, bf16[64,1152]{1,0:T(8,128)(2,1)}) custom-call(s32[1]{0:T(128)} %bitcast.core, bf16[128,1024]{1,0:T(8,128)(2,1)} %refs_0_.3, bf16[256,1024]{1,0:T(8,128)(2,1)} %copy-done.1, bf16[256,1024]{1,0:T(8,128)(2,1)} %copy-done, bf16[128,1024]{1,0:T(8,128)(2,1)} %copy-done.15, ...), custom_call_target="tpu_custom_call" | custom-call | tf_op jit(solution)/shard_map/pallas_call | solution.py:61
  64.0 0.7 broadcast_in_dim.7
  64.7 3.4 %all-to-all-start.3 = ((bf16[8,8,1024]{2,1,0:T(8,128)(2,1)}), bf16[8,8,1024]{2,1,0:T(8,128)(2,1)S(1)}, u32[]{:S(2)}, u32[]{:S(2)}) async-start(bf16[8,8,1024]{2,1,0:T(8,128)(2,1)} %broadcast_in_dim.7), calls=%async_computation.3 | async-start | bytes 262144 | tf_op jit(solution)/shard_map/all_to_all | solution.py:35
  68.1 1.7 %fusion = bf16[8,8,1152]{2,1,0:T(8,128)(2,1)} fusion(f32[64,1152]{1,0:T(8,128)} %get-tuple-element.34, bf16[64,1152]{1,0:T(8,128)(2,1)S(1)} %collective-permute-done.13), kind=kLoop, calls=%fused_computation.5 | loop fusion | flops 221184 | bytes 589824 | tf_op jit(solution)/shard_map/all_to_all | solution.py:35
  69.7 6.4 %all-to-all-done.3 = bf16[8,8,1024]{2,1,0:T(8,128)(2,1)S(1)} async-done(((bf16[8,8,1024]{2,1,0:T(8,128)(2,1)}), bf16[8,8,1024]{2,1,0:T(8,128)(2,1)S(1)}, u32[]{:S(2)}, u32[]{:S(2)}) %all-to-all-start.3) | async-done | bytes 131104 | tf_op jit(solution)/shard_map/all_to_all | solution.py:35
  76.1 3.4 %all-to-all-start.1 = ((bf16[8,8,1152]{2,1,0:T(8,128)(2,1)}), bf16[8,8,1152]{2,1,0:T(8,128)(2,1)S(1)}, u32[]{:S(2)}, u32[]{:S(2)}) async-start(bf16[8,8,1152]{2,1,0:T(8,128)(2,1)} %fusion), calls=%async_computation.1 | async-start | bytes 294912 | tf_op jit(solution)/shard_map/all_to_all | solution.py:35
  79.6 7.8 %all-to-all-done.1 = bf16[8,8,1152]{2,1,0:T(8,128)(2,1)S(1)} async-done(((bf16[8,8,1152]{2,1,0:T(8,128)(2,1)}), bf16[8,8,1152]{2,1,0:T(8,128)(2,1)S(1)}, u32[]{:S(2)}, u32[]{:S(2)}) %all-to-all-start.1) | async-done | bytes 147488 | tf_op jit(solution)/shard_map/all_to_all | solution.py:35
  87.4 0.7 broadcast_in_dim.6
  88.1 3.4 %all-to-all-start.2 = ((bf16[8,8,1024]{2,1,0:T(8,128)(2,1)}), bf16[8,8,1024]{2,1,0:T(8,128)(2,1)S(1)}, u32[]{:S(2)}, u32[]{:S(2)}) async-start(bf16[8,8,1024]{2,1,0:T(8,128)(2,1)} %broadcast_in_dim.6), calls=%async_computation.2 | async-start | bytes 262144 | tf_op jit(solution)/shard_map/all_to_all | solution.py:35
  91.5 0.6 copy-done.6
  92.1 2.9 %shard_map.53 = (f32[128,1024]{1,0:T(8,128)}, f32[64,1024]{1,0:T(8,128)}) custom-call(s32[1]{0:T(128)} %bitcast.core, bf16[64,1024]{1,0:T(8,128)(2,1)} %bitcast.12, bf16[64,1024]{1,0:T(8,128)(2,1)} %copy-done.6, bf16[1024,1024]{1,0:T(8,128)(2,1)} %get-tuple-element.36.other.full.own, bf16[1024,1024]{1,0:T(8,128)(2,1)} %get-tuple-element.33.refs_6_.full.own.other, ...), custom_call_target="tpu_custom_call" | custom-call | tf_op jit(solution)/shard_map/pallas_call | solution.py:61
  95.0 4.3 %all-to-all-done.2 = bf16[8,8,1024]{2,1,0:T(8,128)(2,1)S(1)} async-done(((bf16[8,8,1024]{2,1,0:T(8,128)(2,1)}), bf16[8,8,1024]{2,1,0:T(8,128)(2,1)S(1)}, u32[]{:S(2)}, u32[]{:S(2)}) %all-to-all-start.2) | async-done | bytes 131104 | tf_op jit(solution)/shard_map/all_to_all | solution.py:35
  99.3 3.4 %all-to-all-start.5 = ((f32[8,8,1024]{2,1,0:T(8,128)}), f32[8,8,1024]{2,1,0:T(8,128)S(1)}, u32[]{:S(2)}, u32[]{:S(2)}) async-start(f32[8,8,1024]{2,1,0:T(8,128)} %bitcast.20), calls=%async_computation.5 | async-start | bytes 524288 | tf_op jit(solution)/shard_map/all_to_all | solution.py:305
  102.8 0.1 slice_reduce_fusion
  102.9 1.2 collective-permute-done.14.theirs
  104.2 0.7 copy-done.16
  104.8 3.1 %shard_map.51 = (f32[128,1024]{1,0:T(8,128)}, f32[64,1024]{1,0:T(8,128)}) custom-call(s32[1]{0:T(128)} %bitcast.core, bf16[64,1024]{1,0:T(8,128)(2,1)} %bitcast.17, bf16[64,1024]{1,0:T(8,128)(2,1)} %copy-done.16, bf16[1024,1024]{1,0:T(8,128)(2,1)} %get-tuple-element.33.refs_6_.full.own.other, bf16[1024,1024]{1,0:T(8,128)(2,1)} %get-tuple-element.36.other.full.own, ...), custom_call_target="tpu_custom_call" | custom-call | tf_op jit(solution)/shard_map/pallas_call | solution.py:61
  108.0 2.0 %all-to-all-done.5 = f32[8,8,1024]{2,1,0:T(8,128)S(1)} async-done(((f32[8,8,1024]{2,1,0:T(8,128)}), f32[8,8,1024]{2,1,0:T(8,128)S(1)}, u32[]{:S(2)}, u32[]{:S(2)}) %all-to-all-start.5) | async-done | bytes 262176 | tf_op jit(solution)/shard_map/all_to_all | solution.py:305
  110.0 3.6 %all-to-all-start.4 = ((f32[8,8,1024]{2,1,0:T(8,128)}), f32[8,8,1024]{2,1,0:T(8,128)S(1)}, u32[]{:S(2)}, u32[]{:S(2)}) async-start(f32[8,8,1024]{2,1,0:T(8,128)} %bitcast.19), calls=%async_computation.4 | async-start | bytes 524288 | tf_op jit(solution)/shard_map/all_to_all | solution.py:305
  113.6 1.2 collective-permute-done.16
  114.8 0.7 broadcast_add_fusion.refs_0_
  115.5 2.0 %shard_map.54 = bf16[128,1024]{1,0:T(8,128)(2,1)} custom-call(s32[1]{0:T(128)} %bitcast.core, f32[64,1024]{1,0:T(8,128)} %bitcast.15, f32[128,1024]{1,0:T(8,128)} %get-tuple-element.44.grad, bf16[1024,1024]{1,0:T(8,128)(2,1)} %get-tuple-element.36.other.full.own, f32[8,1024]{1,0:T(8,128)} %get-tuple-element.37.vecs.scale), custom_call_target="tpu_custom_call" | custom-call | tf_op jit(solution)/shard_map/pallas_call | solution.py:61
  117.4 3.7 %all-to-all-done.4 = f32[8,8,1024]{2,1,0:T(8,128)S(1)} async-done(((f32[8,8,1024]{2,1,0:T(8,128)}), f32[8,8,1024]{2,1,0:T(8,128)S(1)}, u32[]{:S(2)}, u32[]{:S(2)}) %all-to-all-start.4) | async-done | bytes 262176 | tf_op jit(solution)/shard_map/all_to_all | solution.py:305
  121.1 0.7 copy-done.3
  121.8 2.0 %shard_map.52 = (bf16[128,1024]{1,0:T(8,128)(2,1)}, f32[1]{0:T(128)}) custom-call(s32[1]{0:T(128)} %bitcast.core, f32[64,1024]{1,0:T(8,128)} %bitcast.14, f32[128,1024]{1,0:T(8,128)} %get-tuple-element.39.grad, bf16[1024,1024]{1,0:T(8,128)(2,1)} %get-tuple-element.33.refs_6_.full.own.other, f32[8,1024]{1,0:T(8,128)} %get-tuple-element.40.scale, ...), custom_call_target="tpu_custom_call" | custom-call | tf_op jit(solution)/shard_map/pallas_call | solution.py:61
  (51 shorter events, 0.7 us)
Async XLA Ops:
  0.6 9.7 %collective-permute-start = (bf16[128,1024]{1,0:T(8,128)(2,1)}, bf16[128,1024]{1,0:T(8,128)(2,1)S(1)}, u32[]{:S(2)}, u32[]{:S(2)}) collective-permute-start(bf16[128,1024]{1,0:T(8,128)(2,1)} %refs_0_.2), channel_id=1, source_target_pairs={{0,16},{16,32},{32,48},{48,0},{64,80},{80,96},{96,112},{112,64},{1... | collective-permute-start | bytes 786440 | tf_op jit(solution)/shard_map/ppermute | solution.py:25
  2.4 8.0 %collective-permute-start.1 = (bf16[128,1024]{1,0:T(8,128)(2,1)}, bf16[128,1024]{1,0:T(8,128)(2,1)S(1)}, u32[]{:S(2)}, u32[]{:S(2)}) collective-permute-start(bf16[128,1024]{1,0:T(8,128)(2,1)} %refs_0_.2), channel_id=1, source_target_pairs={{0,48},{16,0},{32,16},{48,32},{64,112},{80,64},{96,80},{112,96},{1... | collective-permute-start | bytes 786440 | tf_op jit(solution)/shard_map/ppermute | solution.py:25
  3.9 8.1 %collective-permute-start.2 = (bf16[128,1024]{1,0:T(8,128)(2,1)}, bf16[128,1024]{1,0:T(8,128)(2,1)S(1)}, u32[]{:S(2)}, u32[]{:S(2)}) collective-permute-start(bf16[128,1024]{1,0:T(8,128)(2,1)} %refs_0_.2), channel_id=1, source_target_pairs={{0,64},{16,80},{32,96},{48,112},{64,0},{80,16},{96,32},{112,48},{1... | collective-permute-start | bytes 786440 | tf_op jit(solution)/shard_map/ppermute | solution.py:25
  10.3 21.2 %copy-start.8 = (bf16[128,1024]{1,0:T(8,128)(2,1)}, bf16[128,1024]{1,0:T(8,128)(2,1)S(1)}, u32[]{:S(2)}) copy-start(bf16[128,1024]{1,0:T(8,128)(2,1)S(1)} %collective-permute-done.refs_1_) | copy-start | bytes 786436
  10.3 21.2 %copy-start.9 = (bf16[128,1024]{1,0:T(8,128)(2,1)}, bf16[128,1024]{1,0:T(8,128)(2,1)S(1)}, u32[]{:S(2)}) copy-start(bf16[128,1024]{1,0:T(8,128)(2,1)S(1)} %collective-permute-done.1.refs_2_) | copy-start | bytes 786436
  12.1 19.5 %copy-start.10 = (bf16[128,1024]{1,0:T(8,128)(2,1)}, bf16[128,1024]{1,0:T(8,128)(2,1)S(1)}, u32[]{:S(2)}) copy-start(bf16[128,1024]{1,0:T(8,128)(2,1)S(1)} %collective-permute-done.2.refs_4_) | copy-start | bytes 786436
  12.1 7.0 %collective-permute-start.5 = (bf16[128,1024]{1,0:T(8,128)(2,1)S(1)}, bf16[128,1024]{1,0:T(8,128)(2,1)S(1)}, u32[]{:S(2)}, u32[]{:S(2)}) collective-permute-start(bf16[128,1024]{1,0:T(8,128)(2,1)S(1)} %collective-permute-done.2.refs_4_), channel_id=1, source_target_pairs={{0,48},{16,0},{32,16},{48,32},{64,112},{80,64},{96,80},{112,96},{1... | collective-permute-start | bytes 786440 | tf_op jit(solution)/shard_map/ppermute | solution.py:25
  13.7 8.0 %collective-permute-start.3 = (bf16[128,1024]{1,0:T(8,128)(2,1)}, bf16[128,1024]{1,0:T(8,128)(2,1)S(1)}, u32[]{:S(2)}, u32[]{:S(2)}) collective-permute-start(bf16[128,1024]{1,0:T(8,128)(2,1)} %refs_0_.3), channel_id=1, source_target_pairs={{0,64},{16,80},{32,96},{48,112},{64,0},{80,16},{96,32},{112,48},{1... | collective-permute-start | bytes 786440 | tf_op jit(solution)/shard_map/ppermute | solution.py:25
  15.4 10.5 %collective-permute-start.4 = (bf16[128,1024]{1,0:T(8,128)(2,1)S(1)}, bf16[128,1024]{1,0:T(8,128)(2,1)S(1)}, u32[]{:S(2)}, u32[]{:S(2)}) collective-permute-start(bf16[128,1024]{1,0:T(8,128)(2,1)S(1)} %collective-permute-done.2.refs_4_), channel_id=1, source_target_pairs={{0,16},{16,32},{32,48},{48,0},{64,80},{80,96},{96,112},{112,64},{1... | collective-permute-start | bytes 786440 | tf_op jit(solution)/shard_map/ppermute | solution.py:25
  15.8 15.7 %collective-permute-start.8 = (bf16[128,1024]{1,0:T(8,128)(2,1)S(1)}, bf16[128,1024]{1,0:T(8,128)(2,1)S(1)}, u32[]{:S(2)}, u32[]{:S(2)}) collective-permute-start(bf16[128,1024]{1,0:T(8,128)(2,1)S(1)} %collective-permute-done.refs_1_), channel_id=1, source_target_pairs={{0,16},{16,32},{32,48},{48,0},{64,80},{80,96},{96,112},{112,64},{1... | collective-permute-start | bytes 786440 | tf_op jit(solution)/shard_map/ppermute | solution.py:25
  19.1 12.5 %copy-start.11 = (bf16[128,1024]{1,0:T(8,128)(2,1)}, bf16[128,1024]{1,0:T(8,128)(2,1)S(1)}, u32[]{:S(2)}) copy-start(bf16[128,1024]{1,0:T(8,128)(2,1)S(1)} %collective-permute-done.5.refs_6_) | copy-start | bytes 786436
  19.1 12.4 %collective-permute-start.9 = (bf16[128,1024]{1,0:T(8,128)(2,1)S(1)}, bf16[128,1024]{1,0:T(8,128)(2,1)}, u32[]{:S(2)}, u32[]{:S(2)}) collective-permute-start(bf16[128,1024]{1,0:T(8,128)(2,1)S(1)} %collective-permute-done.5.refs_6_), channel_id=1, source_target_pairs={{0,48},{16,0},{32,16},{48,32},{64,112},{80,64},{96,80},{112,96},{1... | collective-permute-start | bytes 786440 | tf_op jit(solution)/shard_map/ppermute | solution.py:25
  21.8 18.3 %copy-start.4 = (bf16[128,1024]{1,0:T(8,128)(2,1)}, bf16[128,1024]{1,0:T(8,128)(2,1)S(1)}, u32[]{:S(2)}) copy-start(bf16[128,1024]{1,0:T(8,128)(2,1)S(1)} %collective-permute-done.3.refs_4_) | copy-start | bytes 786436
  25.9 5.7 %copy-start.12 = (bf16[128,1024]{1,0:T(8,128)(2,1)}, bf16[128,1024]{1,0:T(8,128)(2,1)S(1)}, u32[]{:S(2)}) copy-start(bf16[128,1024]{1,0:T(8,128)(2,1)S(1)} %collective-permute-done.4.refs_5_) | copy-start | bytes 786436
  25.9 14.1 %collective-permute-start.7 = (bf16[256,1024]{1,0:T(8,128)(2,1)S(1)}, bf16[256,1024]{1,0:T(8,128)(2,1)S(1)}, u32[]{:S(2)}, u32[]{:S(2)}) collective-permute-start(bf16[256,1024]{1,0:T(8,128)(2,1)S(1)} %pad_maximum_fusion), channel_id=1, source_target_pairs={{0,48},{16,0},{32,16},{48,32},{64,112},{80,64},{96,80},{112,96},{1... | collective-permute-start | bytes 1572872 | tf_op jit(solution)/shard_map/ppermute | solution.py:25
  25.9 14.4 %collective-permute-start.6 = (bf16[256,1024]{1,0:T(8,128)(2,1)S(1)}, bf16[256,1024]{1,0:T(8,128)(2,1)S(1)}, u32[]{:S(2)}, u32[]{:S(2)}) collective-permute-start(bf16[256,1024]{1,0:T(8,128)(2,1)S(1)} %pad_maximum_fusion), channel_id=1, source_target_pairs={{0,16},{16,32},{32,48},{48,0},{64,80},{80,96},{96,112},{112,64},{1... | collective-permute-start | bytes 1572872 | tf_op jit(solution)/shard_map/ppermute | solution.py:25
  31.5 0.7 copy-start.13
  37.4 1.6 %collective-permute-start.10 = (bf16[64,1024]{1,0:T(8,128)(2,1)}, bf16[64,1024]{1,0:T(8,128)(2,1)S(1)}, u32[]{:S(2)}, u32[]{:S(2)}) collective-permute-start(bf16[64,1024]{1,0:T(8,128)(2,1)} %get-tuple-element.28), channel_id=1, source_target_pairs={{0,1},{1,0},{2,3},{3,2},{4,5},{5,4},{6,7},{7,6},{8,9},{9,8},{10,11... | collective-permute-start | bytes 393224 | tf_op jit(solution)/shard_map/ppermute | solution.py:29
  40.0 17.3 %copy-start = (bf16[256,1024]{1,0:T(8,128)(2,1)}, bf16[256,1024]{1,0:T(8,128)(2,1)S(1)}, u32[]{:S(2)}) copy-start(bf16[256,1024]{1,0:T(8,128)(2,1)S(1)} %collective-permute-done.7.refs_2_) | copy-start | bytes 1572868
  40.1 17.2 %collective-permute-start.12 = (bf16[128,1024]{1,0:T(8,128)(2,1)S(1)}, bf16[128,1024]{1,0:T(8,128)(2,1)S(1)}, u32[]{:S(2)}, u32[]{:S(2)}) collective-permute-start(bf16[128,1024]{1,0:T(8,128)(2,1)S(1)} %slice.18), channel_id=1, source_target_pairs={{0,48},{16,0},{32,16},{48,32},{64,112},{80,64},{96,80},{112,96},{1... | collective-permute-start | bytes 786440 | tf_op jit(solution)/shard_map/ppermute | solution.py:25
  40.3 17.1 %copy-start.1 = (bf16[256,1024]{1,0:T(8,128)(2,1)}, bf16[256,1024]{1,0:T(8,128)(2,1)S(1)}, u32[]{:S(2)}) copy-start(bf16[256,1024]{1,0:T(8,128)(2,1)S(1)} %collective-permute-done.6.refs_1_) | copy-start | bytes 1572868
  40.3 17.0 %collective-permute-start.11 = (bf16[128,1024]{1,0:T(8,128)(2,1)S(1)}, bf16[128,1024]{1,0:T(8,128)(2,1)S(1)}, u32[]{:S(2)}, u32[]{:S(2)}) collective-permute-start(bf16[128,1024]{1,0:T(8,128)(2,1)S(1)} %slice.17), channel_id=1, source_target_pairs={{0,16},{16,32},{32,48},{48,0},{64,80},{80,96},{96,112},{112,64},{1... | collective-permute-start | bytes 786440 | tf_op jit(solution)/shard_map/ppermute | solution.py:25
  57.3 0.7 copy-start.14
  57.4 0.8 copy-start.15
  63.9 4.1 %collective-permute-start.13 = (bf16[64,1152]{1,0:T(8,128)(2,1)}, bf16[64,1152]{1,0:T(8,128)(2,1)S(1)}, u32[]{:S(2)}, u32[]{:S(2)}) collective-permute-start(bf16[64,1152]{1,0:T(8,128)(2,1)} %get-tuple-element.35), channel_id=1, source_target_pairs={{0,1},{1,0},{2,3},{3,2},{4,5},{5,4},{6,7},{7,6},{8,9},{9,8},{10,11... | collective-permute-start | bytes 442376 | tf_op jit(solution)/shard_map/ppermute | solution.py:29
  64.7 11.4 %all-to-all-start.3 = ((bf16[8,8,1024]{2,1,0:T(8,128)(2,1)}), bf16[8,8,1024]{2,1,0:T(8,128)(2,1)S(1)}, u32[]{:S(2)}, u32[]{:S(2)}) async-start(bf16[8,8,1024]{2,1,0:T(8,128)(2,1)} %broadcast_in_dim.7), calls=%async_computation.3 | async-start | bytes 262144 | tf_op jit(solution)/shard_map/all_to_all | solution.py:35
  76.1 15.4 %copy-start.2 = (bf16[8,8,1024]{2,1,0:T(8,128)(2,1)}, bf16[8,8,1024]{2,1,0:T(8,128)(2,1)S(1)}, u32[]{:S(2)}) copy-start(bf16[8,8,1024]{2,1,0:T(8,128)(2,1)S(1)} %all-to-all-done.3) | copy-start | bytes 393220
  76.1 11.3 %all-to-all-start.1 = ((bf16[8,8,1152]{2,1,0:T(8,128)(2,1)}), bf16[8,8,1152]{2,1,0:T(8,128)(2,1)S(1)}, u32[]{:S(2)}, u32[]{:S(2)}) async-start(bf16[8,8,1152]{2,1,0:T(8,128)(2,1)} %fusion), calls=%async_computation.1 | async-start | bytes 294912 | tf_op jit(solution)/shard_map/all_to_all | solution.py:35
  79.5 12.0 %collective-permute-start.15 = (bf16[64,1024]{1,0:T(8,128)(2,1)S(1)}, bf16[64,1024]{1,0:T(8,128)(2,1)S(1)}, u32[]{:S(2)}, u32[]{:S(2)}) collective-permute-start(bf16[64,1024]{1,0:T(8,128)(2,1)S(1)} %bitcast.11), channel_id=1, source_target_pairs={{0,1},{1,0},{2,3},{3,2},{4,5},{5,4},{6,7},{7,6},{8,9},{9,8},{10,11... | collective-permute-start | bytes 393224 | tf_op jit(solution)/shard_map/ppermute | solution.py:29
  88.1 11.2 %all-to-all-start.2 = ((bf16[8,8,1024]{2,1,0:T(8,128)(2,1)}), bf16[8,8,1024]{2,1,0:T(8,128)(2,1)S(1)}, u32[]{:S(2)}, u32[]{:S(2)}) async-start(bf16[8,8,1024]{2,1,0:T(8,128)(2,1)} %broadcast_in_dim.6), calls=%async_computation.2 | async-start | bytes 262144 | tf_op jit(solution)/shard_map/all_to_all | solution.py:35
  91.5 0.7 copy-start.6
  99.3 4.9 %copy-start.7 = (bf16[8,8,1024]{2,1,0:T(8,128)(2,1)}, bf16[8,8,1024]{2,1,0:T(8,128)(2,1)S(1)}, u32[]{:S(2)}) copy-start(bf16[8,8,1024]{2,1,0:T(8,128)(2,1)S(1)} %all-to-all-done.2) | copy-start | bytes 393220
  99.3 10.6 %all-to-all-start.5 = ((f32[8,8,1024]{2,1,0:T(8,128)}), f32[8,8,1024]{2,1,0:T(8,128)S(1)}, u32[]{:S(2)}, u32[]{:S(2)}) async-start(f32[8,8,1024]{2,1,0:T(8,128)} %bitcast.20), calls=%async_computation.5 | async-start | bytes 524288 | tf_op jit(solution)/shard_map/all_to_all | solution.py:305
  102.7 1.4 %collective-permute-start.14 = (bf16[64,1024]{1,0:T(8,128)(2,1)S(1)}, bf16[64,1024]{1,0:T(8,128)(2,1)S(1)}, u32[]{:S(2)}, u32[]{:S(2)}) collective-permute-start(bf16[64,1024]{1,0:T(8,128)(2,1)S(1)} %bitcast.16), channel_id=1, source_target_pairs={{0,1},{1,0},{2,3},{3,2},{4,5},{5,4},{6,7},{7,6},{8,9},{9,8},{10,11... | collective-permute-start | bytes 393224 | tf_op jit(solution)/shard_map/ppermute | solution.py:29
  104.2 0.7 copy-start.16
  110.0 5.5 %copy-start.5 = (f32[8,8,1024]{2,1,0:T(8,128)}, f32[8,8,1024]{2,1,0:T(8,128)S(1)}, u32[]{:S(2)}) copy-start(f32[8,8,1024]{2,1,0:T(8,128)S(1)} %all-to-all-done.5) | copy-start | bytes 786436
  110.0 11.2 %all-to-all-start.4 = ((f32[8,8,1024]{2,1,0:T(8,128)}), f32[8,8,1024]{2,1,0:T(8,128)S(1)}, u32[]{:S(2)}, u32[]{:S(2)}) async-start(f32[8,8,1024]{2,1,0:T(8,128)} %bitcast.19), calls=%async_computation.4 | async-start | bytes 524288 | tf_op jit(solution)/shard_map/all_to_all | solution.py:305
  113.6 1.2 collective-permute-start.16
  121.1 0.7 copy-start.3

commit v5 on v3

--- a/solution.py
+++ b/solution.py
@@ -55,14 +55,15 @@
     a_far = send_sample(a_back[:rows], 0, 1)
     a_far_over = send_sample(a_on[rows:], 0, -1)
     b_far_over = send_sample(b_far, 1, 0)
-    parts_a = [a, a_back, a_on, a_far, a_pair[rows:], a_far_over]
-    parts_b = [b, b_back, b_on, b_far, b_over, b_far_over]
-    return parts_a, parts_b
-
-
-def call(kernel, steps, args, outs, scratch=(), limit=16):
-    def spec(shape, cut):
-        rows, cols = shape
+    parts = [a_pair, a_back, a_on, a_far, a_far_over, b, b_back, b_on, b_far, b_over, b_far_over]
+    where_a = [(0, 0), (1, 0), (2, 0), (3, 0), (0, 1), (1, 1), (2, 1), (4, 0)]
+    where_b = [(5, 0), (6, 0), (7, 0), (8, 0), (9, 0), (9, 1), (9, 2), (10, 0)]
+    return parts, *[[(i, j * rows) for i, j in where] for where in (where_a, where_b)]
+
+
+def call(kernel, steps, args, outs, scratch=(), aliases=None, limit=None):
+    def spec(shape, cut, rows=None):
+        rows, cols = rows or shape[0], shape[1]
         if cut:
             return pl.BlockSpec((rows, cols // steps), lambda i: (0, i))
         return pl.BlockSpec((rows, cols), lambda i: (0, 0))
@@ -76,11 +77,15 @@
         kernel,
         grid=(steps,),
         out_shape=[out for out, _ in outs],
-        in_specs=[pl.BlockSpec(memory_space=pltpu.SMEM)] + [spec(x.shape, c) for x, c in args[1:]],
+        in_specs=[pl.BlockSpec(memory_space=pltpu.SMEM)] + [
+            spec(arg[0].shape, *arg[1:]) for arg in args[1:]
+        ],
         out_specs=[out_spec(out, cut) for out, cut in outs],
         scratch_shapes=list(scratch),
-
-    )(*[args[0]] + [x for x, _ in args[1:]])
+        input_output_aliases=aliases or {},
+        compiler_params=pltpu.CompilerParams(vmem_limit_bytes=limit and limit << 20),
+
+    )(args[0], *[arg[0] for arg in args[1:]])
 
 
 def on_own(shape):
@@ -95,20 +100,15 @@
     return jnp.where(lane < LANES // 2, high, (wide - high).astype(BF16).astype(F32))
 
 
-def gram_kernel(core, *refs):
-    a, a_back, a_on, a_far, a_over, a_far_over = refs[:6]
-    b, b_back, b_on, b_far, b_over, b_far_over = refs[6:12]
-    full_a, full_b, vecs, keep, send, part_a, part_b, loss = refs[12:]
+def gram_kernel(core, *refs, where_a, where_b):
+    vecs, keep, send, part_a, part_b, loss = refs[-6:]
+    count = (len(refs) - 6) // 2
+    blocks, norms = refs[:count], refs[count : 2 * count]
     step = pl.program_id(0)
     steps = pl.num_programs(0)
-    rows, cols = a.shape
-    total_rows = full_a.shape[0]
+    cols = vecs.shape[1]
+    rows, total_rows = part_a.shape
     inv_rows = 1.0 / total_rows
-    top, high = pl.ds(0, rows), pl.ds(rows, rows)
-    raw_a = [(a, top), (a_back, top), (a_on, top), (a_far, top)]
-    raw_a += [(a_over, top), (a_back, high), (a_on, high), (a_far_over, top)]
-    raw_b = [(b, top), (b_back, top), (b_on, top), (b_far, top)]
-    raw_b += [(b_over, pl.ds(i * rows, rows)) for i in range(3)] + [(b_far_over, top)]
 
     @pl.when(step == 0)
     def _():
@@ -116,20 +116,22 @@
         part_b[...] = jnp.zeros_like(part_b)
         loss[...] = jnp.zeros_like(loss)
 
-    def view(raw, full, part):
-        floats = jnp.concatenate([ref[piece, :] for ref, piece in raw]).astype(F32)
+    def view(where, part):
+        floats = jnp.concatenate([blocks[i][pl.ds(first, rows), :] for i, first in where])
+        floats = floats.astype(F32)
         mean = jnp.sum(floats, axis=0, keepdims=True) * inv_rows
         square = jnp.sum(floats * floats, axis=0, keepdims=True) * inv_rows
         scale = lax.rsqrt(square - mean * mean + EPSILON)
         norm = ((floats - mean) * scale).astype(BF16)
-        full[...] = norm
+        for place, (i, first) in enumerate(where):
+            norms[i][pl.ds(first, rows), :] = norm[place * rows : (place + 1) * rows]
         part[...] += lax.dot_general(
             norm[:rows], norm, (((1,), (1,)), ((), ())), preferred_element_type=F32
         )
         return norm, scale
 
-    norm_a, scale_a = view(raw_a, full_a, part_a)
-    norm_b, scale_b = view(raw_b, full_b, part_b)
+    norm_a, scale_a = view(where_a, part_a)
+    norm_b, scale_b = view(where_b, part_b)
     diag = jnp.sum(norm_a.astype(F32) * norm_b.astype(F32), axis=0, keepdims=True) * inv_rows
     loss[...] += (1.0 - diag) * (1.0 - diag) - OFF_WEIGHT * diag * diag
     slope = (diag - 1.0) - OFF_WEIGHT * diag
@@ -154,7 +156,9 @@
             send[:, :total_rows] = gram_a.astype(BF16)
 
 
-def grad_kernel(core, mine, theirs, full_a, full_b, vecs, grad_na, grad_nb, stats, *, total_cols):
+def grad_kernel(core, mine, theirs, vecs, *refs, where_a, where_b, total_cols):
+    blocks = refs[:-3]
+    grad_na, grad_nb, stats = refs[-3:]
     rows, total_rows = mine.shape
     cols = grad_na.shape[1]
     factor = OFF_WEIGHT / total_rows
@@ -162,11 +166,16 @@
     first = core[0] == 0
     gram_a = jnp.where(first, mine[...], theirs[...])
     gram_b = jnp.where(first, theirs[...], mine[...])
-    norm_a = full_a[:rows, :].astype(F32)
-    norm_b = full_b[:rows, :].astype(F32)
+
+    def view(where):
+        return jnp.concatenate([blocks[i][pl.ds(first, rows), :] for i, first in where])
+
+    full_a, full_b = view(where_a), view(where_b)
+    norm_a = full_a[:rows].astype(F32)
+    norm_b = full_b[:rows].astype(F32)
     slope = vecs[2:3, :]
-    wide_a = jnp.dot(gram_b, full_a[...], preferred_element_type=F32)
-    wide_b = jnp.dot(gram_a, full_b[...], preferred_element_type=F32)
+    wide_a = jnp.dot(gram_b, full_a, preferred_element_type=F32)
+    wide_b = jnp.dot(gram_a, full_b, preferred_element_type=F32)
     wide_a = factor * wide_a + shift * norm_a + slope * norm_b
     wide_b = factor * wide_b + shift * norm_b + slope * norm_a
     grad_na[...] = wide_a
@@ -225,14 +234,13 @@
     core = (lax.axis_index("feat") & (CORES - 1)).reshape(1)
     shape = jax.ShapeDtypeStruct
 
-    parts_a, parts_b = gather_views(view_a, view_b)
-    full_a, full_b, vecs, keep, send = call(
-        gram_kernel,
-        4,
-        [core] + [(part, True) for part in parts_a + parts_b],
-        [
-            (shape((total_rows, cols), BF16), True),
-            (shape((total_rows, cols), BF16), True),
+    parts, where_a, where_b = gather_views(view_a, view_b)
+    *norms, vecs, keep, send = call(
+        functools.partial(gram_kernel, where_a=where_a, where_b=where_b),
+        2,
+        [core] + [(part, True) for part in parts],
+        [(shape(part.shape, BF16), True) for part in parts]
+        + [
             (shape((8, cols), F32), True),
             (shape((rows, total_rows + LANES), F32), False),
             (shape((rows, total_rows + LANES), BF16), False),
@@ -240,9 +248,10 @@
         [
             pltpu.VMEM((rows, total_rows), F32),
             pltpu.VMEM((rows, total_rows), F32),
-            pltpu.VMEM((1, cols // 4), F32),
-        ],
-        limit=24,
+            pltpu.VMEM((1, cols // 2), F32),
+        ],
+        aliases={i + 1: i for i in range(len(parts))},
+        limit=20,
     )
     total = (keep + swap_cores(send).astype(F32)).astype(BF16)
     moved = exchange_chips(total)
@@ -253,26 +262,30 @@
     diag = diag + swap_cores(diag)
     theirs = swap_cores(mine)
     grad_na, grad_nb, stats = call(
-        functools.partial(grad_kernel, total_cols=total_cols),
-        2,
-        [core, (mine, False), (theirs, False), (full_a, True), (full_b, True), (vecs, True)],
+        functools.partial(
+            grad_kernel, where_a=where_a, where_b=where_b, total_cols=total_cols
+        ),
+        1,
+        [core, (mine, False), (theirs, False), (vecs, True)] + [(norm, True) for norm in norms],
         [
             (shape((rows, cols), F32), True),
             (shape((rows, cols), F32), True),
             (shape((groups * 8, cols), F32), True),
         ],
+        limit=16,
     )
     stats = lax.all_to_all(stats, "sample", split_axis=0, concat_axis=0, tiled=True)
-    own = [(full_a[:rows], True), (full_b[:rows], True)]
+    own = [(norms[where[0][0]], True, rows) for where in (where_a, where_b)]
     grad_a, grad_b, loss = call(
         functools.partial(out_kernel, total_cols=total_cols),
-        2,
+        1,
         [core, (stats, True), (grad_na, True), (grad_nb, True)] + own + [(vecs, True), (diag, False)],
         [
             (shape((rows, cols), BF16), True),
             (shape((rows, cols), BF16), True),
             (shape((1,), F32), False),
         ],
+        limit=10,
     )
     return (loss.reshape(()), grad_a, grad_b)
 

time: 102 us -> 97.2 us (0.953)
  Pallas kernels: 14.1 us -> 9.44 us
  waiting for transfers between devices: 26.9 us -> 31.2 us
  local copies, waits for them, and re-layouts: 8.96 us -> 6.86 us
  other arithmetic: 3.04 us -> 1.23 us
    pallas_call x3, Pallas kernels: 14.1 us -> 9.44 us  [call(): pl.pallas_call(kernel, grid=(steps,), out_shape=[out for out, _ in outs],...]
    slice x2 -> x0, local copies, waits for them, and re-layouts: 3.34 us -> none  [body(): own = [(full_a[:rows], True), (full_b[:rows], True)]]
    all_to_all x1, waiting for transfers between devices: 3.55 us -> 6.45 us  [body(): lax.all_to_all(stats, 'sample', split_axis=0, concat_axis=0, tiled=True)]
    unnamed x24 -> x13, local copies, waits for them, and re-layouts: 4.01 us -> 5.28 us
    convert_element_type x1, other arithmetic: 1.13 us -> 0.06 us  [body(): total = (keep + swap_cores(send).astype(F32)).astype(BF16)]
  transfers between devices with their start and end apart: 15 -> 15, of which waited for: 8 -> 9; matrix products, arithmetic and copies ran while one was open for 8% -> 4% of each run, Pallas kernels for 0% -> 0%
where the time goes in v5:
time: 97.2 us; the launch traced here: 96.2 us
  waiting for transfers between devices  31.2 us (32%)
  blocking collectives  27.6 us (28%)
  starting transfers between devices  19.1 us (20%)
  Pallas kernels  9.44 us (10%)
  local copies, waits for them, and re-layouts  6.86 us (7%)
  other arithmetic  1.23 us (1%)
    all_to_all x2, blocking collectives, exchange_chips(): lax.all_to_all(block, 'feat', split_axis=0, concat_axis=0, tiled=True, ax...  27.6 us
    ppermute x11, waiting for transfers between devices, send_sample(): return lax.ppermute(block, 'sample', moves)  20.7 us
    ppermute x11, starting transfers between devices, send_sample(): return lax.ppermute(block, 'sample', moves)  15.4 us
    pallas_call x3, Pallas kernels, call(): pl.pallas_call(kernel, grid=(steps,), out_shape=[out for out, _ in outs],...  9.44 us
    all_to_all x1, waiting for transfers between devices, body(): lax.all_to_all(stats, 'sample', split_axis=0, concat_axis=0, tiled=True)  6.45 us
    unnamed x13, local copies, waits for them, and re-layouts  5.28 us
    ppermute x3, waiting for transfers between devices, swap_cores(): lax.ppermute(block, 'feat', [(i, i ^ 1) for i in range(lax.axis_size('fea...  4.04 us
    all_to_all x1, starting transfers between devices, body(): lax.all_to_all(stats, 'sample', split_axis=0, concat_axis=0, tiled=True)  3.54 us
  transfers between devices with their start and end apart: 15, of which 9 were waited for; matrix products, arithmetic and copies ran while one was open for 4% of the time, Pallas kernels for 0%

profile of v5, /device:TPU:0, one launch (start us, length us, event | category | flops | bytes accessed | tf_op | source)
XLA Modules:
  0.0 96.2 jit_solution(8338833185490162982)
XLA Ops:
  0.6 1.0 copy.30.refs_5_
  1.6 2.0 %collective-permute-start = (bf16[128,1024]{1,0:T(8,128)(2,1)}, bf16[128,1024]{1,0:T(8,128)(2,1)S(1)}, u32[]{:S(2)}, u32[]{:S(2)}) collective-permute-start(bf16[128,1024]{1,0:T(8,128)(2,1)} %param.2), channel_id=1, source_target_pairs={{0,64},{16,80},{32,96},{48,112},{64,0},{80,16},{96,32},{112,48},{1... | collective-permute-start | bytes 786440 | tf_op jit(solution)/shard_map/ppermute | solution.py:25
  3.6 3.0 %collective-permute-start.6 = (bf16[128,1024]{1,0:T(8,128)(2,1)S(1)}, bf16[128,1024]{1,0:T(8,128)(2,1)S(1)}, u32[]{:S(2)}, u32[]{:S(2)}) collective-permute-start(bf16[128,1024]{1,0:T(8,128)(2,1)S(1)} %copy.30.refs_5_), channel_id=1, source_target_pairs={{0,48},{16,0},{32,16},{48,32},{64,112},{80,64},{96,80},{112,96},{1... | collective-permute-start | bytes 786440 | tf_op jit(solution)/shard_map/ppermute | solution.py:25
  6.6 0.0 collective-permute-start.5
  6.6 1.0 %constant_dynamic-update-slice_fusion.1 = bf16[256,1024]{1,0:T(8,128)(2,1)S(1)} fusion(bf16[128,1024]{1,0:T(8,128)(2,1)} %param.2), kind=kLoop, calls=%fused_computation.5 | loop fusion | bytes 524288
  7.6 2.5 %collective-permute-done = bf16[128,1024]{1,0:T(8,128)(2,1)S(1)} collective-permute-done((bf16[128,1024]{1,0:T(8,128)(2,1)}, bf16[128,1024]{1,0:T(8,128)(2,1)S(1)}, u32[]{:S(2)}, u32[]{:S(2)}) %collective-permute-start) | collective-permute-done | bytes 262176 | tf_op jit(solution)/shard_map/ppermute | solution.py:25
  10.1 3.1 %collective-permute-start.2 = (bf16[256,1024]{1,0:T(8,128)(2,1)S(1)}, bf16[256,1024]{1,0:T(8,128)(2,1)S(1)}, u32[]{:S(2)}, u32[]{:S(2)}) collective-permute-start(bf16[256,1024]{1,0:T(8,128)(2,1)S(1)} %constant_dynamic-update-slice_fusion.refs_0_), channel_id=1, source_target_pairs={{0,48},{16,0},{32,16},{48,32},{64,112},{80,64},{96,80},{112,96},{1... | collective-permute-start | bytes 1572872 | tf_op jit(solution)/shard_map/ppermute | solution.py:25
  13.2 0.0 collective-permute-start.1
  13.2 0.0 collective-permute-done.6.refs_7_
  13.2 2.1 %collective-permute-done.5.refs_6_ = bf16[128,1024]{1,0:T(8,128)(2,1)S(1)} collective-permute-done((bf16[128,1024]{1,0:T(8,128)(2,1)S(1)}, bf16[128,1024]{1,0:T(8,128)(2,1)S(1)}, u32[]{:S(2)}, u32[]{:S(2)}) %collective-permute-start.5) | collective-permute-done | bytes 262176 | tf_op jit(solution)/shard_map/ppermute | solution.py:25
  15.3 0.9 pad_maximum_fusion
  16.2 0.3 collective-permute-start.9
  16.5 0.1 collective-permute-start.7
  16.6 3.3 %collective-permute-start.8 = (bf16[64,1024]{1,0:T(8,128)(2,1)S(1)}, bf16[64,1024]{1,0:T(8,128)(2,1)S(1)}, u32[]{:S(2)}, u32[]{:S(2)}) collective-permute-start(bf16[64,1024]{1,0:T(8,128)(2,1)S(1)} %slice.28), channel_id=1, source_target_pairs={{0,48},{16,0},{32,16},{48,32},{64,112},{80,64},{96,80},{112,96},{1... | collective-permute-start | bytes 393224 | tf_op jit(solution)/shard_map/ppermute | solution.py:25
  19.9 10.0 %collective-permute-done.7 = bf16[64,1024]{1,0:T(8,128)(2,1)S(1)} collective-permute-done((bf16[64,1024]{1,0:T(8,128)(2,1)S(1)}, bf16[64,1024]{1,0:T(8,128)(2,1)S(1)}, u32[]{:S(2)}, u32[]{:S(2)}) %collective-permute-start.7) | collective-permute-done | bytes 131104 | tf_op jit(solution)/shard_map/ppermute | solution.py:25
  29.9 0.0 collective-permute-done.8
  30.0 1.6 %collective-permute-start.10 = (bf16[128,1024]{1,0:T(8,128)(2,1)S(1)}, bf16[128,1024]{1,0:T(8,128)(2,1)}, u32[]{:S(2)}, u32[]{:S(2)}) collective-permute-start(bf16[128,1024]{1,0:T(8,128)(2,1)S(1)} %constant_dynamic-update-slice_fusion.2.refs_8_), channel_id=1, source_target_pairs={{0,64},{16,80},{32,96},{48,112},{64,0},{80,16},{96,32},{112,48},{1... | collective-permute-start | bytes 786440 | tf_op jit(solution)/shard_map/ppermute | solution.py:25
  31.6 0.0 collective-permute-done.2.refs_2_
  31.6 0.7 slice.26
  32.3 0.2 collective-permute-start.4
  32.6 0.0 collective-permute-done.1.refs_1_
  32.6 0.7 slice.25
  33.3 1.8 %collective-permute-start.3 = (bf16[128,1024]{1,0:T(8,128)(2,1)}, bf16[128,1024]{1,0:T(8,128)(2,1)}, u32[]{:S(2)}, u32[]{:S(2)}) collective-permute-start(bf16[128,1024]{1,0:T(8,128)(2,1)} %slice.25), channel_id=1, source_target_pairs={{0,16},{16,32},{32,48},{48,0},{64,80},{80,96},{96,112},{112,64},{1... | collective-permute-start | bytes 786440 | tf_op jit(solution)/shard_map/ppermute | solution.py:25
  35.1 4.9 %collective-permute-done.10.refs_10_ = bf16[128,1024]{1,0:T(8,128)(2,1)} collective-permute-done((bf16[128,1024]{1,0:T(8,128)(2,1)S(1)}, bf16[128,1024]{1,0:T(8,128)(2,1)}, u32[]{:S(2)}, u32[]{:S(2)}) %collective-permute-start.10) | collective-permute-done | bytes 262176 | tf_op jit(solution)/shard_map/ppermute | solution.py:25
  40.0 0.0 collective-permute-done.4.refs_4_
  40.0 1.2 %collective-permute-done.3.refs_3_ = bf16[128,1024]{1,0:T(8,128)(2,1)} collective-permute-done((bf16[128,1024]{1,0:T(8,128)(2,1)}, bf16[128,1024]{1,0:T(8,128)(2,1)}, u32[]{:S(2)}, u32[]{:S(2)}) %collective-permute-start.3) | collective-permute-done | bytes 262176 | tf_op jit(solution)/shard_map/ppermute | solution.py:25
  41.2 0.0 collective-permute-done.9.refs_9_
  41.2 6.2 %shard_map.49 = (bf16[256,1024]{1,0:T(8,128)(2,1)S(1)}, bf16[256,1024]{1,0:T(8,128)(2,1)S(1)}, bf16[256,1024]{1,0:T(8,128)(2,1)S(1)}, bf16[128,1024]{1,0:T(8,128...) custom-call(s32[1]{0:T(128)} %bitcast.core, ...), custom_call_target="tpu_custom_call", output_to_operand_aliasing={{0}: (1, {}), {1}: (2, {}), {2}: (3, {}), {3}: (4, {}), {4}... | custom-call | tf_op jit(solution)/shard_map/pallas_call | solution.py:76
  47.4 0.0 collective-permute-start.11
  47.4 1.6 %collective-permute-done.11 = bf16[128,1152]{1,0:T(8,128)(2,1)S(1)} collective-permute-done((bf16[128,1152]{1,0:T(8,128)(2,1)S(1)}, bf16[128,1152]{1,0:T(8,128)(2,1)S(1)}, u32[]{:S(2)}, u32[]{:S(2)}) %collective-permute-start.11) | collective-permute-done | bytes 294944 | tf_op jit(solution)/shard_map/ppermute | solution.py:29
  48.9 0.1 add_convert_fusion
  49.0 16.7 %all_to_all.28 = bf16[8,16,1152]{2,1,0:T(8,128)(2,1)S(1)} all-to-all(bf16[8,16,1152]{2,1,0:T(8,128)(2,1)S(1)} %bitcast.10), channel_id=1, replica_groups={{0,2,4,6,8,10,12,14},{1,3,5,7,9,11,13,15},{16,18,20,22,24,26,28,30},{17..., dimensions={0} | all-to-all | bytes 589824 | tf_op jit(solution)/shard_map/all_to_all | solution.py:35
  65.8 10.9 %all_to_all.29 = bf16[8,16,1024]{2,1,0:T(8,128)(2,1)S(1)} all-to-all(bf16[8,16,1024]{2,1,0:T(8,128)(2,1)S(1)} %broadcast_in_dim.4), channel_id=1, replica_groups={{0,2,4,6,8,10,12,14},{1,3,5,7,9,11,13,15},{16,18,20,22,24,26,28,30},{17..., dimensions={0} | all-to-all | bytes 524288 | tf_op jit(solution)/shard_map/all_to_all | solution.py:35
  76.7 0.0 collective-permute-start.12
  76.7 0.1 slice_reduce_fusion
  76.8 1.4 %collective-permute-done.12.theirs = bf16[128,1024]{1,0:T(8,128)(2,1)S(1)} collective-permute-done((bf16[128,1024]{1,0:T(8,128)(2,1)S(1)}, bf16[128,1024]{1,0:T(8,128)(2,1)S(1)}, u32[]{:S(2)}, u32[]{:S(2)}) %collective-permute-start.12) | collective-permute-done | bytes 262176 | tf_op jit(solution)/shard_map/ppermute | solution.py:29
  78.2 2.1 %shard_map.50 = (f32[128,1024]{1,0:T(8,128)S(1)}, f32[128,1024]{1,0:T(8,128)S(1)}, f32[64,1024]{1,0:T(8,128)S(1)}) custom-call(s32[1]{0:T(128)} %bitcast.core, bf16[128,1024]{1,0:T(8,128)(2,1)S(1)} %bitcast.8, bf16[128,1024]{1,0:T(8,128)(2,1)S(1)} %collective-permute-done.12.theirs, f32[8,1024]{1,0:T(8,128)S(1)} %get-tuple-element.25.vecs, ...), custom_call_target="tpu_custom_call" | custom-call | tf_op jit(solution)/shard_map/pallas_call | solution.py:76
  80.3 0.8 copy-done
  81.1 0.8 copy-done.2
  81.9 0.7 copy-done.4
  82.6 3.5 %all-to-all-start.2 = ((f32[8,8,1024]{2,1,0:T(8,128)}), f32[8,8,1024]{2,1,0:T(8,128)S(1)}, u32[]{:S(2)}, u32[]{:S(2)}) async-start(f32[8,8,1024]{2,1,0:T(8,128)} %bitcast.9), calls=%async_computation.2 | async-start | bytes 524288 | tf_op jit(solution)/shard_map/all_to_all | solution.py:277
  86.2 0.1 broadcast_in_dim.5
  86.3 0.1 collective-permute-start.13
  86.4 1.0 %collective-permute-done.13 = f32[8,128]{1,0:T(8,128)S(1)} collective-permute-done((f32[8,128]{1,0:T(8,128)S(1)}, f32[8,128]{1,0:T(8,128)S(1)}, u32[]{:S(2)}, u32[]{:S(2)}) %collective-permute-start.13) | collective-permute-done | bytes 4128 | tf_op jit(solution)/shard_map/ppermute | solution.py:29
  87.4 0.1 broadcast_add_fusion.diag
  87.5 6.4 %all-to-all-done.2 = f32[8,8,1024]{2,1,0:T(8,128)S(1)} async-done(((f32[8,8,1024]{2,1,0:T(8,128)}), f32[8,8,1024]{2,1,0:T(8,128)S(1)}, u32[]{:S(2)}, u32[]{:S(2)}) %all-to-all-start.2) | async-done | bytes 262176 | tf_op jit(solution)/shard_map/all_to_all | solution.py:277
  94.0 1.0 %copy-done.3 = f32[128,1024]{1,0:T(8,128)S(1)} copy-done((f32[128,1024]{1,0:T(8,128)S(1)}, f32[128,1024]{1,0:T(8,128)}, u32[]{:S(2)}) %copy-start.3) | copy-done | bytes 524312
  95.0 1.2 %shard_map.51 = (bf16[128,1024]{1,0:T(8,128)(2,1)}, bf16[128,1024]{1,0:T(8,128)(2,1)}, f32[1]{0:T(128)}) custom-call(s32[1]{0:T(128)} %bitcast.core, f32[64,1024]{1,0:T(8,128)S(1)} %bitcast.6, f32[128,1024]{1,0:T(8,128)S(1)} %copy-done.1, f32[128,1024]{1,0:T(8,128)S(1)} %copy-done.3, bf16[256,1024]{1,0:T(8,128)(2,1)S(1)} %get-tuple-element.26.refs_0_.own_a, ...), custom_call_target="tpu_custom_call" | custom-call | tf_op jit(solution)/shard_map/pallas_call | solution.py:76
  (15 shorter events, 0.1 us)
Async XLA Ops:
  1.6 8.5 %collective-permute-start = (bf16[128,1024]{1,0:T(8,128)(2,1)}, bf16[128,1024]{1,0:T(8,128)(2,1)S(1)}, u32[]{:S(2)}, u32[]{:S(2)}) collective-permute-start(bf16[128,1024]{1,0:T(8,128)(2,1)} %param.2), channel_id=1, source_target_pairs={{0,64},{16,80},{32,96},{48,112},{64,0},{80,16},{96,32},{112,48},{1... | collective-permute-start | bytes 786440 | tf_op jit(solution)/shard_map/ppermute | solution.py:25
  3.6 9.6 %collective-permute-start.6 = (bf16[128,1024]{1,0:T(8,128)(2,1)S(1)}, bf16[128,1024]{1,0:T(8,128)(2,1)S(1)}, u32[]{:S(2)}, u32[]{:S(2)}) collective-permute-start(bf16[128,1024]{1,0:T(8,128)(2,1)S(1)} %copy.30.refs_5_), channel_id=1, source_target_pairs={{0,48},{16,0},{32,16},{48,32},{64,112},{80,64},{96,80},{112,96},{1... | collective-permute-start | bytes 786440 | tf_op jit(solution)/shard_map/ppermute | solution.py:25
  6.6 8.7 %collective-permute-start.5 = (bf16[128,1024]{1,0:T(8,128)(2,1)S(1)}, bf16[128,1024]{1,0:T(8,128)(2,1)S(1)}, u32[]{:S(2)}, u32[]{:S(2)}) collective-permute-start(bf16[128,1024]{1,0:T(8,128)(2,1)S(1)} %copy.30.refs_5_), channel_id=1, source_target_pairs={{0,16},{16,32},{32,48},{48,0},{64,80},{80,96},{96,112},{112,64},{1... | collective-permute-start | bytes 786440 | tf_op jit(solution)/shard_map/ppermute | solution.py:25
  10.1 21.5 %collective-permute-start.2 = (bf16[256,1024]{1,0:T(8,128)(2,1)S(1)}, bf16[256,1024]{1,0:T(8,128)(2,1)S(1)}, u32[]{:S(2)}, u32[]{:S(2)}) collective-permute-start(bf16[256,1024]{1,0:T(8,128)(2,1)S(1)} %constant_dynamic-update-slice_fusion.refs_0_), channel_id=1, source_target_pairs={{0,48},{16,0},{32,16},{48,32},{64,112},{80,64},{96,80},{112,96},{1... | collective-permute-start | bytes 1572872 | tf_op jit(solution)/shard_map/ppermute | solution.py:25
  13.2 19.4 %collective-permute-start.1 = (bf16[256,1024]{1,0:T(8,128)(2,1)S(1)}, bf16[256,1024]{1,0:T(8,128)(2,1)S(1)}, u32[]{:S(2)}, u32[]{:S(2)}) collective-permute-start(bf16[256,1024]{1,0:T(8,128)(2,1)S(1)} %constant_dynamic-update-slice_fusion.refs_0_), channel_id=1, source_target_pairs={{0,16},{16,32},{32,48},{48,0},{64,80},{80,96},{96,112},{112,64},{1... | collective-permute-start | bytes 1572872 | tf_op jit(solution)/shard_map/ppermute | solution.py:25
  16.2 25.0 %collective-permute-start.9 = (bf16[384,1024]{1,0:T(8,128)(2,1)}, bf16[384,1024]{1,0:T(8,128)(2,1)S(1)}, u32[]{:S(2)}, u32[]{:S(2)}) collective-permute-start(bf16[384,1024]{1,0:T(8,128)(2,1)} %pad_maximum_fusion), channel_id=1, source_target_pairs={{0,64},{16,80},{32,96},{48,112},{64,0},{80,16},{96,32},{112,48},{1... | collective-permute-start | bytes 2359304 | tf_op jit(solution)/shard_map/ppermute | solution.py:25
  16.5 13.4 %collective-permute-start.7 = (bf16[64,1024]{1,0:T(8,128)(2,1)S(1)}, bf16[64,1024]{1,0:T(8,128)(2,1)S(1)}, u32[]{:S(2)}, u32[]{:S(2)}) collective-permute-start(bf16[64,1024]{1,0:T(8,128)(2,1)S(1)} %slice.27), channel_id=1, source_target_pairs={{0,16},{16,32},{32,48},{48,0},{64,80},{80,96},{96,112},{112,64},{1... | collective-permute-start | bytes 393224 | tf_op jit(solution)/shard_map/ppermute | solution.py:25
  16.6 13.3 %collective-permute-start.8 = (bf16[64,1024]{1,0:T(8,128)(2,1)S(1)}, bf16[64,1024]{1,0:T(8,128)(2,1)S(1)}, u32[]{:S(2)}, u32[]{:S(2)}) collective-permute-start(bf16[64,1024]{1,0:T(8,128)(2,1)S(1)} %slice.28), channel_id=1, source_target_pairs={{0,48},{16,0},{32,16},{48,32},{64,112},{80,64},{96,80},{112,96},{1... | collective-permute-start | bytes 393224 | tf_op jit(solution)/shard_map/ppermute | solution.py:25
  30.0 10.0 %collective-permute-start.10 = (bf16[128,1024]{1,0:T(8,128)(2,1)S(1)}, bf16[128,1024]{1,0:T(8,128)(2,1)}, u32[]{:S(2)}, u32[]{:S(2)}) collective-permute-start(bf16[128,1024]{1,0:T(8,128)(2,1)S(1)} %constant_dynamic-update-slice_fusion.2.refs_8_), channel_id=1, source_target_pairs={{0,64},{16,80},{32,96},{48,112},{64,0},{80,16},{96,32},{112,48},{1... | collective-permute-start | bytes 786440 | tf_op jit(solution)/shard_map/ppermute | solution.py:25
  32.3 7.6 %collective-permute-start.4 = (bf16[128,1024]{1,0:T(8,128)(2,1)}, bf16[128,1024]{1,0:T(8,128)(2,1)}, u32[]{:S(2)}, u32[]{:S(2)}) collective-permute-start(bf16[128,1024]{1,0:T(8,128)(2,1)} %slice.26), channel_id=1, source_target_pairs={{0,48},{16,0},{32,16},{48,32},{64,112},{80,64},{96,80},{112,96},{1... | collective-permute-start | bytes 786440 | tf_op jit(solution)/shard_map/ppermute | solution.py:25
  33.3 7.9 %collective-permute-start.3 = (bf16[128,1024]{1,0:T(8,128)(2,1)}, bf16[128,1024]{1,0:T(8,128)(2,1)}, u32[]{:S(2)}, u32[]{:S(2)}) collective-permute-start(bf16[128,1024]{1,0:T(8,128)(2,1)} %slice.25), channel_id=1, source_target_pairs={{0,16},{16,32},{32,48},{48,0},{64,80},{80,96},{96,112},{112,64},{1... | collective-permute-start | bytes 786440 | tf_op jit(solution)/shard_map/ppermute | solution.py:25
  47.4 1.6 %collective-permute-start.11 = (bf16[128,1152]{1,0:T(8,128)(2,1)S(1)}, bf16[128,1152]{1,0:T(8,128)(2,1)S(1)}, u32[]{:S(2)}, u32[]{:S(2)}) collective-permute-start(bf16[128,1152]{1,0:T(8,128)(2,1)S(1)} %get-tuple-element.24), channel_id=1, source_target_pairs={{0,1},{1,0},{2,3},{3,2},{4,5},{5,4},{6,7},{7,6},{8,9},{9,8},{10,11... | collective-permute-start | bytes 884744 | tf_op jit(solution)/shard_map/ppermute | solution.py:29
  76.7 1.5 %collective-permute-start.12 = (bf16[128,1024]{1,0:T(8,128)(2,1)S(1)}, bf16[128,1024]{1,0:T(8,128)(2,1)S(1)}, u32[]{:S(2)}, u32[]{:S(2)}) collective-permute-start(bf16[128,1024]{1,0:T(8,128)(2,1)S(1)} %bitcast.7), channel_id=1, source_target_pairs={{0,1},{1,0},{2,3},{3,2},{4,5},{5,4},{6,7},{7,6},{8,9},{9,8},{10,11... | collective-permute-start | bytes 786440 | tf_op jit(solution)/shard_map/ppermute | solution.py:29
  80.3 0.8 copy-start
  81.1 0.8 copy-start.2
  81.9 0.7 copy-start.4
  82.6 11.3 %copy-start.1 = (f32[128,1024]{1,0:T(8,128)S(1)}, f32[128,1024]{1,0:T(8,128)}, u32[]{:S(2)}) copy-start(f32[128,1024]{1,0:T(8,128)} %copy-done) | copy-start | bytes 1572868
  82.6 11.3 %all-to-all-start.2 = ((f32[8,8,1024]{2,1,0:T(8,128)}), f32[8,8,1024]{2,1,0:T(8,128)S(1)}, u32[]{:S(2)}, u32[]{:S(2)}) async-start(f32[8,8,1024]{2,1,0:T(8,128)} %bitcast.9), calls=%async_computation.2 | async-start | bytes 524288 | tf_op jit(solution)/shard_map/all_to_all | solution.py:277
  86.3 1.2 %collective-permute-start.13 = (f32[8,128]{1,0:T(8,128)S(1)}, f32[8,128]{1,0:T(8,128)S(1)}, u32[]{:S(2)}, u32[]{:S(2)}) collective-permute-start(f32[8,128]{1,0:T(8,128)S(1)} %broadcast_in_dim.5), channel_id=1, source_target_pairs={{0,1},{1,0},{2,3},{3,2},{4,5},{5,4},{6,7},{7,6},{8,9},{9,8},{10,11... | collective-permute-start | bytes 12296 | tf_op jit(solution)/shard_map/ppermute | solution.py:29
  94.0 1.0 %copy-start.3 = (f32[128,1024]{1,0:T(8,128)S(1)}, f32[128,1024]{1,0:T(8,128)}, u32[]{:S(2)}) copy-start(f32[128,1024]{1,0:T(8,128)} %copy-done.2) | copy-start | bytes 1572868

commit v6 on v2

v6 whole, which is shorter than its diff:
```python
import functools
import jax
import jax.numpy as jnp
from jax import lax
from jax.experimental import pallas as pl
from jax.experimental.pallas import tpu as pltpu
from jax.sharding import PartitionSpec as P

EPSILON = 1e-05
OFF_WEIGHT = 0.0051
RING = 4
CORES = 2
F32 = jnp.float32
BF16 = jnp.bfloat16
LANES = 128
SUMS = 4
CHUNK = 512


def send_sample(block, turn, step):
    pairs = lax.axis_size("sample") // RING
    moves = [
        (z * RING + y, (z + turn) % pairs * RING + (y + step) % RING)
        for z in range(pairs)
        for y in range(RING)
    ]
    return lax.ppermute(block, "sample", moves)


def swap_cores(block):
    return lax.ppermute(block, "feat", [(i, i ^ 1) for i in range(lax.axis_size("feat"))])


def exchange_chips(block):
    members = lax.axis_size("feat") // CORES
    groups = [[i * CORES + core for i in range(members)] for core in range(CORES)]
    return lax.all_to_all(
        block, "feat", split_axis=0, concat_axis=0, tiled=True, axis_index_groups=groups
    )


def repeat_block(block, members):
    copies = jnp.broadcast_to(block[None], (members,) + block.shape)
    return copies.reshape((members * block.shape[0],) + block.shape[1:])


def call(kernel, args, outs, scratch=(), aliases=None, limit=16):
    def spec(shape):
        return pl.BlockSpec(memory_space=pltpu.SMEM if shape == (1,) else pltpu.VMEM)

    return pl.pallas_call(
        kernel,
        out_shape=outs,
        in_specs=[spec(arg.shape) for arg in args],
        out_specs=[spec(out.shape) for out in outs],
        scratch_shapes=list(scratch),
        input_output_aliases=aliases or {},
        compiler_params=pltpu.CompilerParams(vmem_limit_bytes=limit << 20),
    )(*args)


def bring_kernel(*refs):
    for source, place in zip(refs[: len(refs) // 2], refs[len(refs) // 2 :]):
        place[...] = source[...]


def bring(*blocks):
    return call(bring_kernel, blocks, [jax.ShapeDtypeStruct(x.shape, x.dtype) for x in blocks])


def after(block, *others):
    return lax.optimization_barrier((block,) + others)[0]


def gather_views(a, b):
    rows = a.shape[0]
    b_back = send_sample(b, 0, 1)
    b_on = send_sample(b, 0, -1)
    a_over = send_sample(a, 1, 0)
    a_next = after(a, b_back, b_on, a_over)
    b_far = send_sample(after(b_on, a_over, b_back), 0, -1)
    b_over = send_sample(after(b, a_over, b_back, b_on), 1, 0)
    b_back_over = send_sample(b_back, 1, 0)
    b_on_over = send_sample(b_on, 1, 0)
    a_over_back = send_sample(after(a_over, b_back, b_on), 0, 1)
    a_back = send_sample(a_next, 0, 1)
    a_over_on = send_sample(after(a_over, b_back, b_on), 0, -1)
    a_on = send_sample(a_next, 0, -1)
    a_far = send_sample(a_back, 0, 1)
    a_over_far = send_sample(a_over_back, 0, 1)
    b_far_over = send_sample(b_far, 1, 0)
    a_own, b_own = bring(after(a, a_over, b_back, b_on), b)
    parts = [a_own, a_back, a_on, a_far, a_over, a_over_back, a_over_on, a_over_far]
    parts += [b_own, b_back, b_on, b_far, b_over, b_back_over, b_on_over, b_far_over]
    where_a = [(i, 0) for i in range(8)]
    where_b = [(i, 0) for i in range(8, 16)]
    return parts, *[[(i, j * rows) for i, j in where] for where in (where_a, where_b)]


def column_steps(cols):
    return [pl.ds(first, CHUNK) for first in range(0, cols, CHUNK)]


def on_own(shape):
    row_ids = lax.broadcasted_iota(jnp.int32, shape, 0)
    return row_ids == lax.broadcasted_iota(jnp.int32, shape, 1)


def split_scalar(value, rows):
    wide = jnp.broadcast_to(value, (rows, LANES))
    high = wide.astype(BF16).astype(F32)
    lane = lax.broadcasted_iota(jnp.int32, wide.shape, 1)
    return jnp.where(lane < LANES // 2, high, (wide - high).astype(BF16).astype(F32))


def gram_kernel(core, *refs, where_a, where_b):
    vecs, keep, send, part_a, part_b = refs[-5:]
    count = (len(refs) - 5) // 2
    blocks, norms = refs[:count], refs[count : 2 * count]
    cols = vecs.shape[1]
    rows, total_rows = part_a.shape
    inv_rows = 1.0 / total_rows

    def view(where, part, columns, first_step):
        floats = jnp.concatenate([blocks[i][pl.ds(first, rows), columns] for i, first in where])
        floats = floats.astype(F32)
        mean = jnp.sum(floats, axis=0, keepdims=True) * inv_rows
        square = jnp.sum(floats * floats, axis=0, keepdims=True) * inv_rows
        scale = lax.rsqrt(square - mean * mean + EPSILON)
        norm = ((floats - mean) * scale).astype(BF16)
        for place, (i, first) in enumerate(where):
            norms[i][pl.ds(first, rows), columns] = norm[place * rows : (place + 1) * rows]
        more = lax.dot_general(
            norm[:rows], norm, (((1,), (1,)), ((), ())), preferred_element_type=F32
        )
        part[...] = more if first_step else part[...] + more
        return norm, scale

    loss = jnp.zeros((1, CHUNK), F32)
    for step, columns in enumerate(column_steps(cols)):
        norm_a, scale_a = view(where_a, part_a, columns, step == 0)
        norm_b, scale_b = view(where_b, part_b, columns, step == 0)
        diag = jnp.sum(norm_a.astype(F32) * norm_b.astype(F32), axis=0, keepdims=True) * inv_rows
        loss += (1.0 - diag) * (1.0 - diag) - OFF_WEIGHT * diag * diag
        slope = (diag - 1.0) - OFF_WEIGHT * diag
        vecs[:, columns] = jnp.concatenate([scale_a, scale_b, slope, jnp.zeros((5, CHUNK), F32)])

    shift = jnp.where(on_own(part_a.shape), 1.0 * cols, 0.0)
    gram_a = part_a[...] - shift
    gram_b = part_b[...] - shift
    keep[:, total_rows:] = split_scalar(jnp.sum(loss, axis=1, keepdims=True), rows)
    send[:, total_rows:] = jnp.zeros((rows, LANES), BF16)

    @pl.when(core[0] == 0)
    def _():
        keep[:, :total_rows] = gram_a
        send[:, :total_rows] = gram_b.astype(BF16)

    @pl.when(core[0] != 0)
    def _():
        keep[:, :total_rows] = gram_b
        send[:, :total_rows] = gram_a.astype(BF16)


def by_view(core, mine, theirs):
    first = core[0] == 0
    return jnp.where(first, mine[...], theirs[...]), jnp.where(first, theirs[...], mine[...])


def gradients(grams, blocks, vecs, columns, where_a, where_b, total_cols):
    gram_a, gram_b = grams
    rows, total_rows = gram_a.shape
    factor = OFF_WEIGHT / total_rows

    def view(where):
        return jnp.concatenate([blocks[i][pl.ds(first, rows), columns] for i, first in where])

    full_a, full_b = view(where_a), view(where_b)
    norm_a = full_a[:rows].astype(F32)
    norm_b = full_b[:rows].astype(F32)
    slope = vecs[2:3, columns]
    wide_a = jnp.dot(gram_b, full_a, preferred_element_type=F32)
    wide_b = jnp.dot(gram_a, full_b, preferred_element_type=F32)
    wide_a = factor * wide_a + factor * total_cols * norm_a + slope * norm_b
    wide_b = factor * wide_b + factor * total_cols * norm_b + slope * norm_a
    return norm_a, norm_b, wide_a, wide_b


def grad_kernel(core, mine, theirs, vecs, *refs, **layout):
    blocks, (high_a, low_a, high_b, low_b, stats) = refs[:-5], refs[-5:]
    cols = high_a.shape[1]
    grams = by_view(core, mine, theirs)
    back = jnp.where(on_own(mine.shape), 1.0 * layout["total_cols"], 0.0)
    square = (grams[0].astype(F32) + back) * (grams[1].astype(F32) + back)
    square = jnp.sum(jnp.sum(square, axis=0, keepdims=True), axis=1, keepdims=True)
    for columns in column_steps(cols):
        norm_a, norm_b, wide_a, wide_b = gradients(grams, blocks, vecs, columns, **layout)
        for wide, high, low in ((wide_a, high_a, low_a), (wide_b, high_b, low_b)):
            high[:, columns] = wide.astype(BF16)
            low[:, columns] = (wide - wide.astype(BF16).astype(F32)).astype(BF16)
        sums = [
            jnp.sum(wide_a, axis=0, keepdims=True),
            jnp.sum(wide_a * norm_a, axis=0, keepdims=True),
            jnp.sum(wide_b, axis=0, keepdims=True),
            jnp.sum(wide_b * norm_b, axis=0, keepdims=True),
        ]
        sums = jnp.concatenate(sums)
        for member in range(stats.shape[0]):
            stats[member, :, columns] = sums
    square = jnp.broadcast_to(square, (SUMS, LANES))
    for member in range(stats.shape[0]):
        stats[member, :, pl.ds(cols, LANES)] = square


def out_kernel(
    core,
    stats,
    high_a,
    low_a,
    high_b,
    low_b,
    own_a,
    own_b,
    vecs,
    split,
    other,
    grad_a,
    grad_b,
    loss,
    *,
    total_cols
):
    del core
    rows, cols = grad_a.shape
    members = stats.shape[0]
    inv_rows = 1.0 / (rows * members)
    sums = stats[0]
    for member in range(1, members):
        sums += stats[member]
    square = jnp.max(sums[0:1, cols:]) * (inv_rows * inv_rows)
    means = sums[:, :cols] * inv_rows
    norm_a = own_a[:rows, :].astype(F32)
    norm_b = own_b[:rows, :].astype(F32)
    wide_a = high_a[...].astype(F32) + low_a[...].astype(F32) - means[0:1] - norm_a * means[1:2]
    wide_b = high_b[...].astype(F32) + low_b[...].astype(F32) - means[2:3] - norm_b * means[3:4]
    grad_a[...] = (vecs[0:1, :] * wide_a).astype(BF16)
    grad_b[...] = (vecs[1:2, :] * wide_b).astype(BF16)
    diag = jnp.sum(split[0:1, :] + other[0:1, :]) * (2.0 / LANES)
    loss[0] = (diag + OFF_WEIGHT * square) / total_cols


def body(view_a, view_b):
    rows, cols = view_a.shape
    groups = lax.axis_size("sample")
    blocks = lax.axis_size("feat")
    chips = blocks // CORES
    total_rows = rows * groups
    core = (lax.axis_index("feat") & (CORES - 1)).reshape(1)
    shape = jax.ShapeDtypeStruct

    parts, where_a, where_b = gather_views(view_a, view_b)
    layout = dict(where_a=where_a, where_b=where_b)
    first = [where[0][0] for where in (where_a, where_b)]
    *norms, vecs, keep, send = call(
        functools.partial(gram_kernel, **layout),
        [core] + parts,
        [shape(part.shape, BF16) for part in parts]
        + [
            shape((8, cols), F32),
            shape((rows, total_rows + LANES), F32),
            shape((rows, total_rows + LANES), BF16),
        ],
        [pltpu.VMEM((rows, total_rows), F32)] * 2,
        aliases={i + 1: i for i in range(len(parts))},
        limit=16,
    )
    total = (keep + swap_cores(send).astype(F32)).astype(BF16)
    moved = exchange_chips(total)
    summed = jnp.sum(moved.reshape(chips, -1, moved.shape[1]).astype(F32), axis=0)
    split = summed[:8, total_rows:]
    sums = repeat_block(summed[:, :total_rows].astype(BF16), chips)
    sums, split = lax.optimization_barrier((sums, split))
    mine = exchange_chips(sums)
    theirs = swap_cores(mine)
    layout["total_cols"] = cols * blocks
    spare = [where_a[3][0], where_a[4][0], where_b[3][0], where_b[4][0]]
    *grads, stats = call(
        functools.partial(grad_kernel, **layout),
        [core, mine, theirs, vecs] + norms,
        [shape((rows, cols), BF16)] * 4 + [shape((groups, SUMS, cols + LANES), F32)],
        aliases={4 + index: i for i, index in enumerate(spare)},
        limit=8,
    )
    stats = lax.all_to_all(stats, "sample", split_axis=0, concat_axis=0, tiled=True)
    own = [norms[i] for i in first]
    grad_a, grad_b, loss = call(
        functools.partial(out_kernel, total_cols=cols * blocks),
        [core, stats] + grads + own + [vecs, split, swap_cores(split)],
        [shape((rows, cols), BF16), shape((rows, cols), BF16), shape((1,), F32)],
        limit=8,
    )
    return (loss.reshape(()), grad_a, grad_b)


def solution(mesh):
    in_specs = (P("sample", "feat"), P("sample", "feat"))
    out_specs = (P(), P("sample", "feat"), P("sample", "feat"))
    return jax.shard_map(body, mesh=mesh, in_specs=in_specs, out_specs=out_specs, check_vma=False)
```

time: 108 us -> 91.5 us (0.85)
  Pallas kernels: 0 us -> 10.1 us
  other arithmetic: 9.09 us -> 0.09 us
  between operations: 7.34 us -> 0.71 us
  matrix products: 4.44 us -> 0 us
  local copies, waits for them, and re-layouts: 5.47 us -> 1.93 us
  starting transfers between devices: 21.7 us -> 19.1 us
    pallas_call x0 -> x4, Pallas kernels: none -> 10.1 us  [call(): pl.pallas_call(kernel, out_shape=outs, in_specs=[spec(arg.shape) for arg...]
    reduce_sum x5 -> x0, other arithmetic: 6.18 us -> none  [the longest x1 4.19 us: body(): diag = jnp.sum(full_a.astype(F32) * full_b.astype(F32), axis=0) * inv_rows]
    dot_general x4 -> x0, matrix products: 4.44 us -> none  [the longest x2 3.34 us: gram_rows(): lax.dot_general(own, full, (((1,), (1,)), ((), ())), preferred_element_ty...]
    convert_element_type x3 -> x1, other arithmetic: 2.08 us -> 0.05 us  [body(): total = (keep + swap_cores(send).astype(F32)).astype(BF16)]
    ppermute x11 -> x14, starting transfers between devices: 17.4 us -> 15.5 us  [send_sample(): return lax.ppermute(block, 'sample', moves)]
    slice x9 -> x2, local copies, waits for them, and re-layouts: 1.8 us -> 0.01 us  [the longest x1 0.01 us: body(): sums = repeat_block(summed[:, :total_rows].astype(BF16), chips)]
    ppermute x11 -> x14, waiting for transfers between devices: 23.5 us -> 22.1 us  [send_sample(): return lax.ppermute(block, 'sample', moves)]
    ppermute x2 -> x3, waiting for transfers between devices: 3.1 us -> 4.14 us  [swap_cores(): lax.ppermute(block, 'feat', [(i, i ^ 1) for i in range(lax.axis_size('fea...]
  transfers between devices with their start and end apart: 14 -> 18, of which waited for: 8 -> 13; matrix products, arithmetic and copies ran while one was open for 3% -> 0% of each run, Pallas kernels for 0% -> 0%
where the time goes in v6:
time: 91.5 us; the launch traced here: 91.1 us
  waiting for transfers between devices  31.6 us (35%)
  blocking collectives  27.6 us (30%)
  starting transfers between devices  19.1 us (21%)
  Pallas kernels  10.1 us (11%)
  local copies, waits for them, and re-layouts  1.93 us (2%)
    all_to_all x2, blocking collectives, exchange_chips(): lax.all_to_all(block, 'feat', split_axis=0, concat_axis=0, tiled=True, ax...  27.6 us
    ppermute x14, waiting for transfers between devices, send_sample(): return lax.ppermute(block, 'sample', moves)  22.1 us
    ppermute x14, starting transfers between devices, send_sample(): return lax.ppermute(block, 'sample', moves)  15.5 us
    pallas_call x4, Pallas kernels, call(): pl.pallas_call(kernel, out_shape=outs, in_specs=[spec(arg.shape) for arg...  10.1 us
    all_to_all x1, waiting for transfers between devices, body(): lax.all_to_all(stats, 'sample', split_axis=0, concat_axis=0, tiled=True)  5.36 us
    ppermute x3, waiting for transfers between devices, swap_cores(): lax.ppermute(block, 'feat', [(i, i ^ 1) for i in range(lax.axis_size('fea...  4.14 us
    all_to_all x1, starting transfers between devices, body(): lax.all_to_all(stats, 'sample', split_axis=0, concat_axis=0, tiled=True)  3.38 us
    unnamed x4, local copies, waits for them, and re-layouts  1.9 us
  transfers between devices with their start and end apart: 18, of which 13 were waited for; matrix products, arithmetic and copies ran while one was open for 0% of the time, Pallas kernels for 0%

profile of v6, /device:TPU:0, one launch (start us, length us, event | category | flops | bytes accessed | tf_op | source)
XLA Modules:
  0.0 91.1 jit_solution(8795048221691827976)
XLA Ops:
  0.6 3.2 %collective-permute-start.2 = (bf16[128,1024]{1,0:T(8,128)(2,1)}, bf16[128,1024]{1,0:T(8,128)(2,1)S(1)}, u32[]{:S(2)}, u32[]{:S(2)}) collective-permute-start(bf16[128,1024]{1,0:T(8,128)(2,1)} %refs_1_.1), channel_id=1, source_target_pairs={{0,48},{16,0},{32,16},{48,32},{64,112},{80,64},{96,80},{112,96},{1... | collective-permute-start | bytes 786440 | tf_op jit(solution)/shard_map/ppermute | solution.py:27
  3.8 1.9 %collective-permute-start = (bf16[128,1024]{1,0:T(8,128)(2,1)}, bf16[128,1024]{1,0:T(8,128)(2,1)S(1)}, u32[]{:S(2)}, u32[]{:S(2)}) collective-permute-start(bf16[128,1024]{1,0:T(8,128)(2,1)} %refs_0_), channel_id=1, source_target_pairs={{0,64},{16,80},{32,96},{48,112},{64,0},{80,16},{96,32},{112,48},{1... | collective-permute-start | bytes 786440 | tf_op jit(solution)/shard_map/ppermute | solution.py:27
  5.7 0.0 collective-permute-start.1
  5.7 4.0 %collective-permute-done.2.refs_10_ = bf16[128,1024]{1,0:T(8,128)(2,1)S(1)} collective-permute-done((bf16[128,1024]{1,0:T(8,128)(2,1)}, bf16[128,1024]{1,0:T(8,128)(2,1)S(1)}, u32[]{:S(2)}, u32[]{:S(2)}) %collective-permute-start.2) | collective-permute-done | bytes 262176 | tf_op jit(solution)/shard_map/ppermute | solution.py:27
  9.7 1.9 %collective-permute-start.12 = (bf16[128,1024]{1,0:T(8,128)(2,1)S(1)}, bf16[128,1024]{1,0:T(8,128)(2,1)S(1)}, u32[]{:S(2)}, u32[]{:S(2)}) collective-permute-start(bf16[128,1024]{1,0:T(8,128)(2,1)S(1)} %collective-permute-done.2.refs_10_), channel_id=1, source_target_pairs={{0,64},{16,80},{32,96},{48,112},{64,0},{80,16},{96,32},{112,48},{1... | collective-permute-start | bytes 786440 | tf_op jit(solution)/shard_map/ppermute | solution.py:27
  11.6 0.8 collective-permute-done.refs_4_
  12.4 2.2 %collective-permute-done.1.refs_9_ = bf16[128,1024]{1,0:T(8,128)(2,1)S(1)} collective-permute-done((bf16[128,1024]{1,0:T(8,128)(2,1)}, bf16[128,1024]{1,0:T(8,128)(2,1)S(1)}, u32[]{:S(2)}, u32[]{:S(2)}) %collective-permute-start.1) | collective-permute-done | bytes 262176 | tf_op jit(solution)/shard_map/ppermute | solution.py:27
  14.6 0.6 collective-permute-start.4
  15.2 1.5 %collective-permute-start.3 = (bf16[128,1024]{1,0:T(8,128)(2,1)}, bf16[128,1024]{1,0:T(8,128)(2,1)S(1)}, u32[]{:S(2)}, u32[]{:S(2)}) collective-permute-start(bf16[128,1024]{1,0:T(8,128)(2,1)} %refs_0_), channel_id=1, source_target_pairs={{0,16},{16,32},{32,48},{48,0},{64,80},{80,96},{96,112},{112,64},{1... | collective-permute-start | bytes 786440 | tf_op jit(solution)/shard_map/ppermute | solution.py:27
  16.6 1.8 %collective-permute-start.7 = (bf16[128,1024]{1,0:T(8,128)(2,1)S(1)}, bf16[128,1024]{1,0:T(8,128)(2,1)S(1)}, u32[]{:S(2)}, u32[]{:S(2)}) collective-permute-start(bf16[128,1024]{1,0:T(8,128)(2,1)S(1)} %collective-permute-done.refs_4_), channel_id=1, source_target_pairs={{0,48},{16,0},{32,16},{48,32},{64,112},{80,64},{96,80},{112,96},{1... | collective-permute-start | bytes 786440 | tf_op jit(solution)/shard_map/ppermute | solution.py:27
  18.4 0.2 collective-permute-start.6
  18.7 0.0 collective-permute-done.12.refs_14_
  18.7 3.0 %collective-permute-start.9 = (bf16[128,1024]{1,0:T(8,128)(2,1)S(1)}, bf16[128,1024]{1,0:T(8,128)(2,1)S(1)}, u32[]{:S(2)}, u32[]{:S(2)}) collective-permute-start(bf16[128,1024]{1,0:T(8,128)(2,1)S(1)} %collective-permute-done.2.refs_10_), channel_id=1, source_target_pairs={{0,48},{16,0},{32,16},{48,32},{64,112},{80,64},{96,80},{112,96},{1... | collective-permute-start | bytes 786440 | tf_op jit(solution)/shard_map/ppermute | solution.py:27
  21.7 2.4 %collective-permute-done.4.refs_2_ = bf16[128,1024]{1,0:T(8,128)(2,1)S(1)} collective-permute-done((bf16[128,1024]{1,0:T(8,128)(2,1)}, bf16[128,1024]{1,0:T(8,128)(2,1)S(1)}, u32[]{:S(2)}, u32[]{:S(2)}) %collective-permute-start.4) | collective-permute-done | bytes 262176 | tf_op jit(solution)/shard_map/ppermute | solution.py:27
  24.1 0.3 collective-permute-start.10
  24.4 1.5 %collective-permute-done.3.refs_1_ = bf16[128,1024]{1,0:T(8,128)(2,1)S(1)} collective-permute-done((bf16[128,1024]{1,0:T(8,128)(2,1)}, bf16[128,1024]{1,0:T(8,128)(2,1)S(1)}, u32[]{:S(2)}, u32[]{:S(2)}) %collective-permute-start.3) | collective-permute-done | bytes 262176 | tf_op jit(solution)/shard_map/ppermute | solution.py:27
  25.9 0.3 collective-permute-start.11
  26.1 3.6 %collective-permute-done.7.refs_6_ = bf16[128,1024]{1,0:T(8,128)(2,1)S(1)} collective-permute-done((bf16[128,1024]{1,0:T(8,128)(2,1)S(1)}, bf16[128,1024]{1,0:T(8,128)(2,1)S(1)}, u32[]{:S(2)}, u32[]{:S(2)}) %collective-permute-start.7) | collective-permute-done | bytes 262176 | tf_op jit(solution)/shard_map/ppermute | solution.py:27
  29.7 0.0 collective-permute-start.5
  29.7 0.0 collective-permute-done.6.refs_5_
  29.7 0.4 collective-permute-start.8
  30.1 2.5 %collective-permute-done.9.refs_11_ = bf16[128,1024]{1,0:T(8,128)(2,1)S(1)} collective-permute-done((bf16[128,1024]{1,0:T(8,128)(2,1)S(1)}, bf16[128,1024]{1,0:T(8,128)(2,1)S(1)}, u32[]{:S(2)}, u32[]{:S(2)}) %collective-permute-start.9) | collective-permute-done | bytes 262176 | tf_op jit(solution)/shard_map/ppermute | solution.py:27
  32.6 0.5 collective-permute-start.13
  33.1 0.0 copy-start
  33.1 0.9 %copy-done = bf16[128,1024]{1,0:T(8,128)(2,1)S(1)} copy-done((bf16[128,1024]{1,0:T(8,128)(2,1)S(1)}, bf16[128,1024]{1,0:T(8,128)(2,1)}, u32[]{:S(2)}) %copy-start) | copy-done | bytes 262168
  34.0 0.0 copy-start.1
  34.0 0.9 %copy-done.1 = bf16[128,1024]{1,0:T(8,128)(2,1)S(1)} copy-done((bf16[128,1024]{1,0:T(8,128)(2,1)S(1)}, bf16[128,1024]{1,0:T(8,128)(2,1)}, u32[]{:S(2)}) %copy-start.1) | copy-done | bytes 262168
  35.0 0.0 collective-permute-done.10.refs_12_
  35.0 0.0 collective-permute-done.11.refs_13_
  35.0 2.2 %collective-permute-done.5.refs_3_ = bf16[128,1024]{1,0:T(8,128)(2,1)S(1)} collective-permute-done((bf16[128,1024]{1,0:T(8,128)(2,1)S(1)}, bf16[128,1024]{1,0:T(8,128)(2,1)S(1)}, u32[]{:S(2)}, u32[]{:S(2)}) %collective-permute-start.5) | collective-permute-done | bytes 262176 | tf_op jit(solution)/shard_map/ppermute | solution.py:27
  37.3 2.9 %collective-permute-done.8.refs_7_ = bf16[128,1024]{1,0:T(8,128)(2,1)} collective-permute-done((bf16[128,1024]{1,0:T(8,128)(2,1)S(1)}, bf16[128,1024]{1,0:T(8,128)(2,1)}, u32[]{:S(2)}, u32[]{:S(2)}) %collective-permute-start.8) | collective-permute-done | bytes 262176 | tf_op jit(solution)/shard_map/ppermute | solution.py:27
  40.2 0.0 collective-permute-done.13.refs_15_
  40.2 5.9 %shard_map.50 = (bf16[128,1024]{1,0:T(8,128)(2,1)S(1)}, bf16[128,1024]{1,0:T(8,128)(2,1)S(1)}, bf16[128,1024]{1,0:T(8,128)(2,1)S(1)}, bf16[128,1024]{1,0:T(8,128...) custom-call(s32[1]{0:T(128)} %bitcast.core, ...), custom_call_target="tpu_custom_call", output_to_operand_aliasing={{0}: (1, {}), {1}: (2, {}), {2}: (3, {}), {3}: (4, {}), {4}... | custom-call | tf_op jit(solution)/shard_map/pallas_call | solution.py:51
  46.1 0.0 collective-permute-start.14
  46.1 1.6 %collective-permute-done.14 = bf16[128,1152]{1,0:T(8,128)(2,1)S(1)} collective-permute-done((bf16[128,1152]{1,0:T(8,128)(2,1)S(1)}, bf16[128,1152]{1,0:T(8,128)(2,1)S(1)}, u32[]{:S(2)}, u32[]{:S(2)}) %collective-permute-start.14) | collective-permute-done | bytes 294944 | tf_op jit(solution)/shard_map/ppermute | solution.py:31
  47.7 0.1 add_convert_fusion
  47.7 16.7 %all_to_all.25 = bf16[8,16,1152]{2,1,0:T(8,128)(2,1)S(1)} all-to-all(bf16[8,16,1152]{2,1,0:T(8,128)(2,1)S(1)} %bitcast.8), channel_id=1, replica_groups={{0,2,4,6,8,10,12,14},{1,3,5,7,9,11,13,15},{16,18,20,22,24,26,28,30},{17..., dimensions={0} | all-to-all | bytes 589824 | tf_op jit(solution)/shard_map/all_to_all | solution.py:37
  64.5 10.9 %all_to_all.26 = bf16[8,16,1024]{2,1,0:T(8,128)(2,1)S(1)} all-to-all(bf16[8,16,1024]{2,1,0:T(8,128)(2,1)S(1)} %broadcast_in_dim.2), channel_id=1, replica_groups={{0,2,4,6,8,10,12,14},{1,3,5,7,9,11,13,15},{16,18,20,22,24,26,28,30},{17..., dimensions={0} | all-to-all | bytes 524288 | tf_op jit(solution)/shard_map/all_to_all | solution.py:37
  75.4 0.0 collective-permute-start.15
  75.4 1.5 %collective-permute-done.15.theirs = bf16[128,1024]{1,0:T(8,128)(2,1)S(1)} collective-permute-done((bf16[128,1024]{1,0:T(8,128)(2,1)S(1)}, bf16[128,1024]{1,0:T(8,128)(2,1)S(1)}, u32[]{:S(2)}, u32[]{:S(2)}) %collective-permute-start.15) | collective-permute-done | bytes 262176 | tf_op jit(solution)/shard_map/ppermute | solution.py:31
  76.9 2.9 %shard_map.51 = (bf16[128,1024]{1,0:T(8,128)(2,1)S(1)}, bf16[128,1024]{1,0:T(8,128)(2,1)S(1)}, bf16[128,1024]{1,0:T(8,128)(2,1)S(1)}, bf16[128,1024]{1,0:T(8,128)(2,1)S(1)}, f32[8,4,1152]{2,1,0:T(4,128)}) custom-call(s32[1]{0:T(128)} %bitcast.core, ...), custom_call_target="tpu_custom_call", output_to_operand_aliasing={{0}: (7, {}), {1}: (8, {}), {2}: (15, {}), {3}: (16, {})} | custom-call | tf_op jit(solution)/shard_map/pallas_call | solution.py:51
  79.8 3.4 %all-to-all-start.2 = ((f32[8,4,1152]{2,1,0:T(4,128)}), f32[8,4,1152]{2,1,0:T(4,128)S(1)}, u32[]{:S(2)}, u32[]{:S(2)}) async-start(f32[8,4,1152]{2,1,0:T(4,128)} %get-tuple-element.66), calls=%async_computation.2 | async-start | bytes 294912 | tf_op jit(solution)/shard_map/all_to_all | solution.py:294
  83.2 0.2 collective-permute-start.16
  83.4 1.0 %collective-permute-done.16.other = f32[8,128]{1,0:T(8,128)S(1)} collective-permute-done((f32[8,128]{1,0:T(8,128)S(1)}, f32[8,128]{1,0:T(8,128)S(1)}, u32[]{:S(2)}, u32[]{:S(2)}) %collective-permute-start.16) | collective-permute-done | bytes 4128 | tf_op jit(solution)/shard_map/ppermute | solution.py:31
  84.4 5.4 %all-to-all-done.2.stats = f32[8,4,1152]{2,1,0:T(4,128)S(1)} async-done(((f32[8,4,1152]{2,1,0:T(4,128)}), f32[8,4,1152]{2,1,0:T(4,128)S(1)}, u32[]{:S(2)}, u32[]{:S(2)}) %all-to-all-start.2) | async-done | bytes 147488 | tf_op jit(solution)/shard_map/all_to_all | solution.py:294
  89.8 1.3 %shard_map.52 = (bf16[128,1024]{1,0:T(8,128)(2,1)}, bf16[128,1024]{1,0:T(8,128)(2,1)}, f32[1]{0:T(128)}) custom-call(s32[1]{0:T(128)} %bitcast.core, f32[8,4,1152]{2,1,0:T(4,128)S(1)} %all-to-all-done.2.stats, bf16[128,1024]{1,0:T(8,128)(2,1)S(1)} %get-tuple-element.67.high_a, bf16[128,1024]{1,0:T(8,128)(2,1)S(1)} %get-tuple-element.68.low_a, ...), custom_call_target="tpu_custom_call" | custom-call | tf_op jit(solution)/shard_map/pallas_call | solution.py:51
  (5 shorter events, 0.1 us)
Async XLA Ops:
  0.6 9.0 %collective-permute-start.2 = (bf16[128,1024]{1,0:T(8,128)(2,1)}, bf16[128,1024]{1,0:T(8,128)(2,1)S(1)}, u32[]{:S(2)}, u32[]{:S(2)}) collective-permute-start(bf16[128,1024]{1,0:T(8,128)(2,1)} %refs_1_.1), channel_id=1, source_target_pairs={{0,48},{16,0},{32,16},{48,32},{64,112},{80,64},{96,80},{112,96},{1... | collective-permute-start | bytes 786440 | tf_op jit(solution)/shard_map/ppermute | solution.py:27
  3.8 8.6 %collective-permute-start = (bf16[128,1024]{1,0:T(8,128)(2,1)}, bf16[128,1024]{1,0:T(8,128)(2,1)S(1)}, u32[]{:S(2)}, u32[]{:S(2)}) collective-permute-start(bf16[128,1024]{1,0:T(8,128)(2,1)} %refs_0_), channel_id=1, source_target_pairs={{0,64},{16,80},{32,96},{48,112},{64,0},{80,16},{96,32},{112,48},{1... | collective-permute-start | bytes 786440 | tf_op jit(solution)/shard_map/ppermute | solution.py:27
  5.7 8.9 %collective-permute-start.1 = (bf16[128,1024]{1,0:T(8,128)(2,1)}, bf16[128,1024]{1,0:T(8,128)(2,1)S(1)}, u32[]{:S(2)}, u32[]{:S(2)}) collective-permute-start(bf16[128,1024]{1,0:T(8,128)(2,1)} %refs_1_.1), channel_id=1, source_target_pairs={{0,16},{16,32},{32,48},{48,0},{64,80},{80,96},{96,112},{112,64},{1... | collective-permute-start | bytes 786440 | tf_op jit(solution)/shard_map/ppermute | solution.py:27
  9.7 9.0 %collective-permute-start.12 = (bf16[128,1024]{1,0:T(8,128)(2,1)S(1)}, bf16[128,1024]{1,0:T(8,128)(2,1)S(1)}, u32[]{:S(2)}, u32[]{:S(2)}) collective-permute-start(bf16[128,1024]{1,0:T(8,128)(2,1)S(1)} %collective-permute-done.2.refs_10_), channel_id=1, source_target_pairs={{0,64},{16,80},{32,96},{48,112},{64,0},{80,16},{96,32},{112,48},{1... | collective-permute-start | bytes 786440 | tf_op jit(solution)/shard_map/ppermute | solution.py:27
  14.6 9.5 %collective-permute-start.4 = (bf16[128,1024]{1,0:T(8,128)(2,1)}, bf16[128,1024]{1,0:T(8,128)(2,1)S(1)}, u32[]{:S(2)}, u32[]{:S(2)}) collective-permute-start(bf16[128,1024]{1,0:T(8,128)(2,1)} %refs_0_), channel_id=1, source_target_pairs={{0,48},{16,0},{32,16},{48,32},{64,112},{80,64},{96,80},{112,96},{1... | collective-permute-start | bytes 786440 | tf_op jit(solution)/shard_map/ppermute | solution.py:27
  15.2 10.7 %collective-permute-start.3 = (bf16[128,1024]{1,0:T(8,128)(2,1)}, bf16[128,1024]{1,0:T(8,128)(2,1)S(1)}, u32[]{:S(2)}, u32[]{:S(2)}) collective-permute-start(bf16[128,1024]{1,0:T(8,128)(2,1)} %refs_0_), channel_id=1, source_target_pairs={{0,16},{16,32},{32,48},{48,0},{64,80},{80,96},{96,112},{112,64},{1... | collective-permute-start | bytes 786440 | tf_op jit(solution)/shard_map/ppermute | solution.py:27
  16.6 13.0 %collective-permute-start.7 = (bf16[128,1024]{1,0:T(8,128)(2,1)S(1)}, bf16[128,1024]{1,0:T(8,128)(2,1)S(1)}, u32[]{:S(2)}, u32[]{:S(2)}) collective-permute-start(bf16[128,1024]{1,0:T(8,128)(2,1)S(1)} %collective-permute-done.refs_4_), channel_id=1, source_target_pairs={{0,48},{16,0},{32,16},{48,32},{64,112},{80,64},{96,80},{112,96},{1... | collective-permute-start | bytes 786440 | tf_op jit(solution)/shard_map/ppermute | solution.py:27
  18.4 11.3 %collective-permute-start.6 = (bf16[128,1024]{1,0:T(8,128)(2,1)S(1)}, bf16[128,1024]{1,0:T(8,128)(2,1)S(1)}, u32[]{:S(2)}, u32[]{:S(2)}) collective-permute-start(bf16[128,1024]{1,0:T(8,128)(2,1)S(1)} %collective-permute-done.refs_4_), channel_id=1, source_target_pairs={{0,16},{16,32},{32,48},{48,0},{64,80},{80,96},{96,112},{112,64},{1... | collective-permute-start | bytes 786440 | tf_op jit(solution)/shard_map/ppermute | solution.py:27
  18.7 13.9 %collective-permute-start.9 = (bf16[128,1024]{1,0:T(8,128)(2,1)S(1)}, bf16[128,1024]{1,0:T(8,128)(2,1)S(1)}, u32[]{:S(2)}, u32[]{:S(2)}) collective-permute-start(bf16[128,1024]{1,0:T(8,128)(2,1)S(1)} %collective-permute-done.2.refs_10_), channel_id=1, source_target_pairs={{0,48},{16,0},{32,16},{48,32},{64,112},{80,64},{96,80},{112,96},{1... | collective-permute-start | bytes 786440 | tf_op jit(solution)/shard_map/ppermute | solution.py:27
  24.1 11.0 %collective-permute-start.10 = (bf16[128,1024]{1,0:T(8,128)(2,1)}, bf16[128,1024]{1,0:T(8,128)(2,1)S(1)}, u32[]{:S(2)}, u32[]{:S(2)}) collective-permute-start(bf16[128,1024]{1,0:T(8,128)(2,1)} %refs_1_.1), channel_id=1, source_target_pairs={{0,64},{16,80},{32,96},{48,112},{64,0},{80,16},{96,32},{112,48},{1... | collective-permute-start | bytes 786440 | tf_op jit(solution)/shard_map/ppermute | solution.py:27
  25.9 9.2 %collective-permute-start.11 = (bf16[128,1024]{1,0:T(8,128)(2,1)S(1)}, bf16[128,1024]{1,0:T(8,128)(2,1)}, u32[]{:S(2)}, u32[]{:S(2)}) collective-permute-start(bf16[128,1024]{1,0:T(8,128)(2,1)S(1)} %collective-permute-done.1.refs_9_), channel_id=1, source_target_pairs={{0,64},{16,80},{32,96},{48,112},{64,0},{80,16},{96,32},{112,48},{1... | collective-permute-start | bytes 786440 | tf_op jit(solution)/shard_map/ppermute | solution.py:27
  29.7 7.6 %collective-permute-start.5 = (bf16[128,1024]{1,0:T(8,128)(2,1)S(1)}, bf16[128,1024]{1,0:T(8,128)(2,1)S(1)}, u32[]{:S(2)}, u32[]{:S(2)}) collective-permute-start(bf16[128,1024]{1,0:T(8,128)(2,1)S(1)} %collective-permute-done.3.refs_1_), channel_id=1, source_target_pairs={{0,16},{16,32},{32,48},{48,0},{64,80},{80,96},{96,112},{112,64},{1... | collective-permute-start | bytes 786440 | tf_op jit(solution)/shard_map/ppermute | solution.py:27
  29.7 10.5 %collective-permute-start.8 = (bf16[128,1024]{1,0:T(8,128)(2,1)S(1)}, bf16[128,1024]{1,0:T(8,128)(2,1)}, u32[]{:S(2)}, u32[]{:S(2)}) collective-permute-start(bf16[128,1024]{1,0:T(8,128)(2,1)S(1)} %collective-permute-done.6.refs_5_), channel_id=1, source_target_pairs={{0,16},{16,32},{32,48},{48,0},{64,80},{80,96},{96,112},{112,64},{1... | collective-permute-start | bytes 786440 | tf_op jit(solution)/shard_map/ppermute | solution.py:27
  32.6 7.6 %collective-permute-start.13 = (bf16[128,1024]{1,0:T(8,128)(2,1)S(1)}, bf16[128,1024]{1,0:T(8,128)(2,1)}, u32[]{:S(2)}, u32[]{:S(2)}) collective-permute-start(bf16[128,1024]{1,0:T(8,128)(2,1)S(1)} %collective-permute-done.9.refs_11_), channel_id=1, source_target_pairs={{0,64},{16,80},{32,96},{48,112},{64,0},{80,16},{96,32},{112,48},{1... | collective-permute-start | bytes 786440 | tf_op jit(solution)/shard_map/ppermute | solution.py:27
  33.1 0.9 %copy-start = (bf16[128,1024]{1,0:T(8,128)(2,1)S(1)}, bf16[128,1024]{1,0:T(8,128)(2,1)}, u32[]{:S(2)}) copy-start(bf16[128,1024]{1,0:T(8,128)(2,1)} %refs_0_) | copy-start | bytes 786436
  34.0 0.9 %copy-start.1 = (bf16[128,1024]{1,0:T(8,128)(2,1)S(1)}, bf16[128,1024]{1,0:T(8,128)(2,1)}, u32[]{:S(2)}) copy-start(bf16[128,1024]{1,0:T(8,128)(2,1)} %refs_1_.1) | copy-start | bytes 786436
  46.1 1.6 %collective-permute-start.14 = (bf16[128,1152]{1,0:T(8,128)(2,1)S(1)}, bf16[128,1152]{1,0:T(8,128)(2,1)S(1)}, u32[]{:S(2)}, u32[]{:S(2)}) collective-permute-start(bf16[128,1152]{1,0:T(8,128)(2,1)S(1)} %get-tuple-element.47), channel_id=1, source_target_pairs={{0,1},{1,0},{2,3},{3,2},{4,5},{5,4},{6,7},{7,6},{8,9},{9,8},{10,11... | collective-permute-start | bytes 884744 | tf_op jit(solution)/shard_map/ppermute | solution.py:31
  75.4 1.5 %collective-permute-start.15 = (bf16[128,1024]{1,0:T(8,128)(2,1)S(1)}, bf16[128,1024]{1,0:T(8,128)(2,1)S(1)}, u32[]{:S(2)}, u32[]{:S(2)}) collective-permute-start(bf16[128,1024]{1,0:T(8,128)(2,1)S(1)} %bitcast.6), channel_id=1, source_target_pairs={{0,1},{1,0},{2,3},{3,2},{4,5},{5,4},{6,7},{7,6},{8,9},{9,8},{10,11... | collective-permute-start | bytes 786440 | tf_op jit(solution)/shard_map/ppermute | solution.py:31
  79.8 10.0 %all-to-all-start.2 = ((f32[8,4,1152]{2,1,0:T(4,128)}), f32[8,4,1152]{2,1,0:T(4,128)S(1)}, u32[]{:S(2)}, u32[]{:S(2)}) async-start(f32[8,4,1152]{2,1,0:T(4,128)} %get-tuple-element.66), calls=%async_computation.2 | async-start | bytes 294912 | tf_op jit(solution)/shard_map/all_to_all | solution.py:294
  83.2 1.2 %collective-permute-start.16 = (f32[8,128]{1,0:T(8,128)S(1)}, f32[8,128]{1,0:T(8,128)S(1)}, u32[]{:S(2)}, u32[]{:S(2)}) collective-permute-start(f32[8,128]{1,0:T(8,128)S(1)} %slice.10.split), channel_id=1, source_target_pairs={{0,1},{1,0},{2,3},{3,2},{4,5},{5,4},{6,7},{7,6},{8,9},{9,8},{10,11... | collective-permute-start | bytes 12296 | tf_op jit(solution)/shard_map/ppermute | solution.py:31

commit v7 on v6

--- a/solution.py
+++ b/solution.py
@@ -121,26 +121,44 @@
     rows, total_rows = part_a.shape
     inv_rows = 1.0 / total_rows
 
-    def view(where, part, columns, first_step):
-        floats = jnp.concatenate([blocks[i][pl.ds(first, rows), columns] for i, first in where])
-        floats = floats.astype(F32)
-        mean = jnp.sum(floats, axis=0, keepdims=True) * inv_rows
-        square = jnp.sum(floats * floats, axis=0, keepdims=True) * inv_rows
-        scale = lax.rsqrt(square - mean * mean + EPSILON)
+    def fold(values):
+        return jnp.sum(values.reshape(-1, 8, values.shape[1]), axis=0)
+
+    def moments(where, columns):
+        total = jnp.zeros((8, CHUNK), F32)
+        square = jnp.zeros((8, CHUNK), F32)
+        for i, first in where:
+            floats = blocks[i][pl.ds(first, rows), columns].astype(F32)
+            total += fold(floats)
+            square += fold(floats * floats)
+        mean = jnp.sum(total, axis=0, keepdims=True) * inv_rows
+        square = jnp.sum(square, axis=0, keepdims=True) * inv_rows
+        return mean, lax.rsqrt(square - mean * mean + EPSILON)
+
+    def normal(i, first, columns, mean, scale):
+        floats = blocks[i][pl.ds(first, rows), columns].astype(F32)
         norm = ((floats - mean) * scale).astype(BF16)
-        for place, (i, first) in enumerate(where):
-            norms[i][pl.ds(first, rows), columns] = norm[place * rows : (place + 1) * rows]
-        more = lax.dot_general(
-            norm[:rows], norm, (((1,), (1,)), ((), ())), preferred_element_type=F32
-        )
-        part[...] = more if first_step else part[...] + more
-        return norm, scale
-
+        norms[i][pl.ds(first, rows), columns] = norm
+        return norm
+
+    contract = (((1,), (1,)), ((), ()))
     loss = jnp.zeros((1, CHUNK), F32)
     for step, columns in enumerate(column_steps(cols)):
-        norm_a, scale_a = view(where_a, part_a, columns, step == 0)
-        norm_b, scale_b = view(where_b, part_b, columns, step == 0)
-        diag = jnp.sum(norm_a.astype(F32) * norm_b.astype(F32), axis=0, keepdims=True) * inv_rows
+        mean_a, scale_a = moments(where_a, columns)
+        mean_b, scale_b = moments(where_b, columns)
+        diag = jnp.zeros((8, CHUNK), F32)
+        for place in range(len(where_a)):
+            norm_a = normal(*where_a[place], columns, mean_a, scale_a)
+            norm_b = normal(*where_b[place], columns, mean_b, scale_b)
+            diag += fold(norm_a.astype(F32) * norm_b.astype(F32))
+            if place == 0:
+                own_a, own_b = norm_a, norm_b
+            part = pl.ds(place * rows, rows)
+            more_a = lax.dot_general(own_a, norm_a, contract, preferred_element_type=F32)
+            more_b = lax.dot_general(own_b, norm_b, contract, preferred_element_type=F32)
+            part_a[:, part] = more_a if step == 0 else part_a[:, part] + more_a
+            part_b[:, part] = more_b if step == 0 else part_b[:, part] + more_b
+        diag = jnp.sum(diag, axis=0, keepdims=True) * inv_rows
         loss += (1.0 - diag) * (1.0 - diag) - OFF_WEIGHT * diag * diag
         slope = (diag - 1.0) - OFF_WEIGHT * diag
         vecs[:, columns] = jnp.concatenate([scale_a, scale_b, slope, jnp.zeros((5, CHUNK), F32)])

time: 91.5 us -> 90.8 us (level)
  no operation moved by 1% of the time
where the time goes in v7:
time: 90.8 us; the launch traced here: 90.4 us
  waiting for transfers between devices  31.6 us (35%)
  blocking collectives  27.6 us (30%)
  starting transfers between devices  19.1 us (21%)
  Pallas kernels  9.42 us (10%)
  local copies, waits for them, and re-layouts  1.93 us (2%)
    all_to_all x2, blocking collectives, exchange_chips(): lax.all_to_all(block, 'feat', split_axis=0, concat_axis=0, tiled=True, ax...  27.6 us
    ppermute x14, waiting for transfers between devices, send_sample(): return lax.ppermute(block, 'sample', moves)  22.1 us
    ppermute x14, starting transfers between devices, send_sample(): return lax.ppermute(block, 'sample', moves)  15.5 us
    pallas_call x4, Pallas kernels, call(): pl.pallas_call(kernel, out_shape=outs, in_specs=[spec(arg.shape) for arg...  9.42 us
    all_to_all x1, waiting for transfers between devices, body(): lax.all_to_all(stats, 'sample', split_axis=0, concat_axis=0, tiled=True)  5.36 us
    ppermute x3, waiting for transfers between devices, swap_cores(): lax.ppermute(block, 'feat', [(i, i ^ 1) for i in range(lax.axis_size('fea...  4.15 us
    all_to_all x1, starting transfers between devices, body(): lax.all_to_all(stats, 'sample', split_axis=0, concat_axis=0, tiled=True)  3.38 us
    unnamed x4, local copies, waits for them, and re-layouts  1.9 us
  transfers between devices with their start and end apart: 18, of which 13 were waited for; matrix products, arithmetic and copies ran while one was open for 0% of the time, Pallas kernels for 0%

profile of v7, /device:TPU:0, one launch (start us, length us, event | category | flops | bytes accessed | tf_op | source)
XLA Modules:
  0.0 90.4 jit_solution(4575749644129433089)
XLA Ops:
  0.6 3.2 %collective-permute-start.2 = (bf16[128,1024]{1,0:T(8,128)(2,1)}, bf16[128,1024]{1,0:T(8,128)(2,1)S(1)}, u32[]{:S(2)}, u32[]{:S(2)}) collective-permute-start(bf16[128,1024]{1,0:T(8,128)(2,1)} %refs_1_.1), channel_id=1, source_target_pairs={{0,48},{16,0},{32,16},{48,32},{64,112},{80,64},{96,80},{112,96},{1... | collective-permute-start | bytes 786440 | tf_op jit(solution)/shard_map/ppermute | solution.py:27
  3.8 1.9 %collective-permute-start = (bf16[128,1024]{1,0:T(8,128)(2,1)}, bf16[128,1024]{1,0:T(8,128)(2,1)S(1)}, u32[]{:S(2)}, u32[]{:S(2)}) collective-permute-start(bf16[128,1024]{1,0:T(8,128)(2,1)} %refs_0_), channel_id=1, source_target_pairs={{0,64},{16,80},{32,96},{48,112},{64,0},{80,16},{96,32},{112,48},{1... | collective-permute-start | bytes 786440 | tf_op jit(solution)/shard_map/ppermute | solution.py:27
  5.7 0.0 collective-permute-start.1
  5.7 4.0 %collective-permute-done.2.refs_10_ = bf16[128,1024]{1,0:T(8,128)(2,1)S(1)} collective-permute-done((bf16[128,1024]{1,0:T(8,128)(2,1)}, bf16[128,1024]{1,0:T(8,128)(2,1)S(1)}, u32[]{:S(2)}, u32[]{:S(2)}) %collective-permute-start.2) | collective-permute-done | bytes 262176 | tf_op jit(solution)/shard_map/ppermute | solution.py:27
  9.7 1.9 %collective-permute-start.12 = (bf16[128,1024]{1,0:T(8,128)(2,1)S(1)}, bf16[128,1024]{1,0:T(8,128)(2,1)S(1)}, u32[]{:S(2)}, u32[]{:S(2)}) collective-permute-start(bf16[128,1024]{1,0:T(8,128)(2,1)S(1)} %collective-permute-done.2.refs_10_), channel_id=1, source_target_pairs={{0,64},{16,80},{32,96},{48,112},{64,0},{80,16},{96,32},{112,48},{1... | collective-permute-start | bytes 786440 | tf_op jit(solution)/shard_map/ppermute | solution.py:27
  11.6 0.8 collective-permute-done.refs_4_
  12.4 2.2 %collective-permute-done.1.refs_9_ = bf16[128,1024]{1,0:T(8,128)(2,1)S(1)} collective-permute-done((bf16[128,1024]{1,0:T(8,128)(2,1)}, bf16[128,1024]{1,0:T(8,128)(2,1)S(1)}, u32[]{:S(2)}, u32[]{:S(2)}) %collective-permute-start.1) | collective-permute-done | bytes 262176 | tf_op jit(solution)/shard_map/ppermute | solution.py:27
  14.6 0.6 collective-permute-start.4
  15.2 1.5 %collective-permute-start.3 = (bf16[128,1024]{1,0:T(8,128)(2,1)}, bf16[128,1024]{1,0:T(8,128)(2,1)S(1)}, u32[]{:S(2)}, u32[]{:S(2)}) collective-permute-start(bf16[128,1024]{1,0:T(8,128)(2,1)} %refs_0_), channel_id=1, source_target_pairs={{0,16},{16,32},{32,48},{48,0},{64,80},{80,96},{96,112},{112,64},{1... | collective-permute-start | bytes 786440 | tf_op jit(solution)/shard_map/ppermute | solution.py:27
  16.6 1.8 %collective-permute-start.7 = (bf16[128,1024]{1,0:T(8,128)(2,1)S(1)}, bf16[128,1024]{1,0:T(8,128)(2,1)S(1)}, u32[]{:S(2)}, u32[]{:S(2)}) collective-permute-start(bf16[128,1024]{1,0:T(8,128)(2,1)S(1)} %collective-permute-done.refs_4_), channel_id=1, source_target_pairs={{0,48},{16,0},{32,16},{48,32},{64,112},{80,64},{96,80},{112,96},{1... | collective-permute-start | bytes 786440 | tf_op jit(solution)/shard_map/ppermute | solution.py:27
  18.4 0.2 collective-permute-start.6
  18.7 0.0 collective-permute-done.12.refs_14_
  18.7 3.0 %collective-permute-start.9 = (bf16[128,1024]{1,0:T(8,128)(2,1)S(1)}, bf16[128,1024]{1,0:T(8,128)(2,1)S(1)}, u32[]{:S(2)}, u32[]{:S(2)}) collective-permute-start(bf16[128,1024]{1,0:T(8,128)(2,1)S(1)} %collective-permute-done.2.refs_10_), channel_id=1, source_target_pairs={{0,48},{16,0},{32,16},{48,32},{64,112},{80,64},{96,80},{112,96},{1... | collective-permute-start | bytes 786440 | tf_op jit(solution)/shard_map/ppermute | solution.py:27
  21.7 2.4 %collective-permute-done.4.refs_2_ = bf16[128,1024]{1,0:T(8,128)(2,1)S(1)} collective-permute-done((bf16[128,1024]{1,0:T(8,128)(2,1)}, bf16[128,1024]{1,0:T(8,128)(2,1)S(1)}, u32[]{:S(2)}, u32[]{:S(2)}) %collective-permute-start.4) | collective-permute-done | bytes 262176 | tf_op jit(solution)/shard_map/ppermute | solution.py:27
  24.1 0.3 collective-permute-start.10
  24.4 1.5 %collective-permute-done.3.refs_1_ = bf16[128,1024]{1,0:T(8,128)(2,1)S(1)} collective-permute-done((bf16[128,1024]{1,0:T(8,128)(2,1)}, bf16[128,1024]{1,0:T(8,128)(2,1)S(1)}, u32[]{:S(2)}, u32[]{:S(2)}) %collective-permute-start.3) | collective-permute-done | bytes 262176 | tf_op jit(solution)/shard_map/ppermute | solution.py:27
  25.9 0.3 collective-permute-start.11
  26.1 3.6 %collective-permute-done.7.refs_6_ = bf16[128,1024]{1,0:T(8,128)(2,1)S(1)} collective-permute-done((bf16[128,1024]{1,0:T(8,128)(2,1)S(1)}, bf16[128,1024]{1,0:T(8,128)(2,1)S(1)}, u32[]{:S(2)}, u32[]{:S(2)}) %collective-permute-start.7) | collective-permute-done | bytes 262176 | tf_op jit(solution)/shard_map/ppermute | solution.py:27
  29.7 0.0 collective-permute-start.5
  29.7 0.0 collective-permute-done.6.refs_5_
  29.7 0.4 collective-permute-start.8
  30.1 2.5 %collective-permute-done.9.refs_11_ = bf16[128,1024]{1,0:T(8,128)(2,1)S(1)} collective-permute-done((bf16[128,1024]{1,0:T(8,128)(2,1)S(1)}, bf16[128,1024]{1,0:T(8,128)(2,1)S(1)}, u32[]{:S(2)}, u32[]{:S(2)}) %collective-permute-start.9) | collective-permute-done | bytes 262176 | tf_op jit(solution)/shard_map/ppermute | solution.py:27
  32.6 0.5 collective-permute-start.13
  33.1 0.0 copy-start
  33.1 0.9 %copy-done = bf16[128,1024]{1,0:T(8,128)(2,1)S(1)} copy-done((bf16[128,1024]{1,0:T(8,128)(2,1)S(1)}, bf16[128,1024]{1,0:T(8,128)(2,1)}, u32[]{:S(2)}) %copy-start) | copy-done | bytes 262168
  34.0 0.0 copy-start.1
  34.0 0.9 %copy-done.1 = bf16[128,1024]{1,0:T(8,128)(2,1)S(1)} copy-done((bf16[128,1024]{1,0:T(8,128)(2,1)S(1)}, bf16[128,1024]{1,0:T(8,128)(2,1)}, u32[]{:S(2)}) %copy-start.1) | copy-done | bytes 262168
  35.0 0.0 collective-permute-done.10.refs_12_
  35.0 0.0 collective-permute-done.11.refs_13_
  35.0 2.2 %collective-permute-done.5.refs_3_ = bf16[128,1024]{1,0:T(8,128)(2,1)S(1)} collective-permute-done((bf16[128,1024]{1,0:T(8,128)(2,1)S(1)}, bf16[128,1024]{1,0:T(8,128)(2,1)S(1)}, u32[]{:S(2)}, u32[]{:S(2)}) %collective-permute-start.5) | collective-permute-done | bytes 262176 | tf_op jit(solution)/shard_map/ppermute | solution.py:27
  37.3 2.9 %collective-permute-done.8.refs_7_ = bf16[128,1024]{1,0:T(8,128)(2,1)} collective-permute-done((bf16[128,1024]{1,0:T(8,128)(2,1)S(1)}, bf16[128,1024]{1,0:T(8,128)(2,1)}, u32[]{:S(2)}, u32[]{:S(2)}) %collective-permute-start.8) | collective-permute-done | bytes 262176 | tf_op jit(solution)/shard_map/ppermute | solution.py:27
  40.2 0.0 collective-permute-done.13.refs_15_
  40.2 5.2 %shard_map.50 = (bf16[128,1024]{1,0:T(8,128)(2,1)S(1)}, bf16[128,1024]{1,0:T(8,128)(2,1)S(1)}, bf16[128,1024]{1,0:T(8,128)(2,1)S(1)}, bf16[128,1024]{1,0:T(8,128...) custom-call(s32[1]{0:T(128)} %bitcast.core, ...), custom_call_target="tpu_custom_call", output_to_operand_aliasing={{0}: (1, {}), {1}: (2, {}), {2}: (3, {}), {3}: (4, {}), {4}... | custom-call | tf_op jit(solution)/shard_map/pallas_call | solution.py:51
  45.4 0.0 collective-permute-start.14
  45.4 1.6 %collective-permute-done.14 = bf16[128,1152]{1,0:T(8,128)(2,1)S(1)} collective-permute-done((bf16[128,1152]{1,0:T(8,128)(2,1)S(1)}, bf16[128,1152]{1,0:T(8,128)(2,1)S(1)}, u32[]{:S(2)}, u32[]{:S(2)}) %collective-permute-start.14) | collective-permute-done | bytes 294944 | tf_op jit(solution)/shard_map/ppermute | solution.py:31
  47.0 0.1 add_convert_fusion
  47.0 16.7 %all_to_all.25 = bf16[8,16,1152]{2,1,0:T(8,128)(2,1)S(1)} all-to-all(bf16[8,16,1152]{2,1,0:T(8,128)(2,1)S(1)} %bitcast.8), channel_id=1, replica_groups={{0,2,4,6,8,10,12,14},{1,3,5,7,9,11,13,15},{16,18,20,22,24,26,28,30},{17..., dimensions={0} | all-to-all | bytes 589824 | tf_op jit(solution)/shard_map/all_to_all | solution.py:37
  63.8 10.9 %all_to_all.26 = bf16[8,16,1024]{2,1,0:T(8,128)(2,1)S(1)} all-to-all(bf16[8,16,1024]{2,1,0:T(8,128)(2,1)S(1)} %broadcast_in_dim.2), channel_id=1, replica_groups={{0,2,4,6,8,10,12,14},{1,3,5,7,9,11,13,15},{16,18,20,22,24,26,28,30},{17..., dimensions={0} | all-to-all | bytes 524288 | tf_op jit(solution)/shard_map/all_to_all | solution.py:37
  74.7 0.0 collective-permute-start.15
  74.7 1.5 %collective-permute-done.15.theirs = bf16[128,1024]{1,0:T(8,128)(2,1)S(1)} collective-permute-done((bf16[128,1024]{1,0:T(8,128)(2,1)S(1)}, bf16[128,1024]{1,0:T(8,128)(2,1)S(1)}, u32[]{:S(2)}, u32[]{:S(2)}) %collective-permute-start.15) | collective-permute-done | bytes 262176 | tf_op jit(solution)/shard_map/ppermute | solution.py:31
  76.2 2.9 %shard_map.51 = (bf16[128,1024]{1,0:T(8,128)(2,1)S(1)}, bf16[128,1024]{1,0:T(8,128)(2,1)S(1)}, bf16[128,1024]{1,0:T(8,128)(2,1)S(1)}, bf16[128,1024]{1,0:T(8,128)(2,1)S(1)}, f32[8,4,1152]{2,1,0:T(4,128)}) custom-call(s32[1]{0:T(128)} %bitcast.core, ...), custom_call_target="tpu_custom_call", output_to_operand_aliasing={{0}: (7, {}), {1}: (8, {}), {2}: (15, {}), {3}: (16, {})} | custom-call | tf_op jit(solution)/shard_map/pallas_call | solution.py:51
  79.1 3.4 %all-to-all-start.2 = ((f32[8,4,1152]{2,1,0:T(4,128)}), f32[8,4,1152]{2,1,0:T(4,128)S(1)}, u32[]{:S(2)}, u32[]{:S(2)}) async-start(f32[8,4,1152]{2,1,0:T(4,128)} %get-tuple-element.66), calls=%async_computation.2 | async-start | bytes 294912 | tf_op jit(solution)/shard_map/all_to_all | solution.py:312
  82.5 0.2 collective-permute-start.16
  82.7 1.0 %collective-permute-done.16.other = f32[8,128]{1,0:T(8,128)S(1)} collective-permute-done((f32[8,128]{1,0:T(8,128)S(1)}, f32[8,128]{1,0:T(8,128)S(1)}, u32[]{:S(2)}, u32[]{:S(2)}) %collective-permute-start.16) | collective-permute-done | bytes 4128 | tf_op jit(solution)/shard_map/ppermute | solution.py:31
  83.7 5.4 %all-to-all-done.2.stats = f32[8,4,1152]{2,1,0:T(4,128)S(1)} async-done(((f32[8,4,1152]{2,1,0:T(4,128)}), f32[8,4,1152]{2,1,0:T(4,128)S(1)}, u32[]{:S(2)}, u32[]{:S(2)}) %all-to-all-start.2) | async-done | bytes 147488 | tf_op jit(solution)/shard_map/all_to_all | solution.py:312
  89.1 1.3 %shard_map.52 = (bf16[128,1024]{1,0:T(8,128)(2,1)}, bf16[128,1024]{1,0:T(8,128)(2,1)}, f32[1]{0:T(128)}) custom-call(s32[1]{0:T(128)} %bitcast.core, f32[8,4,1152]{2,1,0:T(4,128)S(1)} %all-to-all-done.2.stats, bf16[128,1024]{1,0:T(8,128)(2,1)S(1)} %get-tuple-element.67.high_a, bf16[128,1024]{1,0:T(8,128)(2,1)S(1)} %get-tuple-element.68.low_a, ...), custom_call_target="tpu_custom_call" | custom-call | tf_op jit(solution)/shard_map/pallas_call | solution.py:51
  (5 shorter events, 0.1 us)
Async XLA Ops:
  0.6 9.0 %collective-permute-start.2 = (bf16[128,1024]{1,0:T(8,128)(2,1)}, bf16[128,1024]{1,0:T(8,128)(2,1)S(1)}, u32[]{:S(2)}, u32[]{:S(2)}) collective-permute-start(bf16[128,1024]{1,0:T(8,128)(2,1)} %refs_1_.1), channel_id=1, source_target_pairs={{0,48},{16,0},{32,16},{48,32},{64,112},{80,64},{96,80},{112,96},{1... | collective-permute-start | bytes 786440 | tf_op jit(solution)/shard_map/ppermute | solution.py:27
  3.8 8.6 %collective-permute-start = (bf16[128,1024]{1,0:T(8,128)(2,1)}, bf16[128,1024]{1,0:T(8,128)(2,1)S(1)}, u32[]{:S(2)}, u32[]{:S(2)}) collective-permute-start(bf16[128,1024]{1,0:T(8,128)(2,1)} %refs_0_), channel_id=1, source_target_pairs={{0,64},{16,80},{32,96},{48,112},{64,0},{80,16},{96,32},{112,48},{1... | collective-permute-start | bytes 786440 | tf_op jit(solution)/shard_map/ppermute | solution.py:27
  5.7 8.9 %collective-permute-start.1 = (bf16[128,1024]{1,0:T(8,128)(2,1)}, bf16[128,1024]{1,0:T(8,128)(2,1)S(1)}, u32[]{:S(2)}, u32[]{:S(2)}) collective-permute-start(bf16[128,1024]{1,0:T(8,128)(2,1)} %refs_1_.1), channel_id=1, source_target_pairs={{0,16},{16,32},{32,48},{48,0},{64,80},{80,96},{96,112},{112,64},{1... | collective-permute-start | bytes 786440 | tf_op jit(solution)/shard_map/ppermute | solution.py:27
  9.7 9.0 %collective-permute-start.12 = (bf16[128,1024]{1,0:T(8,128)(2,1)S(1)}, bf16[128,1024]{1,0:T(8,128)(2,1)S(1)}, u32[]{:S(2)}, u32[]{:S(2)}) collective-permute-start(bf16[128,1024]{1,0:T(8,128)(2,1)S(1)} %collective-permute-done.2.refs_10_), channel_id=1, source_target_pairs={{0,64},{16,80},{32,96},{48,112},{64,0},{80,16},{96,32},{112,48},{1... | collective-permute-start | bytes 786440 | tf_op jit(solution)/shard_map/ppermute | solution.py:27
  14.6 9.5 %collective-permute-start.4 = (bf16[128,1024]{1,0:T(8,128)(2,1)}, bf16[128,1024]{1,0:T(8,128)(2,1)S(1)}, u32[]{:S(2)}, u32[]{:S(2)}) collective-permute-start(bf16[128,1024]{1,0:T(8,128)(2,1)} %refs_0_), channel_id=1, source_target_pairs={{0,48},{16,0},{32,16},{48,32},{64,112},{80,64},{96,80},{112,96},{1... | collective-permute-start | bytes 786440 | tf_op jit(solution)/shard_map/ppermute | solution.py:27
  15.2 10.7 %collective-permute-start.3 = (bf16[128,1024]{1,0:T(8,128)(2,1)}, bf16[128,1024]{1,0:T(8,128)(2,1)S(1)}, u32[]{:S(2)}, u32[]{:S(2)}) collective-permute-start(bf16[128,1024]{1,0:T(8,128)(2,1)} %refs_0_), channel_id=1, source_target_pairs={{0,16},{16,32},{32,48},{48,0},{64,80},{80,96},{96,112},{112,64},{1... | collective-permute-start | bytes 786440 | tf_op jit(solution)/shard_map/ppermute | solution.py:27
  16.6 13.0 %collective-permute-start.7 = (bf16[128,1024]{1,0:T(8,128)(2,1)S(1)}, bf16[128,1024]{1,0:T(8,128)(2,1)S(1)}, u32[]{:S(2)}, u32[]{:S(2)}) collective-permute-start(bf16[128,1024]{1,0:T(8,128)(2,1)S(1)} %collective-permute-done.refs_4_), channel_id=1, source_target_pairs={{0,48},{16,0},{32,16},{48,32},{64,112},{80,64},{96,80},{112,96},{1... | collective-permute-start | bytes 786440 | tf_op jit(solution)/shard_map/ppermute | solution.py:27
  18.4 11.3 %collective-permute-start.6 = (bf16[128,1024]{1,0:T(8,128)(2,1)S(1)}, bf16[128,1024]{1,0:T(8,128)(2,1)S(1)}, u32[]{:S(2)}, u32[]{:S(2)}) collective-permute-start(bf16[128,1024]{1,0:T(8,128)(2,1)S(1)} %collective-permute-done.refs_4_), channel_id=1, source_target_pairs={{0,16},{16,32},{32,48},{48,0},{64,80},{80,96},{96,112},{112,64},{1... | collective-permute-start | bytes 786440 | tf_op jit(solution)/shard_map/ppermute | solution.py:27
  18.7 13.9 %collective-permute-start.9 = (bf16[128,1024]{1,0:T(8,128)(2,1)S(1)}, bf16[128,1024]{1,0:T(8,128)(2,1)S(1)}, u32[]{:S(2)}, u32[]{:S(2)}) collective-permute-start(bf16[128,1024]{1,0:T(8,128)(2,1)S(1)} %collective-permute-done.2.refs_10_), channel_id=1, source_target_pairs={{0,48},{16,0},{32,16},{48,32},{64,112},{80,64},{96,80},{112,96},{1... | collective-permute-start | bytes 786440 | tf_op jit(solution)/shard_map/ppermute | solution.py:27
  24.1 11.0 %collective-permute-start.10 = (bf16[128,1024]{1,0:T(8,128)(2,1)}, bf16[128,1024]{1,0:T(8,128)(2,1)S(1)}, u32[]{:S(2)}, u32[]{:S(2)}) collective-permute-start(bf16[128,1024]{1,0:T(8,128)(2,1)} %refs_1_.1), channel_id=1, source_target_pairs={{0,64},{16,80},{32,96},{48,112},{64,0},{80,16},{96,32},{112,48},{1... | collective-permute-start | bytes 786440 | tf_op jit(solution)/shard_map/ppermute | solution.py:27
  25.9 9.2 %collective-permute-start.11 = (bf16[128,1024]{1,0:T(8,128)(2,1)S(1)}, bf16[128,1024]{1,0:T(8,128)(2,1)}, u32[]{:S(2)}, u32[]{:S(2)}) collective-permute-start(bf16[128,1024]{1,0:T(8,128)(2,1)S(1)} %collective-permute-done.1.refs_9_), channel_id=1, source_target_pairs={{0,64},{16,80},{32,96},{48,112},{64,0},{80,16},{96,32},{112,48},{1... | collective-permute-start | bytes 786440 | tf_op jit(solution)/shard_map/ppermute | solution.py:27
  29.7 7.6 %collective-permute-start.5 = (bf16[128,1024]{1,0:T(8,128)(2,1)S(1)}, bf16[128,1024]{1,0:T(8,128)(2,1)S(1)}, u32[]{:S(2)}, u32[]{:S(2)}) collective-permute-start(bf16[128,1024]{1,0:T(8,128)(2,1)S(1)} %collective-permute-done.3.refs_1_), channel_id=1, source_target_pairs={{0,16},{16,32},{32,48},{48,0},{64,80},{80,96},{96,112},{112,64},{1... | collective-permute-start | bytes 786440 | tf_op jit(solution)/shard_map/ppermute | solution.py:27
  29.7 10.5 %collective-permute-start.8 = (bf16[128,1024]{1,0:T(8,128)(2,1)S(1)}, bf16[128,1024]{1,0:T(8,128)(2,1)}, u32[]{:S(2)}, u32[]{:S(2)}) collective-permute-start(bf16[128,1024]{1,0:T(8,128)(2,1)S(1)} %collective-permute-done.6.refs_5_), channel_id=1, source_target_pairs={{0,16},{16,32},{32,48},{48,0},{64,80},{80,96},{96,112},{112,64},{1... | collective-permute-start | bytes 786440 | tf_op jit(solution)/shard_map/ppermute | solution.py:27
  32.6 7.6 %collective-permute-start.13 = (bf16[128,1024]{1,0:T(8,128)(2,1)S(1)}, bf16[128,1024]{1,0:T(8,128)(2,1)}, u32[]{:S(2)}, u32[]{:S(2)}) collective-permute-start(bf16[128,1024]{1,0:T(8,128)(2,1)S(1)} %collective-permute-done.9.refs_11_), channel_id=1, source_target_pairs={{0,64},{16,80},{32,96},{48,112},{64,0},{80,16},{96,32},{112,48},{1... | collective-permute-start | bytes 786440 | tf_op jit(solution)/shard_map/ppermute | solution.py:27
  33.1 0.9 %copy-start = (bf16[128,1024]{1,0:T(8,128)(2,1)S(1)}, bf16[128,1024]{1,0:T(8,128)(2,1)}, u32[]{:S(2)}) copy-start(bf16[128,1024]{1,0:T(8,128)(2,1)} %refs_0_) | copy-start | bytes 786436
  34.0 0.9 %copy-start.1 = (bf16[128,1024]{1,0:T(8,128)(2,1)S(1)}, bf16[128,1024]{1,0:T(8,128)(2,1)}, u32[]{:S(2)}) copy-start(bf16[128,1024]{1,0:T(8,128)(2,1)} %refs_1_.1) | copy-start | bytes 786436
  45.4 1.6 %collective-permute-start.14 = (bf16[128,1152]{1,0:T(8,128)(2,1)S(1)}, bf16[128,1152]{1,0:T(8,128)(2,1)S(1)}, u32[]{:S(2)}, u32[]{:S(2)}) collective-permute-start(bf16[128,1152]{1,0:T(8,128)(2,1)S(1)} %get-tuple-element.47), channel_id=1, source_target_pairs={{0,1},{1,0},{2,3},{3,2},{4,5},{5,4},{6,7},{7,6},{8,9},{9,8},{10,11... | collective-permute-start | bytes 884744 | tf_op jit(solution)/shard_map/ppermute | solution.py:31
  74.7 1.5 %collective-permute-start.15 = (bf16[128,1024]{1,0:T(8,128)(2,1)S(1)}, bf16[128,1024]{1,0:T(8,128)(2,1)S(1)}, u32[]{:S(2)}, u32[]{:S(2)}) collective-permute-start(bf16[128,1024]{1,0:T(8,128)(2,1)S(1)} %bitcast.6), channel_id=1, source_target_pairs={{0,1},{1,0},{2,3},{3,2},{4,5},{5,4},{6,7},{7,6},{8,9},{9,8},{10,11... | collective-permute-start | bytes 786440 | tf_op jit(solution)/shard_map/ppermute | solution.py:31
  79.1 10.0 %all-to-all-start.2 = ((f32[8,4,1152]{2,1,0:T(4,128)}), f32[8,4,1152]{2,1,0:T(4,128)S(1)}, u32[]{:S(2)}, u32[]{:S(2)}) async-start(f32[8,4,1152]{2,1,0:T(4,128)} %get-tuple-element.66), calls=%async_computation.2 | async-start | bytes 294912 | tf_op jit(solution)/shard_map/all_to_all | solution.py:312
  82.5 1.2 %collective-permute-start.16 = (f32[8,128]{1,0:T(8,128)S(1)}, f32[8,128]{1,0:T(8,128)S(1)}, u32[]{:S(2)}, u32[]{:S(2)}) collective-permute-start(f32[8,128]{1,0:T(8,128)S(1)} %slice.10.split), channel_id=1, source_target_pairs={{0,1},{1,0},{2,3},{3,2},{4,5},{5,4},{6,7},{7,6},{8,9},{9,8},{10,11... | collective-permute-start | bytes 12296 | tf_op jit(solution)/shard_map/ppermute | solution.py:31

commit v8 on v7

--- a/solution.py
+++ b/solution.py
@@ -106,11 +106,13 @@
     return row_ids == lax.broadcasted_iota(jnp.int32, shape, 1)
 
 
-def split_scalar(value, rows):
+def split_scalar(value, rows, half):
     wide = jnp.broadcast_to(value, (rows, LANES))
     high = wide.astype(BF16).astype(F32)
-    lane = lax.broadcasted_iota(jnp.int32, wide.shape, 1)
-    return jnp.where(lane < LANES // 2, high, (wide - high).astype(BF16).astype(F32))
+    low = (wide - high).astype(BF16).astype(F32)
+    lane = lax.broadcasted_iota(jnp.int32, wide.shape, 1) - half * (LANES // 2)
+    inside = (lane >= 0) & (lane < LANES // 2)
+    return jnp.where(inside, jnp.where(lane < LANES // 4, high, low), 0.0)
 
 
 def gram_kernel(core, *refs, where_a, where_b):
@@ -166,8 +168,9 @@
     shift = jnp.where(on_own(part_a.shape), 1.0 * cols, 0.0)
     gram_a = part_a[...] - shift
     gram_b = part_b[...] - shift
-    keep[:, total_rows:] = split_scalar(jnp.sum(loss, axis=1, keepdims=True), rows)
-    send[:, total_rows:] = jnp.zeros((rows, LANES), BF16)
+    loss = jnp.sum(loss, axis=1, keepdims=True)
+    keep[:, total_rows:] = split_scalar(loss, rows, 0)
+    send[:, total_rows:] = split_scalar(loss, rows, 1).astype(BF16)
 
     @pl.when(core[0] == 0)
     def _():
@@ -241,7 +244,6 @@
     own_b,
     vecs,
     split,
-    other,
     grad_a,
     grad_b,
     loss,
@@ -263,7 +265,7 @@
     wide_b = high_b[...].astype(F32) + low_b[...].astype(F32) - means[2:3] - norm_b * means[3:4]
     grad_a[...] = (vecs[0:1, :] * wide_a).astype(BF16)
     grad_b[...] = (vecs[1:2, :] * wide_b).astype(BF16)
-    diag = jnp.sum(split[0:1, :] + other[0:1, :]) * (2.0 / LANES)
+    diag = jnp.sum(split[0:1, :]) * (4.0 / LANES)
     loss[0] = (diag + OFF_WEIGHT * square) / total_cols
 
 
@@ -313,7 +315,7 @@
     own = [norms[i] for i in first]
     grad_a, grad_b, loss = call(
         functools.partial(out_kernel, total_cols=cols * blocks),
-        [core, stats] + grads + own + [vecs, split, swap_cores(split)],
+        [core, stats] + grads + own + [vecs, split],
         [shape((rows, cols), BF16), shape((rows, cols), BF16), shape((1,), F32)],
         limit=8,
     )

time: 90.8 us -> 88.6 us (0.976)
  blocking collectives: 27.6 us -> 36.6 us
  waiting for transfers between devices: 31.6 us -> 25.1 us
  starting transfers between devices: 19.1 us -> 15.5 us
  Pallas kernels: 9.42 us -> 8.31 us
    all_to_all x0 -> x1, blocking collectives: none -> 9.06 us  [body(): lax.all_to_all(stats, 'sample', split_axis=0, concat_axis=0, tiled=True)]
    all_to_all x1 -> x0, waiting for transfers between devices: 5.36 us -> none  [body(): lax.all_to_all(stats, 'sample', split_axis=0, concat_axis=0, tiled=True)]
    all_to_all x1 -> x0, starting transfers between devices: 3.38 us -> none  [body(): lax.all_to_all(stats, 'sample', split_axis=0, concat_axis=0, tiled=True)]
    pallas_call x4, Pallas kernels: 9.42 us -> 8.31 us  [call(): pl.pallas_call(kernel, out_shape=outs, in_specs=[spec(arg.shape) for arg...]
    ppermute x3 -> x2, waiting for transfers between devices: 4.15 us -> 3.11 us  [swap_cores(): lax.ppermute(block, 'feat', [(i, i ^ 1) for i in range(lax.axis_size('fea...]
  transfers between devices with their start and end apart: 18 -> 16, of which waited for: 13 -> 11; matrix products, arithmetic and copies ran while one was open for 0% -> 0% of each run, Pallas kernels for 0% -> 0%
where the time goes in v8:
time: 88.6 us; the launch traced here: 88.3 us
  blocking collectives  36.6 us (41%)
  waiting for transfers between devices  25.1 us (28%)
  starting transfers between devices  15.5 us (17%)
  Pallas kernels  8.31 us (9%)
  local copies, waits for them, and re-layouts  1.93 us (2%)
    all_to_all x2, blocking collectives, exchange_chips(): lax.all_to_all(block, 'feat', split_axis=0, concat_axis=0, tiled=True, ax...  27.6 us
    ppermute x14, waiting for transfers between devices, send_sample(): return lax.ppermute(block, 'sample', moves)  22 us
    ppermute x14, starting transfers between devices, send_sample(): return lax.ppermute(block, 'sample', moves)  15.5 us
    all_to_all x1, blocking collectives, body(): lax.all_to_all(stats, 'sample', split_axis=0, concat_axis=0, tiled=True)  9.06 us
    pallas_call x4, Pallas kernels, call(): pl.pallas_call(kernel, out_shape=outs, in_specs=[spec(arg.shape) for arg...  8.31 us
    ppermute x2, waiting for transfers between devices, swap_cores(): lax.ppermute(block, 'feat', [(i, i ^ 1) for i in range(lax.axis_size('fea...  3.11 us
    unnamed x4, local copies, waits for them, and re-layouts  1.9 us
  transfers between devices with their start and end apart: 16, of which 11 were waited for; matrix products, arithmetic and copies ran while one was open for 0% of the time, Pallas kernels for 0%

profile of v8, /device:TPU:0, one launch (start us, length us, event | category | flops | bytes accessed | tf_op | source)
XLA Modules:
  0.0 88.3 jit_solution(12006610303307323324)
XLA Ops:
  0.6 3.2 %collective-permute-start.2 = (bf16[128,1024]{1,0:T(8,128)(2,1)}, bf16[128,1024]{1,0:T(8,128)(2,1)S(1)}, u32[]{:S(2)}, u32[]{:S(2)}) collective-permute-start(bf16[128,1024]{1,0:T(8,128)(2,1)} %refs_1_.1), channel_id=1, source_target_pairs={{0,48},{16,0},{32,16},{48,32},{64,112},{80,64},{96,80},{112,96},{1... | collective-permute-start | bytes 786440 | tf_op jit(solution)/shard_map/ppermute | solution.py:27
  3.8 1.9 %collective-permute-start = (bf16[128,1024]{1,0:T(8,128)(2,1)}, bf16[128,1024]{1,0:T(8,128)(2,1)S(1)}, u32[]{:S(2)}, u32[]{:S(2)}) collective-permute-start(bf16[128,1024]{1,0:T(8,128)(2,1)} %refs_0_), channel_id=1, source_target_pairs={{0,64},{16,80},{32,96},{48,112},{64,0},{80,16},{96,32},{112,48},{1... | collective-permute-start | bytes 786440 | tf_op jit(solution)/shard_map/ppermute | solution.py:27
  5.7 0.0 collective-permute-start.1
  5.7 4.0 %collective-permute-done.2.refs_10_ = bf16[128,1024]{1,0:T(8,128)(2,1)S(1)} collective-permute-done((bf16[128,1024]{1,0:T(8,128)(2,1)}, bf16[128,1024]{1,0:T(8,128)(2,1)S(1)}, u32[]{:S(2)}, u32[]{:S(2)}) %collective-permute-start.2) | collective-permute-done | bytes 262176 | tf_op jit(solution)/shard_map/ppermute | solution.py:27
  9.7 1.9 %collective-permute-start.12 = (bf16[128,1024]{1,0:T(8,128)(2,1)S(1)}, bf16[128,1024]{1,0:T(8,128)(2,1)S(1)}, u32[]{:S(2)}, u32[]{:S(2)}) collective-permute-start(bf16[128,1024]{1,0:T(8,128)(2,1)S(1)} %collective-permute-done.2.refs_10_), channel_id=1, source_target_pairs={{0,64},{16,80},{32,96},{48,112},{64,0},{80,16},{96,32},{112,48},{1... | collective-permute-start | bytes 786440 | tf_op jit(solution)/shard_map/ppermute | solution.py:27
  11.6 0.8 collective-permute-done.refs_4_
  12.4 2.2 %collective-permute-done.1.refs_9_ = bf16[128,1024]{1,0:T(8,128)(2,1)S(1)} collective-permute-done((bf16[128,1024]{1,0:T(8,128)(2,1)}, bf16[128,1024]{1,0:T(8,128)(2,1)S(1)}, u32[]{:S(2)}, u32[]{:S(2)}) %collective-permute-start.1) | collective-permute-done | bytes 262176 | tf_op jit(solution)/shard_map/ppermute | solution.py:27
  14.6 0.6 collective-permute-start.4
  15.2 1.5 %collective-permute-start.3 = (bf16[128,1024]{1,0:T(8,128)(2,1)}, bf16[128,1024]{1,0:T(8,128)(2,1)S(1)}, u32[]{:S(2)}, u32[]{:S(2)}) collective-permute-start(bf16[128,1024]{1,0:T(8,128)(2,1)} %refs_0_), channel_id=1, source_target_pairs={{0,16},{16,32},{32,48},{48,0},{64,80},{80,96},{96,112},{112,64},{1... | collective-permute-start | bytes 786440 | tf_op jit(solution)/shard_map/ppermute | solution.py:27
  16.6 1.8 %collective-permute-start.7 = (bf16[128,1024]{1,0:T(8,128)(2,1)S(1)}, bf16[128,1024]{1,0:T(8,128)(2,1)S(1)}, u32[]{:S(2)}, u32[]{:S(2)}) collective-permute-start(bf16[128,1024]{1,0:T(8,128)(2,1)S(1)} %collective-permute-done.refs_4_), channel_id=1, source_target_pairs={{0,48},{16,0},{32,16},{48,32},{64,112},{80,64},{96,80},{112,96},{1... | collective-permute-start | bytes 786440 | tf_op jit(solution)/shard_map/ppermute | solution.py:27
  18.4 0.2 collective-permute-start.6
  18.7 0.0 collective-permute-done.12.refs_14_
  18.7 3.0 %collective-permute-start.9 = (bf16[128,1024]{1,0:T(8,128)(2,1)S(1)}, bf16[128,1024]{1,0:T(8,128)(2,1)S(1)}, u32[]{:S(2)}, u32[]{:S(2)}) collective-permute-start(bf16[128,1024]{1,0:T(8,128)(2,1)S(1)} %collective-permute-done.2.refs_10_), channel_id=1, source_target_pairs={{0,48},{16,0},{32,16},{48,32},{64,112},{80,64},{96,80},{112,96},{1... | collective-permute-start | bytes 786440 | tf_op jit(solution)/shard_map/ppermute | solution.py:27
  21.7 2.4 %collective-permute-done.4.refs_2_ = bf16[128,1024]{1,0:T(8,128)(2,1)S(1)} collective-permute-done((bf16[128,1024]{1,0:T(8,128)(2,1)}, bf16[128,1024]{1,0:T(8,128)(2,1)S(1)}, u32[]{:S(2)}, u32[]{:S(2)}) %collective-permute-start.4) | collective-permute-done | bytes 262176 | tf_op jit(solution)/shard_map/ppermute | solution.py:27
  24.1 0.3 collective-permute-start.10
  24.4 1.5 %collective-permute-done.3.refs_1_ = bf16[128,1024]{1,0:T(8,128)(2,1)S(1)} collective-permute-done((bf16[128,1024]{1,0:T(8,128)(2,1)}, bf16[128,1024]{1,0:T(8,128)(2,1)S(1)}, u32[]{:S(2)}, u32[]{:S(2)}) %collective-permute-start.3) | collective-permute-done | bytes 262176 | tf_op jit(solution)/shard_map/ppermute | solution.py:27
  25.9 0.3 collective-permute-start.11
  26.1 3.6 %collective-permute-done.7.refs_6_ = bf16[128,1024]{1,0:T(8,128)(2,1)S(1)} collective-permute-done((bf16[128,1024]{1,0:T(8,128)(2,1)S(1)}, bf16[128,1024]{1,0:T(8,128)(2,1)S(1)}, u32[]{:S(2)}, u32[]{:S(2)}) %collective-permute-start.7) | collective-permute-done | bytes 262176 | tf_op jit(solution)/shard_map/ppermute | solution.py:27
  29.7 0.0 collective-permute-start.5
  29.7 0.0 collective-permute-done.6.refs_5_
  29.7 0.4 collective-permute-start.8
  30.1 2.5 %collective-permute-done.9.refs_11_ = bf16[128,1024]{1,0:T(8,128)(2,1)S(1)} collective-permute-done((bf16[128,1024]{1,0:T(8,128)(2,1)S(1)}, bf16[128,1024]{1,0:T(8,128)(2,1)S(1)}, u32[]{:S(2)}, u32[]{:S(2)}) %collective-permute-start.9) | collective-permute-done | bytes 262176 | tf_op jit(solution)/shard_map/ppermute | solution.py:27
  32.6 0.5 collective-permute-start.13
  33.1 0.0 copy-start
  33.1 0.9 %copy-done = bf16[128,1024]{1,0:T(8,128)(2,1)S(1)} copy-done((bf16[128,1024]{1,0:T(8,128)(2,1)S(1)}, bf16[128,1024]{1,0:T(8,128)(2,1)}, u32[]{:S(2)}) %copy-start) | copy-done | bytes 262168
  34.0 0.0 copy-start.1
  34.0 0.9 %copy-done.1 = bf16[128,1024]{1,0:T(8,128)(2,1)S(1)} copy-done((bf16[128,1024]{1,0:T(8,128)(2,1)S(1)}, bf16[128,1024]{1,0:T(8,128)(2,1)}, u32[]{:S(2)}) %copy-start.1) | copy-done | bytes 262168
  35.0 0.0 collective-permute-done.10.refs_12_
  35.0 0.0 collective-permute-done.11.refs_13_
  35.0 2.2 %collective-permute-done.5.refs_3_ = bf16[128,1024]{1,0:T(8,128)(2,1)S(1)} collective-permute-done((bf16[128,1024]{1,0:T(8,128)(2,1)S(1)}, bf16[128,1024]{1,0:T(8,128)(2,1)S(1)}, u32[]{:S(2)}, u32[]{:S(2)}) %collective-permute-start.5) | collective-permute-done | bytes 262176 | tf_op jit(solution)/shard_map/ppermute | solution.py:27
  37.3 2.8 %collective-permute-done.8.refs_7_ = bf16[128,1024]{1,0:T(8,128)(2,1)S(1)} collective-permute-done((bf16[128,1024]{1,0:T(8,128)(2,1)S(1)}, bf16[128,1024]{1,0:T(8,128)(2,1)S(1)}, u32[]{:S(2)}, u32[]{:S(2)}) %collective-permute-start.8) | collective-permute-done | bytes 262176 | tf_op jit(solution)/shard_map/ppermute | solution.py:27
  40.1 0.0 collective-permute-done.13.refs_15_
  40.1 4.9 %shard_map.50 = (bf16[128,1024]{1,0:T(8,128)(2,1)S(1)}, bf16[128,1024]{1,0:T(8,128)(2,1)S(1)}, bf16[128,1024]{1,0:T(8,128)(2,1)S(1)}, bf16[128,1024]{1,0:T(8,128...) custom-call(s32[1]{0:T(128)} %bitcast.core, ...), custom_call_target="tpu_custom_call", output_to_operand_aliasing={{0}: (1, {}), {1}: (2, {}), {2}: (3, {}), {3}: (4, {}), {4}... | custom-call | tf_op jit(solution)/shard_map/pallas_call | solution.py:51
  45.0 0.0 collective-permute-start.14
  45.0 1.6 %collective-permute-done.14 = bf16[128,1152]{1,0:T(8,128)(2,1)S(1)} collective-permute-done((bf16[128,1152]{1,0:T(8,128)(2,1)S(1)}, bf16[128,1152]{1,0:T(8,128)(2,1)S(1)}, u32[]{:S(2)}, u32[]{:S(2)}) %collective-permute-start.14) | collective-permute-done | bytes 294944 | tf_op jit(solution)/shard_map/ppermute | solution.py:31
  46.6 0.1 add_convert_fusion
  46.7 16.7 %all_to_all.25 = bf16[8,16,1152]{2,1,0:T(8,128)(2,1)S(1)} all-to-all(bf16[8,16,1152]{2,1,0:T(8,128)(2,1)S(1)} %bitcast.8), channel_id=1, replica_groups={{0,2,4,6,8,10,12,14},{1,3,5,7,9,11,13,15},{16,18,20,22,24,26,28,30},{17..., dimensions={0} | all-to-all | bytes 589824 | tf_op jit(solution)/shard_map/all_to_all | solution.py:37
  63.5 10.9 %all_to_all.26 = bf16[8,16,1024]{2,1,0:T(8,128)(2,1)S(1)} all-to-all(bf16[8,16,1024]{2,1,0:T(8,128)(2,1)S(1)} %broadcast_in_dim.2), channel_id=1, replica_groups={{0,2,4,6,8,10,12,14},{1,3,5,7,9,11,13,15},{16,18,20,22,24,26,28,30},{17..., dimensions={0} | all-to-all | bytes 524288 | tf_op jit(solution)/shard_map/all_to_all | solution.py:37
  74.3 0.0 collective-permute-start.15
  74.3 1.5 %collective-permute-done.15.theirs = bf16[128,1024]{1,0:T(8,128)(2,1)S(1)} collective-permute-done((bf16[128,1024]{1,0:T(8,128)(2,1)S(1)}, bf16[128,1024]{1,0:T(8,128)(2,1)S(1)}, u32[]{:S(2)}, u32[]{:S(2)}) %collective-permute-start.15) | collective-permute-done | bytes 262176 | tf_op jit(solution)/shard_map/ppermute | solution.py:31
  75.9 2.0 %shard_map.51 = (bf16[128,1024]{1,0:T(8,128)(2,1)S(1)}, bf16[128,1024]{1,0:T(8,128)(2,1)S(1)}, bf16[128,1024]{1,0:T(8,128)(2,1)S(1)}, bf16[128,1024]{1,0:T(8,128)(2,1)S(1)}, f32[8,4,1152]{2,1,0:T(4,128)S(1)}) custom-call(s32[1]{0:T(128)} %bitcast.core, ...), custom_call_target="tpu_custom_call", output_to_operand_aliasing={{0}: (7, {}), {1}: (8, {}), {2}: (15, {}), {3}: (16, {})} | custom-call | tf_op jit(solution)/shard_map/pallas_call | solution.py:51
  77.9 9.1 %all_to_all.27.stats = f32[8,4,1152]{2,1,0:T(4,128)S(1)} all-to-all(f32[8,4,1152]{2,1,0:T(4,128)S(1)} %get-tuple-element.66), channel_id=1, replica_groups=mesh['sample'=8,'feat'=16] {'sample'}, dimensions={0} | all-to-all | bytes 294912 | tf_op jit(solution)/shard_map/all_to_all | solution.py:314
  87.0 1.3 %shard_map.52 = (bf16[128,1024]{1,0:T(8,128)(2,1)}, bf16[128,1024]{1,0:T(8,128)(2,1)}, f32[1]{0:T(128)}) custom-call(s32[1]{0:T(128)} %bitcast.core, f32[8,4,1152]{2,1,0:T(4,128)S(1)} %all_to_all.27.stats, bf16[128,1024]{1,0:T(8,128)(2,1)S(1)} %get-tuple-element.67.high_a, bf16[128,1024]{1,0:T(8,128)(2,1)S(1)} %get-tuple-element.68.low_a, ...), custom_call_target="tpu_custom_call" | custom-call | tf_op jit(solution)/shard_map/pallas_call | solution.py:51
  (5 shorter events, 0.1 us)
Async XLA Ops:
  0.6 9.0 %collective-permute-start.2 = (bf16[128,1024]{1,0:T(8,128)(2,1)}, bf16[128,1024]{1,0:T(8,128)(2,1)S(1)}, u32[]{:S(2)}, u32[]{:S(2)}) collective-permute-start(bf16[128,1024]{1,0:T(8,128)(2,1)} %refs_1_.1), channel_id=1, source_target_pairs={{0,48},{16,0},{32,16},{48,32},{64,112},{80,64},{96,80},{112,96},{1... | collective-permute-start | bytes 786440 | tf_op jit(solution)/shard_map/ppermute | solution.py:27
  3.8 8.6 %collective-permute-start = (bf16[128,1024]{1,0:T(8,128)(2,1)}, bf16[128,1024]{1,0:T(8,128)(2,1)S(1)}, u32[]{:S(2)}, u32[]{:S(2)}) collective-permute-start(bf16[128,1024]{1,0:T(8,128)(2,1)} %refs_0_), channel_id=1, source_target_pairs={{0,64},{16,80},{32,96},{48,112},{64,0},{80,16},{96,32},{112,48},{1... | collective-permute-start | bytes 786440 | tf_op jit(solution)/shard_map/ppermute | solution.py:27
  5.7 8.9 %collective-permute-start.1 = (bf16[128,1024]{1,0:T(8,128)(2,1)}, bf16[128,1024]{1,0:T(8,128)(2,1)S(1)}, u32[]{:S(2)}, u32[]{:S(2)}) collective-permute-start(bf16[128,1024]{1,0:T(8,128)(2,1)} %refs_1_.1), channel_id=1, source_target_pairs={{0,16},{16,32},{32,48},{48,0},{64,80},{80,96},{96,112},{112,64},{1... | collective-permute-start | bytes 786440 | tf_op jit(solution)/shard_map/ppermute | solution.py:27
  9.7 9.0 %collective-permute-start.12 = (bf16[128,1024]{1,0:T(8,128)(2,1)S(1)}, bf16[128,1024]{1,0:T(8,128)(2,1)S(1)}, u32[]{:S(2)}, u32[]{:S(2)}) collective-permute-start(bf16[128,1024]{1,0:T(8,128)(2,1)S(1)} %collective-permute-done.2.refs_10_), channel_id=1, source_target_pairs={{0,64},{16,80},{32,96},{48,112},{64,0},{80,16},{96,32},{112,48},{1... | collective-permute-start | bytes 786440 | tf_op jit(solution)/shard_map/ppermute | solution.py:27
  14.6 9.5 %collective-permute-start.4 = (bf16[128,1024]{1,0:T(8,128)(2,1)}, bf16[128,1024]{1,0:T(8,128)(2,1)S(1)}, u32[]{:S(2)}, u32[]{:S(2)}) collective-permute-start(bf16[128,1024]{1,0:T(8,128)(2,1)} %refs_0_), channel_id=1, source_target_pairs={{0,48},{16,0},{32,16},{48,32},{64,112},{80,64},{96,80},{112,96},{1... | collective-permute-start | bytes 786440 | tf_op jit(solution)/shard_map/ppermute | solution.py:27
  15.2 10.7 %collective-permute-start.3 = (bf16[128,1024]{1,0:T(8,128)(2,1)}, bf16[128,1024]{1,0:T(8,128)(2,1)S(1)}, u32[]{:S(2)}, u32[]{:S(2)}) collective-permute-start(bf16[128,1024]{1,0:T(8,128)(2,1)} %refs_0_), channel_id=1, source_target_pairs={{0,16},{16,32},{32,48},{48,0},{64,80},{80,96},{96,112},{112,64},{1... | collective-permute-start | bytes 786440 | tf_op jit(solution)/shard_map/ppermute | solution.py:27
  16.6 13.0 %collective-permute-start.7 = (bf16[128,1024]{1,0:T(8,128)(2,1)S(1)}, bf16[128,1024]{1,0:T(8,128)(2,1)S(1)}, u32[]{:S(2)}, u32[]{:S(2)}) collective-permute-start(bf16[128,1024]{1,0:T(8,128)(2,1)S(1)} %collective-permute-done.refs_4_), channel_id=1, source_target_pairs={{0,48},{16,0},{32,16},{48,32},{64,112},{80,64},{96,80},{112,96},{1... | collective-permute-start | bytes 786440 | tf_op jit(solution)/shard_map/ppermute | solution.py:27
  18.4 11.3 %collective-permute-start.6 = (bf16[128,1024]{1,0:T(8,128)(2,1)S(1)}, bf16[128,1024]{1,0:T(8,128)(2,1)S(1)}, u32[]{:S(2)}, u32[]{:S(2)}) collective-permute-start(bf16[128,1024]{1,0:T(8,128)(2,1)S(1)} %collective-permute-done.refs_4_), channel_id=1, source_target_pairs={{0,16},{16,32},{32,48},{48,0},{64,80},{80,96},{96,112},{112,64},{1... | collective-permute-start | bytes 786440 | tf_op jit(solution)/shard_map/ppermute | solution.py:27
  18.7 13.9 %collective-permute-start.9 = (bf16[128,1024]{1,0:T(8,128)(2,1)S(1)}, bf16[128,1024]{1,0:T(8,128)(2,1)S(1)}, u32[]{:S(2)}, u32[]{:S(2)}) collective-permute-start(bf16[128,1024]{1,0:T(8,128)(2,1)S(1)} %collective-permute-done.2.refs_10_), channel_id=1, source_target_pairs={{0,48},{16,0},{32,16},{48,32},{64,112},{80,64},{96,80},{112,96},{1... | collective-permute-start | bytes 786440 | tf_op jit(solution)/shard_map/ppermute | solution.py:27
  24.1 11.0 %collective-permute-start.10 = (bf16[128,1024]{1,0:T(8,128)(2,1)}, bf16[128,1024]{1,0:T(8,128)(2,1)S(1)}, u32[]{:S(2)}, u32[]{:S(2)}) collective-permute-start(bf16[128,1024]{1,0:T(8,128)(2,1)} %refs_1_.1), channel_id=1, source_target_pairs={{0,64},{16,80},{32,96},{48,112},{64,0},{80,16},{96,32},{112,48},{1... | collective-permute-start | bytes 786440 | tf_op jit(solution)/shard_map/ppermute | solution.py:27
  25.9 9.2 %collective-permute-start.11 = (bf16[128,1024]{1,0:T(8,128)(2,1)S(1)}, bf16[128,1024]{1,0:T(8,128)(2,1)S(1)}, u32[]{:S(2)}, u32[]{:S(2)}) collective-permute-start(bf16[128,1024]{1,0:T(8,128)(2,1)S(1)} %collective-permute-done.1.refs_9_), channel_id=1, source_target_pairs={{0,64},{16,80},{32,96},{48,112},{64,0},{80,16},{96,32},{112,48},{1... | collective-permute-start | bytes 786440 | tf_op jit(solution)/shard_map/ppermute | solution.py:27
  29.7 7.6 %collective-permute-start.5 = (bf16[128,1024]{1,0:T(8,128)(2,1)S(1)}, bf16[128,1024]{1,0:T(8,128)(2,1)S(1)}, u32[]{:S(2)}, u32[]{:S(2)}) collective-permute-start(bf16[128,1024]{1,0:T(8,128)(2,1)S(1)} %collective-permute-done.3.refs_1_), channel_id=1, source_target_pairs={{0,16},{16,32},{32,48},{48,0},{64,80},{80,96},{96,112},{112,64},{1... | collective-permute-start | bytes 786440 | tf_op jit(solution)/shard_map/ppermute | solution.py:27
  29.7 10.4 %collective-permute-start.8 = (bf16[128,1024]{1,0:T(8,128)(2,1)S(1)}, bf16[128,1024]{1,0:T(8,128)(2,1)S(1)}, u32[]{:S(2)}, u32[]{:S(2)}) collective-permute-start(bf16[128,1024]{1,0:T(8,128)(2,1)S(1)} %collective-permute-done.6.refs_5_), channel_id=1, source_target_pairs={{0,16},{16,32},{32,48},{48,0},{64,80},{80,96},{96,112},{112,64},{1... | collective-permute-start | bytes 786440 | tf_op jit(solution)/shard_map/ppermute | solution.py:27
  32.6 7.5 %collective-permute-start.13 = (bf16[128,1024]{1,0:T(8,128)(2,1)S(1)}, bf16[128,1024]{1,0:T(8,128)(2,1)}, u32[]{:S(2)}, u32[]{:S(2)}) collective-permute-start(bf16[128,1024]{1,0:T(8,128)(2,1)S(1)} %collective-permute-done.9.refs_11_), channel_id=1, source_target_pairs={{0,64},{16,80},{32,96},{48,112},{64,0},{80,16},{96,32},{112,48},{1... | collective-permute-start | bytes 786440 | tf_op jit(solution)/shard_map/ppermute | solution.py:27
  33.1 0.9 %copy-start = (bf16[128,1024]{1,0:T(8,128)(2,1)S(1)}, bf16[128,1024]{1,0:T(8,128)(2,1)}, u32[]{:S(2)}) copy-start(bf16[128,1024]{1,0:T(8,128)(2,1)} %refs_0_) | copy-start | bytes 786436
  34.0 0.9 %copy-start.1 = (bf16[128,1024]{1,0:T(8,128)(2,1)S(1)}, bf16[128,1024]{1,0:T(8,128)(2,1)}, u32[]{:S(2)}) copy-start(bf16[128,1024]{1,0:T(8,128)(2,1)} %refs_1_.1) | copy-start | bytes 786436
  45.0 1.6 %collective-permute-start.14 = (bf16[128,1152]{1,0:T(8,128)(2,1)S(1)}, bf16[128,1152]{1,0:T(8,128)(2,1)S(1)}, u32[]{:S(2)}, u32[]{:S(2)}) collective-permute-start(bf16[128,1152]{1,0:T(8,128)(2,1)S(1)} %get-tuple-element.47), channel_id=1, source_target_pairs={{0,1},{1,0},{2,3},{3,2},{4,5},{5,4},{6,7},{7,6},{8,9},{9,8},{10,11... | collective-permute-start | bytes 884744 | tf_op jit(solution)/shard_map/ppermute | solution.py:31
  74.3 1.5 %collective-permute-start.15 = (bf16[128,1024]{1,0:T(8,128)(2,1)S(1)}, bf16[128,1024]{1,0:T(8,128)(2,1)S(1)}, u32[]{:S(2)}, u32[]{:S(2)}) collective-permute-start(bf16[128,1024]{1,0:T(8,128)(2,1)S(1)} %bitcast.6), channel_id=1, source_target_pairs={{0,1},{1,0},{2,3},{3,2},{4,5},{5,4},{6,7},{7,6},{8,9},{9,8},{10,11... | collective-permute-start | bytes 786440 | tf_op jit(solution)/shard_map/ppermute | solution.py:31

commit v9 on v8

--- a/solution.py
+++ b/solution.py
@@ -14,7 +14,7 @@
 BF16 = jnp.bfloat16
 LANES = 128
 SUMS = 4
-CHUNK = 512
+CHUNK = 256
 
 
 def send_sample(block, turn, step):
@@ -78,8 +78,8 @@
     b_on = send_sample(b, 0, -1)
     a_over = send_sample(a, 1, 0)
     a_next = after(a, b_back, b_on, a_over)
-    b_far = send_sample(after(b_on, a_over, b_back), 0, -1)
-    b_over = send_sample(after(b, a_over, b_back, b_on), 1, 0)
+    b_far = send_sample(after(b_on, b_back), 0, -1)
+    b_over = send_sample(after(b, a_over), 1, 0)
     b_back_over = send_sample(b_back, 1, 0)
     b_on_over = send_sample(b_on, 1, 0)
     a_over_back = send_sample(after(a_over, b_back, b_on), 0, 1)
@@ -89,7 +89,7 @@
     a_far = send_sample(a_back, 0, 1)
     a_over_far = send_sample(a_over_back, 0, 1)
     b_far_over = send_sample(b_far, 1, 0)
-    a_own, b_own = bring(after(a, a_over, b_back, b_on), b)
+    a_own, b_own = bring(after(a, a_back), after(b, a_back))
     parts = [a_own, a_back, a_on, a_far, a_over, a_over_back, a_over_on, a_over_far]
     parts += [b_own, b_back, b_on, b_far, b_over, b_back_over, b_on_over, b_far_over]
     where_a = [(i, 0) for i in range(8)]

time: 88.6 us -> 88.3 us (level)
  waiting for transfers between devices: 25.1 us -> 21.1 us
  starting transfers between devices: 15.5 us -> 19.2 us
    ppermute x14, waiting for transfers between devices: 22 us -> 18 us  [send_sample(): return lax.ppermute(block, 'sample', moves)]
    ppermute x14, starting transfers between devices: 15.5 us -> 19.2 us  [send_sample(): return lax.ppermute(block, 'sample', moves)]
  transfers between devices with their start and end apart: 16 -> 16, of which waited for: 11 -> 10; matrix products, arithmetic and copies ran while one was open for 0% -> 0% of each run, Pallas kernels for 0% -> 0%
where the time goes in v9:
time: 88.3 us; the launch traced here: 88 us
  blocking collectives  36.6 us (41%)
  waiting for transfers between devices  21.1 us (24%)
  starting transfers between devices  19.2 us (22%)
  Pallas kernels  8.32 us (9%)
  local copies, waits for them, and re-layouts  1.93 us (2%)
    all_to_all x2, blocking collectives, exchange_chips(): lax.all_to_all(block, 'feat', split_axis=0, concat_axis=0, tiled=True, ax...  27.6 us
    ppermute x14, starting transfers between devices, send_sample(): return lax.ppermute(block, 'sample', moves)  19.2 us
    ppermute x14, waiting for transfers between devices, send_sample(): return lax.ppermute(block, 'sample', moves)  18 us
    all_to_all x1, blocking collectives, body(): lax.all_to_all(stats, 'sample', split_axis=0, concat_axis=0, tiled=True)  9.06 us
    pallas_call x4, Pallas kernels, call(): pl.pallas_call(kernel, out_shape=outs, in_specs=[spec(arg.shape) for arg...  8.32 us
    ppermute x2, waiting for transfers between devices, swap_cores(): lax.ppermute(block, 'feat', [(i, i ^ 1) for i in range(lax.axis_size('fea...  3.11 us
    unnamed x4, local copies, waits for them, and re-layouts  1.9 us
  transfers between devices with their start and end apart: 16, of which 10 were waited for; matrix products, arithmetic and copies ran while one was open for 0% of the time, Pallas kernels for 0%

profile of v9, /device:TPU:0, one launch (start us, length us, event | category | flops | bytes accessed | tf_op | source)
XLA Modules:
  0.0 88.0 jit_solution(9941780834537381300)
XLA Ops:
  0.6 2.1 %collective-permute-start.2 = (bf16[128,1024]{1,0:T(8,128)(2,1)}, bf16[128,1024]{1,0:T(8,128)(2,1)S(1)}, u32[]{:S(2)}, u32[]{:S(2)}) collective-permute-start(bf16[128,1024]{1,0:T(8,128)(2,1)} %refs_0_), channel_id=1, source_target_pairs={{0,64},{16,80},{32,96},{48,112},{64,0},{80,16},{96,32},{112,48},{1... | collective-permute-start | bytes 786440 | tf_op jit(solution)/shard_map/ppermute | solution.py:27
  2.7 3.0 %collective-permute-start.1 = (bf16[128,1024]{1,0:T(8,128)(2,1)}, bf16[128,1024]{1,0:T(8,128)(2,1)S(1)}, u32[]{:S(2)}, u32[]{:S(2)}) collective-permute-start(bf16[128,1024]{1,0:T(8,128)(2,1)} %refs_1_), channel_id=1, source_target_pairs={{0,48},{16,0},{32,16},{48,32},{64,112},{80,64},{96,80},{112,96},{1... | collective-permute-start | bytes 786440 | tf_op jit(solution)/shard_map/ppermute | solution.py:27
  5.7 0.0 collective-permute-start
  5.7 3.5 %collective-permute-done.2.refs_4_ = bf16[128,1024]{1,0:T(8,128)(2,1)S(1)} collective-permute-done((bf16[128,1024]{1,0:T(8,128)(2,1)}, bf16[128,1024]{1,0:T(8,128)(2,1)S(1)}, u32[]{:S(2)}, u32[]{:S(2)}) %collective-permute-start.2) | collective-permute-done | bytes 262176 | tf_op jit(solution)/shard_map/ppermute | solution.py:27
  9.2 1.7 %collective-permute-start.10 = (bf16[128,1024]{1,0:T(8,128)(2,1)}, bf16[128,1024]{1,0:T(8,128)(2,1)S(1)}, u32[]{:S(2)}, u32[]{:S(2)}) collective-permute-start(bf16[128,1024]{1,0:T(8,128)(2,1)} %refs_1_), channel_id=1, source_target_pairs={{0,64},{16,80},{32,96},{48,112},{64,0},{80,16},{96,32},{112,48},{1... | collective-permute-start | bytes 786440 | tf_op jit(solution)/shard_map/ppermute | solution.py:27
  11.0 0.4 collective-permute-done.1.refs_10_
  11.3 3.3 %collective-permute-done.refs_9_ = bf16[128,1024]{1,0:T(8,128)(2,1)S(1)} collective-permute-done((bf16[128,1024]{1,0:T(8,128)(2,1)}, bf16[128,1024]{1,0:T(8,128)(2,1)S(1)}, u32[]{:S(2)}, u32[]{:S(2)}) %collective-permute-start) | collective-permute-done | bytes 262176 | tf_op jit(solution)/shard_map/ppermute | solution.py:27
  14.6 0.3 collective-permute-start.4
  14.9 1.7 %collective-permute-start.3 = (bf16[128,1024]{1,0:T(8,128)(2,1)}, bf16[128,1024]{1,0:T(8,128)(2,1)S(1)}, u32[]{:S(2)}, u32[]{:S(2)}) collective-permute-start(bf16[128,1024]{1,0:T(8,128)(2,1)} %refs_0_), channel_id=1, source_target_pairs={{0,16},{16,32},{32,48},{48,0},{64,80},{80,96},{96,112},{112,64},{1... | collective-permute-start | bytes 786440 | tf_op jit(solution)/shard_map/ppermute | solution.py:27
  16.7 0.4 collective-permute-start.12
  17.0 0.0 collective-permute-start.6
  17.0 0.0 collective-permute-done.10.refs_12_
  17.0 3.8 %collective-permute-start.9 = (bf16[128,1024]{1,0:T(8,128)(2,1)S(1)}, bf16[128,1024]{1,0:T(8,128)(2,1)S(1)}, u32[]{:S(2)}, u32[]{:S(2)}) collective-permute-start(bf16[128,1024]{1,0:T(8,128)(2,1)S(1)} %collective-permute-done.1.refs_10_), channel_id=1, source_target_pairs={{0,48},{16,0},{32,16},{48,32},{64,112},{80,64},{96,80},{112,96},{1... | collective-permute-start | bytes 786440 | tf_op jit(solution)/shard_map/ppermute | solution.py:27
  20.8 2.2 %collective-permute-done.12.refs_14_ = bf16[128,1024]{1,0:T(8,128)(2,1)S(1)} collective-permute-done((bf16[128,1024]{1,0:T(8,128)(2,1)S(1)}, bf16[128,1024]{1,0:T(8,128)(2,1)S(1)}, u32[]{:S(2)}, u32[]{:S(2)}) %collective-permute-start.12) | collective-permute-done | bytes 262176 | tf_op jit(solution)/shard_map/ppermute | solution.py:27
  23.0 2.4 %collective-permute-start.7 = (bf16[128,1024]{1,0:T(8,128)(2,1)S(1)}, bf16[128,1024]{1,0:T(8,128)(2,1)S(1)}, u32[]{:S(2)}, u32[]{:S(2)}) collective-permute-start(bf16[128,1024]{1,0:T(8,128)(2,1)S(1)} %collective-permute-done.2.refs_4_), channel_id=1, source_target_pairs={{0,48},{16,0},{32,16},{48,32},{64,112},{80,64},{96,80},{112,96},{1... | collective-permute-start | bytes 786440 | tf_op jit(solution)/shard_map/ppermute | solution.py:27
  25.4 0.0 collective-permute-done.4.refs_2_
  25.4 1.5 %collective-permute-start.11 = (bf16[128,1024]{1,0:T(8,128)(2,1)S(1)}, bf16[128,1024]{1,0:T(8,128)(2,1)S(1)}, u32[]{:S(2)}, u32[]{:S(2)}) collective-permute-start(bf16[128,1024]{1,0:T(8,128)(2,1)S(1)} %collective-permute-done.refs_9_), channel_id=1, source_target_pairs={{0,64},{16,80},{32,96},{48,112},{64,0},{80,16},{96,32},{112,48},{1... | collective-permute-start | bytes 786440 | tf_op jit(solution)/shard_map/ppermute | solution.py:27
  27.0 0.0 collective-permute-done.3.refs_1_
  27.0 0.0 collective-permute-start.5
  27.0 1.5 %collective-permute-done.6.refs_5_ = bf16[128,1024]{1,0:T(8,128)(2,1)S(1)} collective-permute-done((bf16[128,1024]{1,0:T(8,128)(2,1)S(1)}, bf16[128,1024]{1,0:T(8,128)(2,1)S(1)}, u32[]{:S(2)}, u32[]{:S(2)}) %collective-permute-start.6) | collective-permute-done | bytes 262176 | tf_op jit(solution)/shard_map/ppermute | solution.py:27
  28.5 1.3 %collective-permute-start.8 = (bf16[128,1024]{1,0:T(8,128)(2,1)S(1)}, bf16[128,1024]{1,0:T(8,128)(2,1)S(1)}, u32[]{:S(2)}, u32[]{:S(2)}) collective-permute-start(bf16[128,1024]{1,0:T(8,128)(2,1)S(1)} %collective-permute-done.6.refs_5_), channel_id=1, source_target_pairs={{0,16},{16,32},{32,48},{48,0},{64,80},{80,96},{96,112},{112,64},{1... | collective-permute-start | bytes 786440 | tf_op jit(solution)/shard_map/ppermute | solution.py:27
  29.9 0.0 collective-permute-done.9.refs_11_
  29.9 0.9 %collective-permute-start.13 = (bf16[128,1024]{1,0:T(8,128)(2,1)S(1)}, bf16[128,1024]{1,0:T(8,128)(2,1)}, u32[]{:S(2)}, u32[]{:S(2)}) collective-permute-start(bf16[128,1024]{1,0:T(8,128)(2,1)S(1)} %collective-permute-done.9.refs_11_), channel_id=1, source_target_pairs={{0,64},{16,80},{32,96},{48,112},{64,0},{80,16},{96,32},{112,48},{1... | collective-permute-start | bytes 786440 | tf_op jit(solution)/shard_map/ppermute | solution.py:27
  30.8 0.0 copy-start
  30.8 0.9 %copy-done = bf16[128,1024]{1,0:T(8,128)(2,1)S(1)} copy-done((bf16[128,1024]{1,0:T(8,128)(2,1)S(1)}, bf16[128,1024]{1,0:T(8,128)(2,1)}, u32[]{:S(2)}) %copy-start) | copy-done | bytes 262168
  31.7 0.0 copy-start.1
  31.7 0.9 %copy-done.1 = bf16[128,1024]{1,0:T(8,128)(2,1)S(1)} copy-done((bf16[128,1024]{1,0:T(8,128)(2,1)S(1)}, bf16[128,1024]{1,0:T(8,128)(2,1)}, u32[]{:S(2)}) %copy-start.1) | copy-done | bytes 262168
  32.7 0.0 collective-permute-done.7.refs_6_
  32.7 1.6 %collective-permute-done.11.refs_13_ = bf16[128,1024]{1,0:T(8,128)(2,1)S(1)} collective-permute-done((bf16[128,1024]{1,0:T(8,128)(2,1)S(1)}, bf16[128,1024]{1,0:T(8,128)(2,1)S(1)}, u32[]{:S(2)}, u32[]{:S(2)}) %collective-permute-start.11) | collective-permute-done | bytes 262176 | tf_op jit(solution)/shard_map/ppermute | solution.py:27
  34.3 2.6 %collective-permute-done.5.refs_3_ = bf16[128,1024]{1,0:T(8,128)(2,1)S(1)} collective-permute-done((bf16[128,1024]{1,0:T(8,128)(2,1)S(1)}, bf16[128,1024]{1,0:T(8,128)(2,1)S(1)}, u32[]{:S(2)}, u32[]{:S(2)}) %collective-permute-start.5) | collective-permute-done | bytes 262176 | tf_op jit(solution)/shard_map/ppermute | solution.py:27
  37.0 2.8 %collective-permute-done.8.refs_7_ = bf16[128,1024]{1,0:T(8,128)(2,1)S(1)} collective-permute-done((bf16[128,1024]{1,0:T(8,128)(2,1)S(1)}, bf16[128,1024]{1,0:T(8,128)(2,1)S(1)}, u32[]{:S(2)}, u32[]{:S(2)}) %collective-permute-start.8) | collective-permute-done | bytes 262176 | tf_op jit(solution)/shard_map/ppermute | solution.py:27
  39.8 0.0 collective-permute-done.13.refs_15_
  39.8 4.9 %shard_map.50 = (bf16[128,1024]{1,0:T(8,128)(2,1)S(1)}, bf16[128,1024]{1,0:T(8,128)(2,1)S(1)}, bf16[128,1024]{1,0:T(8,128)(2,1)S(1)}, bf16[128,1024]{1,0:T(8,128...) custom-call(s32[1]{0:T(128)} %bitcast.core, ...), custom_call_target="tpu_custom_call", output_to_operand_aliasing={{0}: (1, {}), {1}: (2, {}), {2}: (3, {}), {3}: (4, {}), {4}... | custom-call | tf_op jit(solution)/shard_map/pallas_call | solution.py:51
  44.7 0.0 collective-permute-start.14
  44.7 1.6 %collective-permute-done.14 = bf16[128,1152]{1,0:T(8,128)(2,1)S(1)} collective-permute-done((bf16[128,1152]{1,0:T(8,128)(2,1)S(1)}, bf16[128,1152]{1,0:T(8,128)(2,1)S(1)}, u32[]{:S(2)}, u32[]{:S(2)}) %collective-permute-start.14) | collective-permute-done | bytes 294944 | tf_op jit(solution)/shard_map/ppermute | solution.py:31
  46.2 0.1 add_convert_fusion
  46.3 16.7 %all_to_all.25 = bf16[8,16,1152]{2,1,0:T(8,128)(2,1)S(1)} all-to-all(bf16[8,16,1152]{2,1,0:T(8,128)(2,1)S(1)} %bitcast.8), channel_id=1, replica_groups={{0,2,4,6,8,10,12,14},{1,3,5,7,9,11,13,15},{16,18,20,22,24,26,28,30},{17..., dimensions={0} | all-to-all | bytes 589824 | tf_op jit(solution)/shard_map/all_to_all | solution.py:37
  63.1 10.9 %all_to_all.26 = bf16[8,16,1024]{2,1,0:T(8,128)(2,1)S(1)} all-to-all(bf16[8,16,1024]{2,1,0:T(8,128)(2,1)S(1)} %broadcast_in_dim.2), channel_id=1, replica_groups={{0,2,4,6,8,10,12,14},{1,3,5,7,9,11,13,15},{16,18,20,22,24,26,28,30},{17..., dimensions={0} | all-to-all | bytes 524288 | tf_op jit(solution)/shard_map/all_to_all | solution.py:37
  74.0 0.0 collective-permute-start.15
  74.0 1.5 %collective-permute-done.15.theirs = bf16[128,1024]{1,0:T(8,128)(2,1)S(1)} collective-permute-done((bf16[128,1024]{1,0:T(8,128)(2,1)S(1)}, bf16[128,1024]{1,0:T(8,128)(2,1)S(1)}, u32[]{:S(2)}, u32[]{:S(2)}) %collective-permute-start.15) | collective-permute-done | bytes 262176 | tf_op jit(solution)/shard_map/ppermute | solution.py:31
  75.5 2.1 %shard_map.51 = (bf16[128,1024]{1,0:T(8,128)(2,1)S(1)}, bf16[128,1024]{1,0:T(8,128)(2,1)S(1)}, bf16[128,1024]{1,0:T(8,128)(2,1)S(1)}, bf16[128,1024]{1,0:T(8,128)(2,1)S(1)}, f32[8,4,1152]{2,1,0:T(4,128)S(1)}) custom-call(s32[1]{0:T(128)} %bitcast.core, ...), custom_call_target="tpu_custom_call", output_to_operand_aliasing={{0}: (7, {}), {1}: (8, {}), {2}: (15, {}), {3}: (16, {})} | custom-call | tf_op jit(solution)/shard_map/pallas_call | solution.py:51
  77.6 9.1 %all_to_all.27.stats = f32[8,4,1152]{2,1,0:T(4,128)S(1)} all-to-all(f32[8,4,1152]{2,1,0:T(4,128)S(1)} %get-tuple-element.68), channel_id=1, replica_groups=mesh['sample'=8,'feat'=16] {'sample'}, dimensions={0} | all-to-all | bytes 294912 | tf_op jit(solution)/shard_map/all_to_all | solution.py:314
  86.6 1.3 %shard_map.52 = (bf16[128,1024]{1,0:T(8,128)(2,1)}, bf16[128,1024]{1,0:T(8,128)(2,1)}, f32[1]{0:T(128)}) custom-call(s32[1]{0:T(128)} %bitcast.core, f32[8,4,1152]{2,1,0:T(4,128)S(1)} %all_to_all.27.stats, bf16[128,1024]{1,0:T(8,128)(2,1)S(1)} %get-tuple-element.69.high_a, bf16[128,1024]{1,0:T(8,128)(2,1)S(1)} %get-tuple-element.70.low_a, ...), custom_call_target="tpu_custom_call" | custom-call | tf_op jit(solution)/shard_map/pallas_call | solution.py:51
  (5 shorter events, 0.1 us)
Async XLA Ops:
  0.6 8.6 %collective-permute-start.2 = (bf16[128,1024]{1,0:T(8,128)(2,1)}, bf16[128,1024]{1,0:T(8,128)(2,1)S(1)}, u32[]{:S(2)}, u32[]{:S(2)}) collective-permute-start(bf16[128,1024]{1,0:T(8,128)(2,1)} %refs_0_), channel_id=1, source_target_pairs={{0,64},{16,80},{32,96},{48,112},{64,0},{80,16},{96,32},{112,48},{1... | collective-permute-start | bytes 786440 | tf_op jit(solution)/shard_map/ppermute | solution.py:27
  2.7 8.6 %collective-permute-start.1 = (bf16[128,1024]{1,0:T(8,128)(2,1)}, bf16[128,1024]{1,0:T(8,128)(2,1)S(1)}, u32[]{:S(2)}, u32[]{:S(2)}) collective-permute-start(bf16[128,1024]{1,0:T(8,128)(2,1)} %refs_1_), channel_id=1, source_target_pairs={{0,48},{16,0},{32,16},{48,32},{64,112},{80,64},{96,80},{112,96},{1... | collective-permute-start | bytes 786440 | tf_op jit(solution)/shard_map/ppermute | solution.py:27
  5.7 8.9 %collective-permute-start = (bf16[128,1024]{1,0:T(8,128)(2,1)}, bf16[128,1024]{1,0:T(8,128)(2,1)S(1)}, u32[]{:S(2)}, u32[]{:S(2)}) collective-permute-start(bf16[128,1024]{1,0:T(8,128)(2,1)} %refs_1_), channel_id=1, source_target_pairs={{0,16},{16,32},{32,48},{48,0},{64,80},{80,96},{96,112},{112,64},{1... | collective-permute-start | bytes 786440 | tf_op jit(solution)/shard_map/ppermute | solution.py:27
  9.2 7.8 %collective-permute-start.10 = (bf16[128,1024]{1,0:T(8,128)(2,1)}, bf16[128,1024]{1,0:T(8,128)(2,1)S(1)}, u32[]{:S(2)}, u32[]{:S(2)}) collective-permute-start(bf16[128,1024]{1,0:T(8,128)(2,1)} %refs_1_), channel_id=1, source_target_pairs={{0,64},{16,80},{32,96},{48,112},{64,0},{80,16},{96,32},{112,48},{1... | collective-permute-start | bytes 786440 | tf_op jit(solution)/shard_map/ppermute | solution.py:27
  14.6 10.8 %collective-permute-start.4 = (bf16[128,1024]{1,0:T(8,128)(2,1)}, bf16[128,1024]{1,0:T(8,128)(2,1)S(1)}, u32[]{:S(2)}, u32[]{:S(2)}) collective-permute-start(bf16[128,1024]{1,0:T(8,128)(2,1)} %refs_0_), channel_id=1, source_target_pairs={{0,48},{16,0},{32,16},{48,32},{64,112},{80,64},{96,80},{112,96},{1... | collective-permute-start | bytes 786440 | tf_op jit(solution)/shard_map/ppermute | solution.py:27
  14.9 12.1 %collective-permute-start.3 = (bf16[128,1024]{1,0:T(8,128)(2,1)}, bf16[128,1024]{1,0:T(8,128)(2,1)S(1)}, u32[]{:S(2)}, u32[]{:S(2)}) collective-permute-start(bf16[128,1024]{1,0:T(8,128)(2,1)} %refs_0_), channel_id=1, source_target_pairs={{0,16},{16,32},{32,48},{48,0},{64,80},{80,96},{96,112},{112,64},{1... | collective-permute-start | bytes 786440 | tf_op jit(solution)/shard_map/ppermute | solution.py:27
  16.7 6.4 %collective-permute-start.12 = (bf16[128,1024]{1,0:T(8,128)(2,1)S(1)}, bf16[128,1024]{1,0:T(8,128)(2,1)S(1)}, u32[]{:S(2)}, u32[]{:S(2)}) collective-permute-start(bf16[128,1024]{1,0:T(8,128)(2,1)S(1)} %collective-permute-done.1.refs_10_), channel_id=1, source_target_pairs={{0,64},{16,80},{32,96},{48,112},{64,0},{80,16},{96,32},{112,48},{1... | collective-permute-start | bytes 786440 | tf_op jit(solution)/shard_map/ppermute | solution.py:27
  17.0 11.5 %collective-permute-start.6 = (bf16[128,1024]{1,0:T(8,128)(2,1)S(1)}, bf16[128,1024]{1,0:T(8,128)(2,1)S(1)}, u32[]{:S(2)}, u32[]{:S(2)}) collective-permute-start(bf16[128,1024]{1,0:T(8,128)(2,1)S(1)} %collective-permute-done.2.refs_4_), channel_id=1, source_target_pairs={{0,16},{16,32},{32,48},{48,0},{64,80},{80,96},{96,112},{112,64},{1... | collective-permute-start | bytes 786440 | tf_op jit(solution)/shard_map/ppermute | solution.py:27
  17.0 12.9 %collective-permute-start.9 = (bf16[128,1024]{1,0:T(8,128)(2,1)S(1)}, bf16[128,1024]{1,0:T(8,128)(2,1)S(1)}, u32[]{:S(2)}, u32[]{:S(2)}) collective-permute-start(bf16[128,1024]{1,0:T(8,128)(2,1)S(1)} %collective-permute-done.1.refs_10_), channel_id=1, source_target_pairs={{0,48},{16,0},{32,16},{48,32},{64,112},{80,64},{96,80},{112,96},{1... | collective-permute-start | bytes 786440 | tf_op jit(solution)/shard_map/ppermute | solution.py:27
  23.0 9.7 %collective-permute-start.7 = (bf16[128,1024]{1,0:T(8,128)(2,1)S(1)}, bf16[128,1024]{1,0:T(8,128)(2,1)S(1)}, u32[]{:S(2)}, u32[]{:S(2)}) collective-permute-start(bf16[128,1024]{1,0:T(8,128)(2,1)S(1)} %collective-permute-done.2.refs_4_), channel_id=1, source_target_pairs={{0,48},{16,0},{32,16},{48,32},{64,112},{80,64},{96,80},{112,96},{1... | collective-permute-start | bytes 786440 | tf_op jit(solution)/shard_map/ppermute | solution.py:27
  25.4 8.9 %collective-permute-start.11 = (bf16[128,1024]{1,0:T(8,128)(2,1)S(1)}, bf16[128,1024]{1,0:T(8,128)(2,1)S(1)}, u32[]{:S(2)}, u32[]{:S(2)}) collective-permute-start(bf16[128,1024]{1,0:T(8,128)(2,1)S(1)} %collective-permute-done.refs_9_), channel_id=1, source_target_pairs={{0,64},{16,80},{32,96},{48,112},{64,0},{80,16},{96,32},{112,48},{1... | collective-permute-start | bytes 786440 | tf_op jit(solution)/shard_map/ppermute | solution.py:27
  27.0 10.0 %collective-permute-start.5 = (bf16[128,1024]{1,0:T(8,128)(2,1)S(1)}, bf16[128,1024]{1,0:T(8,128)(2,1)S(1)}, u32[]{:S(2)}, u32[]{:S(2)}) collective-permute-start(bf16[128,1024]{1,0:T(8,128)(2,1)S(1)} %collective-permute-done.3.refs_1_), channel_id=1, source_target_pairs={{0,16},{16,32},{32,48},{48,0},{64,80},{80,96},{96,112},{112,64},{1... | collective-permute-start | bytes 786440 | tf_op jit(solution)/shard_map/ppermute | solution.py:27
  28.5 11.2 %collective-permute-start.8 = (bf16[128,1024]{1,0:T(8,128)(2,1)S(1)}, bf16[128,1024]{1,0:T(8,128)(2,1)S(1)}, u32[]{:S(2)}, u32[]{:S(2)}) collective-permute-start(bf16[128,1024]{1,0:T(8,128)(2,1)S(1)} %collective-permute-done.6.refs_5_), channel_id=1, source_target_pairs={{0,16},{16,32},{32,48},{48,0},{64,80},{80,96},{96,112},{112,64},{1... | collective-permute-start | bytes 786440 | tf_op jit(solution)/shard_map/ppermute | solution.py:27
  29.9 9.9 %collective-permute-start.13 = (bf16[128,1024]{1,0:T(8,128)(2,1)S(1)}, bf16[128,1024]{1,0:T(8,128)(2,1)}, u32[]{:S(2)}, u32[]{:S(2)}) collective-permute-start(bf16[128,1024]{1,0:T(8,128)(2,1)S(1)} %collective-permute-done.9.refs_11_), channel_id=1, source_target_pairs={{0,64},{16,80},{32,96},{48,112},{64,0},{80,16},{96,32},{112,48},{1... | collective-permute-start | bytes 786440 | tf_op jit(solution)/shard_map/ppermute | solution.py:27
  30.8 0.9 %copy-start = (bf16[128,1024]{1,0:T(8,128)(2,1)S(1)}, bf16[128,1024]{1,0:T(8,128)(2,1)}, u32[]{:S(2)}) copy-start(bf16[128,1024]{1,0:T(8,128)(2,1)} %refs_0_) | copy-start | bytes 786436
  31.7 0.9 %copy-start.1 = (bf16[128,1024]{1,0:T(8,128)(2,1)S(1)}, bf16[128,1024]{1,0:T(8,128)(2,1)}, u32[]{:S(2)}) copy-start(bf16[128,1024]{1,0:T(8,128)(2,1)} %refs_1_) | copy-start | bytes 786436
  44.7 1.6 %collective-permute-start.14 = (bf16[128,1152]{1,0:T(8,128)(2,1)S(1)}, bf16[128,1152]{1,0:T(8,128)(2,1)S(1)}, u32[]{:S(2)}, u32[]{:S(2)}) collective-permute-start(bf16[128,1152]{1,0:T(8,128)(2,1)S(1)} %get-tuple-element.49), channel_id=1, source_target_pairs={{0,1},{1,0},{2,3},{3,2},{4,5},{5,4},{6,7},{7,6},{8,9},{9,8},{10,11... | collective-permute-start | bytes 884744 | tf_op jit(solution)/shard_map/ppermute | solution.py:31
  74.0 1.5 %collective-permute-start.15 = (bf16[128,1024]{1,0:T(8,128)(2,1)S(1)}, bf16[128,1024]{1,0:T(8,128)(2,1)S(1)}, u32[]{:S(2)}, u32[]{:S(2)}) collective-permute-start(bf16[128,1024]{1,0:T(8,128)(2,1)S(1)} %bitcast.6), channel_id=1, source_target_pairs={{0,1},{1,0},{2,3},{3,2},{4,5},{5,4},{6,7},{7,6},{8,9},{9,8},{10,11... | collective-permute-start | bytes 786440 | tf_op jit(solution)/shard_map/ppermute | solution.py:31
